TPU v7x, 32 devices: a whole 2x2x4 slice. The times are simulated.
32 devices in a mesh: section: 16 (over z, x, core), tensor: 2 (over y).
Axes of the slice: x: 2, y: 2, z: 4, core: 2. Of those that a mesh axis runs over, the one named last changes fastest.
Arguments:
- stream: float32 [16, 512, 8192], P('section', None, 'tensor'), may hold values from -40 to 40
- down_factor: bfloat16 [2, 16, 8192, 512], P(None, 'section', 'tensor'), may hold values from -0.0625 to 0.0625
- router: bfloat16 [2, 16, 8192, 512], P(None, 'section', 'tensor'), may hold values from -0.0625 to 0.0625
- expert_factor: bfloat16 [2, 16, 512, 32], P(None, 'section'), may hold values from -0.25 to 0.25
- core_tensor: bfloat16 [2, 16, 512, 32, 512], P(None, 'section', 'tensor'), may hold values from -0.046875 to 0.046875
- up_factor: bfloat16 [2, 16, 512, 8192], P(None, 'section', None, 'tensor'), may hold values from -0.25 to 0.25
Outputs:
- stream_out: float32 [16, 512, 8192], P('section', None, 'tensor')
All inputs are finite; a program needn't handle non-finite values.
Results may differ from a plain program's by a relative error of at most 0.0095.
Values may be sent and summed in bfloat16 or wider, within the bound.
No kernel may reach another device: no remote copies, remote signals or barrier semaphores. Data moves between devices by JAX's collectives and lax.ppermute only.
A program may use at most 192 MiB of HBM per device.

v0:
```python
import jax
import jax.numpy as jnp
from jax import lax
from jax.sharding import PartitionSpec as P

D = 8192
TICKS = 6


EPSILON = 1e-05


def from_behind(value, axis, steps):
    count = lax.axis_size(axis)
    pairs = [(source, (source + steps) % count) for source in range(count)]
    return lax.ppermute(value, axis, pairs)


def select_lap(stacked, lap_id):
    return lax.dynamic_index_in_dim(stacked[:, 0], lap_id, 0, keepdims=False)


def finish_rows(projected, logits, squares, expert_part):
    factor = lax.rsqrt(squares / D + EPSILON)
    reduced = (projected * factor).astype(jnp.bfloat16)
    gating = jax.nn.sigmoid(logits * factor).astype(jnp.bfloat16)
    mixing = jnp.dot(gating, expert_part, preferred_element_type=jnp.float32).astype(jnp.bfloat16)
    return (reduced, mixing)


def core_rows(reduced, mixing, core_part):
    flattened = core_part.reshape(core_part.shape[0] * core_part.shape[1], core_part.shape[2])
    partial_value = lax.dot_general(
        reduced, flattened, (((1,), (1,)), ((), ())), preferred_element_type=jnp.float32
    )
    partial_value = partial_value.reshape(reduced.shape[0], core_part.shape[0], core_part.shape[1])
    return jnp.sum(partial_value * mixing.astype(jnp.float32)[:, None, :], axis=2).astype(
        jnp.bfloat16
    )


def per_device(stream, down_factor, router, expert_factor, core_tensor, up_factor):
    section_id = lax.axis_index("section")
    sections = lax.axis_size("section")
    front_edge = sections // 2
    carried = stream[0]
    for tick_index in range(TICKS):
        anchor = (section_id - tick_index) % sections
        lap_id = (anchor < front_edge).astype(jnp.int32) + (section_id < tick_index).astype(
            jnp.int32
        )
        down_part = select_lap(down_factor, lap_id)
        router_part = select_lap(router, lap_id)
        expert_part = select_lap(expert_factor, lap_id)
        core_part = select_lap(core_tensor, lap_id)
        up_part = select_lap(up_factor, lap_id)
        lowered = carried.astype(jnp.bfloat16)
        projected = jnp.dot(lowered, down_part, preferred_element_type=jnp.float32)
        logits = jnp.dot(lowered, router_part, preferred_element_type=jnp.float32)
        squares = jnp.sum(carried * carried, axis=1, keepdims=True)
        projected, logits, squares = (
            lax.psum_scatter(projected, "tensor", scatter_dimension=0, tiled=True),
            lax.psum_scatter(logits, "tensor", scatter_dimension=0, tiled=True),
            lax.psum_scatter(squares, "tensor", scatter_dimension=0, tiled=True),
        )
        reduced, mixing = finish_rows(projected, logits, squares, expert_part)
        pieces = lax.all_gather((reduced, mixing), "tensor", axis=0, tiled=True)
        ranked = core_rows(pieces[0], pieces[1], core_part)
        update = jnp.dot(
            lax.all_gather(ranked, "tensor", axis=1, tiled=True),
            up_part,
            preferred_element_type=jnp.float32,
        )
        carried = from_behind(carried + update, "section", 1)
    return carried[None]


def solution(mesh):
    return jax.shard_map(
        per_device,
        mesh=mesh,
        in_specs=(
            P("section", None, "tensor"),
            P(None, "section", "tensor", None),
            P(None, "section", "tensor", None),
            P(None, "section", None, None),
            P(None, "section", "tensor", None, None),
            P(None, "section", None, "tensor"),
        ),
        out_specs=P("section", None, "tensor"),
        check_vma=False,
    )
```

profile of v0, /device:TPU:0, one launch (start us, length us, event | category | flops | bytes accessed | tf_op | source)
XLA Modules:
  0.0 1194.9 jit_solution(11488401751437310234)
XLA Ops:
  11.5 8.0 fusion.98
  19.6 8.1 fusion.93
  27.9 36.3 %constant_dynamic-slice_fusion = (bf16[1,1,256,32,512]{4,3,2,1,0:T(8,128)(2,1)}, bf16[1,1,256,32,512]{4,3,2,1,0:T(8,128)(2,1)}, bf16[1,1,256,32,512]{4,3,2,1,0:T...) fusion(bf16[2,1,256,32,512]{4,3,2,1,0:T(8,128)(2,1)} %param.10,, ...), kind=kLoop, calls=%fused_computation.146 | loop fusion | bytes 100663320 | tf_op jit(solution)/shard_map/jit(dynamic_index_in_dim)/dynamic_slice | solution.py:20
  73.1 8.2 all_gather.54
  81.3 17.7 %multiply_reduce_fusion.5 = bf16[512,256]{1,0:T(8,128)(2,1)S(1)} fusion(f32[512,32]{0,1:T(8,128)S(1)} %convert_element_type.155, bf16[1,1,256,32,512]{4,3,2,1,0:T(8,128)(2,1)} %get-tuple-element.9, bf16[512,512]{0,1:T(8,128)(2,1)S(1)} %all_gather.54), kind=kOutput, calls=%fused_computation.5 | convolution fusion | flops 4303224832 | bytes 9240576 | tf_op jit(solution)/shard_map/dot_general | solution.py:33
  99.0 7.1 all_gather.56
  106.1 7.2 bitcast_add_fusion
  113.4 95.6 %collective-permute-done = f32[512,4096]{1,0:T(8,128)S(1)} collective-permute-done((f32[512,4096]{1,0:T(8,128)S(1)}, f32[512,4096]{1,0:T(8,128)S(1)}, u32[]{:S(2)}, u32[]{:S(2)}) %collective-permute-start) | collective-permute-done | bytes 8388640 | tf_op jit(solution)/shard_map/ppermute | solution.py:16
  214.1 8.0 fusion.40
  222.2 8.1 fusion.42
  231.3 15.6 %reduce-scatter.37.cloned.1.call-done = f32[256,512]{0,1:T(8,128)} async-done(((f32[512,512]{0,1:T(8,128)}), f32[256,512]{0,1:T(8,128)}) %reduce-scatter.37.cloned.1.call-update) | async-done | bytes 524304 | tf_op jit(solution)/shard_map/reduce_scatter | solution.py:63
  252.6 16.8 %reduce-scatter.35.cloned.1.call-done = f32[256,512]{0,1:T(8,128)} async-done(((f32[512,512]{0,1:T(8,128)}), f32[256,512]{0,1:T(8,128)}) %reduce-scatter.35.cloned.1.call-update) | async-done | bytes 524304 | tf_op jit(solution)/shard_map/reduce_scatter | solution.py:62
  270.5 8.7 all_gather.57
  279.2 17.8 %multiply_reduce_fusion.4 = bf16[512,256]{1,0:T(8,128)(2,1)S(1)} fusion(f32[512,32]{0,1:T(8,128)S(1)} %convert_element_type.163, bf16[1,1,256,32,512]{4,3,2,1,0:T(8,128)(2,1)} %get-tuple-element.8, bf16[512,512]{0,1:T(8,128)(2,1)S(1)} %all_gather.57), kind=kOutput, calls=%fused_computation.4 | convolution fusion | flops 4303224832 | bytes 9240576 | tf_op jit(solution)/shard_map/dot_general | solution.py:33
  297.1 7.7 all_gather.59
  309.6 95.6 %collective-permute-done.1 = f32[512,4096]{1,0:T(8,128)S(1)} collective-permute-done((f32[512,4096]{1,0:T(8,128)S(1)}, f32[512,4096]{1,0:T(8,128)S(1)}, u32[]{:S(2)}, u32[]{:S(2)}) %collective-permute-start.1) | collective-permute-done | bytes 8388640 | tf_op jit(solution)/shard_map/ppermute | solution.py:16
  410.1 8.0 fusion.35
  418.2 8.0 fusion.37
  427.3 14.4 %reduce-scatter.41.cloned.1.call-done = f32[256,512]{0,1:T(8,128)} async-done(((f32[512,512]{0,1:T(8,128)}), f32[256,512]{0,1:T(8,128)}) %reduce-scatter.41.cloned.1.call-update) | async-done | bytes 524304 | tf_op jit(solution)/shard_map/reduce_scatter | solution.py:63
  447.4 17.0 %reduce-scatter.39.cloned.1.call-done = f32[256,512]{0,1:T(8,128)} async-done(((f32[512,512]{0,1:T(8,128)}), f32[256,512]{0,1:T(8,128)}) %reduce-scatter.39.cloned.1.call-update) | async-done | bytes 524304 | tf_op jit(solution)/shard_map/reduce_scatter | solution.py:62
  465.5 8.7 all_gather.60
  474.2 17.8 %multiply_reduce_fusion.3 = bf16[512,256]{1,0:T(8,128)(2,1)S(1)} fusion(f32[512,32]{0,1:T(8,128)S(1)} %convert_element_type.171, bf16[1,1,256,32,512]{4,3,2,1,0:T(8,128)(2,1)} %get-tuple-element.7, bf16[512,512]{0,1:T(8,128)(2,1)S(1)} %all_gather.60), kind=kOutput, calls=%fused_computation.3 | convolution fusion | flops 4303224832 | bytes 9240576 | tf_op jit(solution)/shard_map/dot_general | solution.py:33
  492.0 7.7 all_gather.62
  504.5 95.6 %collective-permute-done.2 = f32[512,4096]{1,0:T(8,128)S(1)} collective-permute-done((f32[512,4096]{1,0:T(8,128)S(1)}, f32[512,4096]{1,0:T(8,128)S(1)}, u32[]{:S(2)}, u32[]{:S(2)}) %collective-permute-start.2) | collective-permute-done | bytes 8388640 | tf_op jit(solution)/shard_map/ppermute | solution.py:16
  605.3 8.1 fusion.30
  613.5 7.9 fusion.32
  622.6 14.1 %reduce-scatter.45.cloned.1.call-done = f32[256,512]{0,1:T(8,128)} async-done(((f32[512,512]{0,1:T(8,128)}), f32[256,512]{0,1:T(8,128)}) %reduce-scatter.45.cloned.1.call-update) | async-done | bytes 524304 | tf_op jit(solution)/shard_map/reduce_scatter | solution.py:63
  642.4 16.8 %reduce-scatter.43.cloned.1.call-done = f32[256,512]{0,1:T(8,128)} async-done(((f32[512,512]{0,1:T(8,128)}), f32[256,512]{0,1:T(8,128)}) %reduce-scatter.43.cloned.1.call-update) | async-done | bytes 524304 | tf_op jit(solution)/shard_map/reduce_scatter | solution.py:62
  660.3 8.7 all_gather.63
  669.0 17.8 %multiply_reduce_fusion.2 = bf16[512,256]{1,0:T(8,128)(2,1)S(1)} fusion(f32[512,32]{0,1:T(8,128)S(1)} %convert_element_type.179, bf16[1,1,256,32,512]{4,3,2,1,0:T(8,128)(2,1)} %get-tuple-element.6, bf16[512,512]{0,1:T(8,128)(2,1)S(1)} %all_gather.63), kind=kOutput, calls=%fused_computation.2 | convolution fusion | flops 4303224832 | bytes 9240576 | tf_op jit(solution)/shard_map/dot_general | solution.py:33
  686.9 7.7 all_gather.65
  699.4 95.6 %collective-permute-done.3 = f32[512,4096]{1,0:T(8,128)S(1)} collective-permute-done((f32[512,4096]{1,0:T(8,128)S(1)}, f32[512,4096]{1,0:T(8,128)S(1)}, u32[]{:S(2)}, u32[]{:S(2)}) %collective-permute-start.3) | collective-permute-done | bytes 8388640 | tf_op jit(solution)/shard_map/ppermute | solution.py:16
  799.9 8.0 fusion.25
  808.0 8.0 fusion.27
  817.2 14.2 %reduce-scatter.49.cloned.1.call-done = f32[256,512]{0,1:T(8,128)} async-done(((f32[512,512]{0,1:T(8,128)}), f32[256,512]{0,1:T(8,128)}) %reduce-scatter.49.cloned.1.call-update) | async-done | bytes 524304 | tf_op jit(solution)/shard_map/reduce_scatter | solution.py:63
  837.1 16.8 %reduce-scatter.47.cloned.1.call-done = f32[256,512]{0,1:T(8,128)} async-done(((f32[512,512]{0,1:T(8,128)}), f32[256,512]{0,1:T(8,128)}) %reduce-scatter.47.cloned.1.call-update) | async-done | bytes 524304 | tf_op jit(solution)/shard_map/reduce_scatter | solution.py:62
  855.0 8.7 all_gather.66
  863.7 17.8 %multiply_reduce_fusion.1 = bf16[512,256]{1,0:T(8,128)(2,1)S(1)} fusion(f32[512,32]{0,1:T(8,128)S(1)} %convert_element_type.187, bf16[1,1,256,32,512]{4,3,2,1,0:T(8,128)(2,1)} %get-tuple-element.10, bf16[512,512]{0,1:T(8,128)(2,1)S(1)} %all_gather.66), kind=kOutput, calls=%fused_computation.1 | convolution fusion | flops 4303224832 | bytes 9240576 | tf_op jit(solution)/shard_map/dot_general | solution.py:33
  881.5 7.7 all_gather.68
  894.0 95.6 %collective-permute-done.4 = f32[512,4096]{1,0:T(8,128)S(1)} collective-permute-done((f32[512,4096]{1,0:T(8,128)S(1)}, f32[512,4096]{1,0:T(8,128)S(1)}, u32[]{:S(2)}, u32[]{:S(2)}) %collective-permute-start.4) | collective-permute-done | bytes 8388640 | tf_op jit(solution)/shard_map/ppermute | solution.py:16
  994.6 8.1 fusion.20
  1002.8 8.0 fusion.22
  1011.8 14.2 %reduce-scatter.53.cloned.1.call-done = f32[256,512]{0,1:T(8,128)} async-done(((f32[512,512]{0,1:T(8,128)}), f32[256,512]{0,1:T(8,128)}) %reduce-scatter.53.cloned.1.call-update) | async-done | bytes 524304 | tf_op jit(solution)/shard_map/reduce_scatter | solution.py:63
  1031.8 16.8 %reduce-scatter.51.cloned.1.call-done = f32[256,512]{0,1:T(8,128)} async-done(((f32[512,512]{0,1:T(8,128)}), f32[256,512]{0,1:T(8,128)}) %reduce-scatter.51.cloned.1.call-update) | async-done | bytes 524304 | tf_op jit(solution)/shard_map/reduce_scatter | solution.py:62
  1049.7 8.7 all_gather.69
  1058.3 17.8 %multiply_reduce_fusion = bf16[512,256]{1,0:T(8,128)(2,1)S(1)} fusion(f32[512,32]{0,1:T(8,128)S(1)} %convert_element_type.195, bf16[1,1,256,32,512]{4,3,2,1,0:T(8,128)(2,1)} %get-tuple-element.5, bf16[512,512]{0,1:T(8,128)(2,1)S(1)} %all_gather.69), kind=kOutput, calls=%fused_computation | convolution fusion | flops 4303224832 | bytes 9240576 | tf_op jit(solution)/shard_map/dot_general | solution.py:33
  1076.2 7.7 all_gather.71
  1088.7 95.6 %collective-permute-done.5 = f32[512,4096]{1,0:T(8,128)S(1)} collective-permute-done((f32[512,4096]{1,0:T(8,128)S(1)}, f32[512,4096]{1,0:T(8,128)S(1)}, u32[]{:S(2)}, u32[]{:S(2)}) %collective-permute-start.5) | collective-permute-done | bytes 8388640 | tf_op jit(solution)/shard_map/ppermute | solution.py:16
  (141 shorter events, 106.3 us)
Async XLA Ops:
  6.5 58.7 %copy-start = (bf16[2,1,512,32]{2,3,1,0:T(8,128)(2,1)S(1)}, bf16[2,1,512,32]{2,3,1,0:T(8,128)(2,1)}, u32[]{:S(2)}) copy-start(bf16[2,1,512,32]{2,3,1,0:T(8,128)(2,1)} %param.9) | copy-start | bytes 196612
  6.5 57.7 %reduce-scatter.55.cloned.1.call-start = ((), (), s32[]{:S(2)}) async-start(), calls=%async_computation.30 | async-start | bytes 393216
  11.5 53.7 %reduce-scatter.33.cloned.1.call-start = ((), (), s32[]{:S(2)}) async-start(), calls=%async_computation.19 | async-start | bytes 1572864 | tf_op jit(solution)/shard_map/reduce_scatter | solution.py:63
  19.6 52.4 %reduce-scatter.31.cloned.1.call-start = ((), (), s32[]{:S(2)}) async-start(), calls=%async_computation.18 | async-start | bytes 1572864 | tf_op jit(solution)/shard_map/reduce_scatter | solution.py:62
  27.7 202.6 %reduce-scatter.57.cloned.1.call-start = ((), (), s32[]{:S(2)}) async-start(), calls=%async_computation.31 | async-start | bytes 393216
  113.3 95.6 %collective-permute-start = (f32[512,4096]{1,0:T(8,128)S(1)}, f32[512,4096]{1,0:T(8,128)S(1)}, u32[]{:S(2)}, u32[]{:S(2)}) collective-permute-start(f32[512,4096]{1,0:T(8,128)S(1)} %bitcast_add_fusion), channel_id=1, source_target_pairs={{0,2},{2,4},{4,6},{6,8},{8,10},{10,12},{12,14},{14,16},{16,18},{18... | collective-permute-start | bytes 25165832 | tf_op jit(solution)/shard_map/ppermute | solution.py:16
  208.9 3.2 copy-start.1
  213.6 33.3 %reduce-scatter.37.cloned.1.call-start = ((), (), s32[]{:S(2)}) async-start(), calls=%async_computation.21 | async-start | bytes 1572864 | tf_op jit(solution)/shard_map/reduce_scatter | solution.py:63
  222.1 47.3 %reduce-scatter.35.cloned.1.call-start = ((), (), s32[]{:S(2)}) async-start(), calls=%async_computation.20 | async-start | bytes 1572864 | tf_op jit(solution)/shard_map/reduce_scatter | solution.py:62
  230.2 196.0 %reduce-scatter.59.cloned.1.call-start = ((), (), s32[]{:S(2)}) async-start(), calls=%async_computation.32 | async-start | bytes 393216
  270.5 34.3 %slice-start = ((s8[8388608]{0:T(1024)(128)(4,1)}), s8[4194304]{0:T(1024)(128)(4,1)S(1)}, s32[]{:S(2)}) async-start(s8[8388608]{0:T(1024)(128)(4,1)} %bitcast.167), calls=%async_computation.36 | async-start | bytes 8388608
  279.2 25.6 %slice-start.1 = ((s8[8388608]{0:T(1024)(128)(4,1)}), s8[4194304]{0:T(1024)(128)(4,1)S(1)}, s32[]{:S(2)}) async-start(s8[8388608]{0:T(1024)(128)(4,1)} %bitcast.167), calls=%async_computation.37 | async-start | bytes 8388608
  309.5 95.6 %collective-permute-start.1 = (f32[512,4096]{1,0:T(8,128)S(1)}, f32[512,4096]{1,0:T(8,128)S(1)}, u32[]{:S(2)}, u32[]{:S(2)}) collective-permute-start(f32[512,4096]{1,0:T(8,128)S(1)} %convolution_add_fusion.4), channel_id=1, source_target_pairs={{0,2},{2,4},{4,6},{6,8},{8,10},{10,12},{12,14},{14,16},{16,18},{18... | collective-permute-start | bytes 25165832 | tf_op jit(solution)/shard_map/ppermute | solution.py:16
  405.1 3.2 copy-start.2
  409.9 31.9 %reduce-scatter.41.cloned.1.call-start = ((), (), s32[]{:S(2)}) async-start(), calls=%async_computation.23 | async-start | bytes 1572864 | tf_op jit(solution)/shard_map/reduce_scatter | solution.py:63
  418.2 46.2 %reduce-scatter.39.cloned.1.call-start = ((), (), s32[]{:S(2)}) async-start(), calls=%async_computation.22 | async-start | bytes 1572864 | tf_op jit(solution)/shard_map/reduce_scatter | solution.py:62
  426.2 195.3 %reduce-scatter.61.cloned.1.call-start = ((), (), s32[]{:S(2)}) async-start(), calls=%async_computation.33 | async-start | bytes 393216
  465.5 34.3 %slice-start.2 = ((s8[8388608]{0:T(1024)(128)(4,1)}), s8[4194304]{0:T(1024)(128)(4,1)S(1)}, s32[]{:S(2)}) async-start(s8[8388608]{0:T(1024)(128)(4,1)} %bitcast.169), calls=%async_computation.38 | async-start | bytes 8388608
  474.2 25.6 %slice-start.3 = ((s8[8388608]{0:T(1024)(128)(4,1)}), s8[4194304]{0:T(1024)(128)(4,1)S(1)}, s32[]{:S(2)}) async-start(s8[8388608]{0:T(1024)(128)(4,1)} %bitcast.169), calls=%async_computation.39 | async-start | bytes 8388608
  504.5 95.6 %collective-permute-start.2 = (f32[512,4096]{1,0:T(8,128)S(1)}, f32[512,4096]{1,0:T(8,128)S(1)}, u32[]{:S(2)}, u32[]{:S(2)}) collective-permute-start(f32[512,4096]{1,0:T(8,128)S(1)} %convolution_add_fusion.3), channel_id=1, source_target_pairs={{0,2},{2,4},{4,6},{6,8},{8,10},{10,12},{12,14},{14,16},{16,18},{18... | collective-permute-start | bytes 25165832 | tf_op jit(solution)/shard_map/ppermute | solution.py:16
  600.1 3.2 copy-start.3
  604.8 31.9 %reduce-scatter.45.cloned.1.call-start = ((), (), s32[]{:S(2)}) async-start(), calls=%async_computation.25 | async-start | bytes 1572864 | tf_op jit(solution)/shard_map/reduce_scatter | solution.py:63
  613.4 45.8 %reduce-scatter.43.cloned.1.call-start = ((), (), s32[]{:S(2)}) async-start(), calls=%async_computation.24 | async-start | bytes 1572864 | tf_op jit(solution)/shard_map/reduce_scatter | solution.py:62
  621.4 194.7 %reduce-scatter.63.cloned.1.call-start = ((), (), s32[]{:S(2)}) async-start(), calls=%async_computation.34 | async-start | bytes 393216
  660.3 34.2 %slice-start.4 = ((s8[8388608]{0:T(1024)(128)(4,1)}), s8[4194304]{0:T(1024)(128)(4,1)S(1)}, s32[]{:S(2)}) async-start(s8[8388608]{0:T(1024)(128)(4,1)} %bitcast.171), calls=%async_computation.40 | async-start | bytes 8388608
  669.0 25.5 %slice-start.5 = ((s8[8388608]{0:T(1024)(128)(4,1)}), s8[4194304]{0:T(1024)(128)(4,1)S(1)}, s32[]{:S(2)}) async-start(s8[8388608]{0:T(1024)(128)(4,1)} %bitcast.171), calls=%async_computation.41 | async-start | bytes 8388608
  699.3 95.6 %collective-permute-start.3 = (f32[512,4096]{1,0:T(8,128)S(1)}, f32[512,4096]{1,0:T(8,128)S(1)}, u32[]{:S(2)}, u32[]{:S(2)}) collective-permute-start(f32[512,4096]{1,0:T(8,128)S(1)} %convolution_add_fusion.2), channel_id=1, source_target_pairs={{0,2},{2,4},{4,6},{6,8},{8,10},{10,12},{12,14},{14,16},{16,18},{18... | collective-permute-start | bytes 25165832 | tf_op jit(solution)/shard_map/ppermute | solution.py:16
  794.9 3.2 copy-start.4
  799.7 31.7 %reduce-scatter.49.cloned.1.call-start = ((), (), s32[]{:S(2)}) async-start(), calls=%async_computation.27 | async-start | bytes 1572864 | tf_op jit(solution)/shard_map/reduce_scatter | solution.py:63
  807.9 45.9 %reduce-scatter.47.cloned.1.call-start = ((), (), s32[]{:S(2)}) async-start(), calls=%async_computation.26 | async-start | bytes 1572864 | tf_op jit(solution)/shard_map/reduce_scatter | solution.py:62
  816.0 194.7 %reduce-scatter.65.cloned.1.call-start = ((), (), s32[]{:S(2)}) async-start(), calls=%async_computation.35 | async-start | bytes 393216
  855.0 34.3 %slice-start.6 = ((s8[8388608]{0:T(1024)(128)(4,1)}), s8[4194304]{0:T(1024)(128)(4,1)S(1)}, s32[]{:S(2)}) async-start(s8[8388608]{0:T(1024)(128)(4,1)} %bitcast.173), calls=%async_computation.42 | async-start | bytes 8388608
  863.7 25.6 %slice-start.7 = ((s8[8388608]{0:T(1024)(128)(4,1)}), s8[4194304]{0:T(1024)(128)(4,1)S(1)}, s32[]{:S(2)}) async-start(s8[8388608]{0:T(1024)(128)(4,1)} %bitcast.173), calls=%async_computation.43 | async-start | bytes 8388608
  894.0 95.6 %collective-permute-start.4 = (f32[512,4096]{1,0:T(8,128)S(1)}, f32[512,4096]{1,0:T(8,128)S(1)}, u32[]{:S(2)}, u32[]{:S(2)}) collective-permute-start(f32[512,4096]{1,0:T(8,128)S(1)} %convolution_add_fusion.1), channel_id=1, source_target_pairs={{0,2},{2,4},{4,6},{6,8},{8,10},{10,12},{12,14},{14,16},{16,18},{18... | collective-permute-start | bytes 25165832 | tf_op jit(solution)/shard_map/ppermute | solution.py:16
  989.6 3.2 copy-start.5
  994.3 31.7 %reduce-scatter.53.cloned.1.call-start = ((), (), s32[]{:S(2)}) async-start(), calls=%async_computation.29 | async-start | bytes 1572864 | tf_op jit(solution)/shard_map/reduce_scatter | solution.py:63
  1002.7 45.8 %reduce-scatter.51.cloned.1.call-start = ((), (), s32[]{:S(2)}) async-start(), calls=%async_computation.28 | async-start | bytes 1572864 | tf_op jit(solution)/shard_map/reduce_scatter | solution.py:62
  1049.7 34.2 %slice-start.8 = ((s8[8388608]{0:T(1024)(128)(4,1)}), s8[4194304]{0:T(1024)(128)(4,1)S(1)}, s32[]{:S(2)}) async-start(s8[8388608]{0:T(1024)(128)(4,1)} %bitcast.175), calls=%async_computation.44 | async-start | bytes 8388608
  1058.3 25.5 %slice-start.9 = ((s8[8388608]{0:T(1024)(128)(4,1)}), s8[4194304]{0:T(1024)(128)(4,1)S(1)}, s32[]{:S(2)}) async-start(s8[8388608]{0:T(1024)(128)(4,1)} %bitcast.175), calls=%async_computation.45 | async-start | bytes 8388608
  1088.6 95.6 %collective-permute-start.5 = (f32[512,4096]{1,0:T(8,128)S(1)}, f32[512,4096]{1,0:T(8,128)S(1)}, u32[]{:S(2)}, u32[]{:S(2)}) collective-permute-start(f32[512,4096]{1,0:T(8,128)S(1)} %convolution_add_fusion), channel_id=1, source_target_pairs={{0,2},{2,4},{4,6},{6,8},{8,10},{10,12},{12,14},{14,16},{16,18},{18... | collective-permute-start | bytes 25165832 | tf_op jit(solution)/shard_map/ppermute | solution.py:16
Sparse Core Ops, SparseCore 0:
  11.6 14.4 reduce-scatter.54
  28.3 20.3 reduce-scatter.32
  51.0 20.3 reduce-scatter.30
  213.7 10.6 reduce-scatter.56
  226.5 20.3 reduce-scatter.36
  249.0 20.3 reduce-scatter.34
  410.0 9.0 reduce-scatter.58
  421.3 20.3 reduce-scatter.40
  444.0 20.3 reduce-scatter.38
  604.9 9.0 reduce-scatter.60
  616.3 20.3 reduce-scatter.44
  638.8 20.3 reduce-scatter.42
  799.8 9.0 reduce-scatter.62
  811.0 20.3 reduce-scatter.48
  833.5 20.3 reduce-scatter.46
  994.4 9.0 reduce-scatter.64
  1005.6 20.3 reduce-scatter.52
  1028.2 20.3 reduce-scatter.50
where the time goes:
time: 1200 us; the launch traced here: 1190 us
  waiting for transfers between devices  731 us (61%)
  matrix products  242 us (20%)
  blocking collectives  125 us (10%)
  local copies, waits for them, and re-layouts  61.4 us (5%)
  other arithmetic  19.4 us (2%)
  between operations  14.5 us (1%)
    ppermute x6, waiting for transfers between devices, from_behind(): return lax.ppermute(value, axis, pairs)  573 us
    dot_general x6, matrix products, core_rows(): lax.dot_general(reduced, flattened, (((1,), (1,)), ((), ())), preferred_e...  107 us
    reduce_scatter x6, waiting for transfers between devices, per_device(): lax.psum_scatter(projected, 'tensor', scatter_dimension=0, tiled=True)  84.2 us
    all_gather x12, blocking collectives, per_device(): pieces = lax.all_gather((reduced, mixing), 'tensor', axis=0, tiled=True)  79.1 us
    reduce_scatter x6, waiting for transfers between devices, per_device(): lax.psum_scatter(logits, 'tensor', scatter_dimension=0, tiled=True)  72.6 us
    dot_general x6, matrix products, per_device(): logits = jnp.dot(lowered, router_part, preferred_element_type=jnp.float32)  48.3 us
    dot_general x6, matrix products, per_device(): projected = jnp.dot(lowered, down_part, preferred_element_type=jnp.float32)  48 us
    all_gather x6, blocking collectives, per_device(): lax.all_gather(ranked, 'tensor', axis=1, tiled=True)  45.6 us
  transfers between devices with their start and end apart: 24, of which 16 were waited for; matrix products, arithmetic and copies ran while one was open for 12% of the time, Pallas kernels for 0%

commit v1 on v0

v1 whole, which is shorter than its diff:
```python
import functools

import jax
import jax.numpy as jnp
from jax import lax
from jax.experimental import pallas as pl
from jax.experimental.pallas import tpu as pltpu
from jax.sharding import PartitionSpec as P

TICKS = 6
CHUNKS = 2
EPSILON = 1e-05


def from_behind(value, axis, steps):
    count = lax.axis_size(axis)
    pairs = [(source, (source + steps) % count) for source in range(count)]
    return lax.ppermute(value, axis, pairs)


def largest_divisor(extent, limit):
    size = min(extent, limit)
    while extent % size:
        size -= 1
    return size


def project_body(d_tiles, table, h_ref, down_ref, router_ref, own_ref, sent_ref, square_ref, low_ref):
    step = pl.program_id(0)

    @pl.when(step == 0)
    def _():
        rows, features = low_ref.shape
        partial = jnp.zeros((rows, 128), jnp.float32)
        for at in range(0, features, 128):
            piece = h_ref[:, at : at + 128]
            wide = piece.astype(jnp.float32)
            partial = partial + wide * wide
            low_ref[:, at : at + 128] = piece.astype(jnp.bfloat16)
        square_ref[...] = jnp.sum(partial.T, axis=0, keepdims=True)

    def emit(weight):
        value = jnp.dot(low_ref[...], weight, preferred_element_type=jnp.float32)
        own_ref[...] = value
        sent_ref[...] = value.astype(jnp.bfloat16)

    @pl.when(step < d_tiles)
    def _():
        emit(down_ref[...])

    @pl.when(step >= d_tiles)
    def _():
        emit(router_ref[...])


def project(table, tick, h, row_block, rows, down, router):
    features, d_rank = down.shape[2:]
    experts = router.shape[3]
    block = largest_divisor(d_rank, 256)
    d_tiles, r_tiles = d_rank // block, experts // block
    total = d_rank + experts
    return pl.pallas_call(
        functools.partial(project_body, d_tiles),
        grid_spec=pltpu.PrefetchScalarGridSpec(
            num_scalar_prefetch=1,
            grid=(d_tiles + r_tiles,),
            in_specs=[
                pl.BlockSpec((rows, features), lambda i, t: (row_block, 0), pipeline_mode=pl.Buffered(1)),
                pl.BlockSpec((None, None, features, block), lambda i, t: (t[tick], 0, 0, jnp.minimum(i, d_tiles - 1))),
                pl.BlockSpec((None, None, features, block), lambda i, t: (t[tick], 0, 0, jnp.maximum(i - d_tiles, 0))),
            ],
            out_specs=[
                pl.BlockSpec((rows, block), lambda i, t: (0, i)),
                pl.BlockSpec((rows, block), lambda i, t: (0, i)),
                pl.BlockSpec((1, rows), lambda i, t: (0, 0)),
            ],
            scratch_shapes=[pltpu.VMEM((rows, features), jnp.bfloat16)],
        ),
        out_shape=[
            jax.ShapeDtypeStruct((rows, total), jnp.float32),
            jax.ShapeDtypeStruct((rows, total), jnp.bfloat16),
            jax.ShapeDtypeStruct((1, rows), jnp.float32),
        ],
        cost_estimate=pl.CostEstimate(
            flops=2 * rows * features * total,
            bytes_accessed=2 * features * total + 2 * rows * features + 6 * rows * total,
            transcendentals=0,
        ),
        name="project",
    )(table, h, down, router)


def core_body(others, width, d_rank, table, own_ref, square_ref, *rest):
    sent_refs, squares = rest[:others], rest[others : 2 * others]
    expert_ref, core_ref, out_ref, reduced_ref, mixing_ref, ranked_ref = rest[2 * others :]
    step = pl.program_id(0)

    @pl.when(step == 0)
    def _():
        square = square_ref[...]
        for other in squares:
            square = square + other[...]
        rows = square.shape[1]
        factor = lax.rsqrt(square / width + EPSILON)
        factor = jnp.broadcast_to(factor, (128, rows)).T

        def total(at, size):
            value = own_ref[:, at : at + size]
            for other in sent_refs:
                value = value + other[:, at : at + size].astype(jnp.float32)
            return value

        for at in range(0, d_rank, 128):
            reduced_ref[at : at + 128, :] = (total(at, 128) * factor).astype(jnp.bfloat16).T
        mixing = jnp.zeros(mixing_ref.shape, jnp.float32)
        for at in range(0, expert_ref.shape[1], 128):
            gating = jax.nn.sigmoid(total(d_rank + at, 128) * factor).astype(jnp.bfloat16)
            mixing = mixing + lax.dot_general(
                expert_ref[:, at : at + 128], gating, (((1,), (1,)), ((), ())), preferred_element_type=jnp.float32
            )
        mixing_ref[...] = mixing.astype(jnp.bfloat16).astype(jnp.float32)

    block, ranks, depth = core_ref.shape
    group = 8
    mixing = mixing_ref[...]
    reduced = reduced_ref[...]
    for at in range(0, block, group):
        part = core_ref[at : at + group].reshape(group * ranks, depth)
        value = jnp.dot(part, reduced, preferred_element_type=jnp.float32)
        value = value.reshape(group, ranks, value.shape[1]) * mixing[None]
        ranked_ref[pl.ds(pl.multiple_of(step * block, group) + at, group), :] = jnp.sum(value, axis=1)

    @pl.when(step == pl.num_programs(0) - 1)
    def _():
        out_ref[...] = ranked_ref[...].T.astype(jnp.bfloat16)


def core(table, tick, own, square, sent, squares, expert, core_tensor, width):
    rows, total = own.shape
    ranks, experts = expert.shape[2:]
    f_rank, _, d_rank = core_tensor.shape[2:]
    block = largest_divisor(f_rank, 32)
    others = len(sent)
    whole = lambda i, t: (0, 0)
    return pl.pallas_call(
        functools.partial(core_body, others, width, d_rank),
        grid_spec=pltpu.PrefetchScalarGridSpec(
            num_scalar_prefetch=1,
            grid=(f_rank // block,),
            in_specs=[pl.BlockSpec((rows, total), whole), pl.BlockSpec((1, rows), whole)]
            + [pl.BlockSpec((rows, total), whole)] * others
            + [pl.BlockSpec((1, rows), whole)] * others
            + [
                pl.BlockSpec((None, None, ranks, experts), lambda i, t: (t[tick], 0, 0, 0)),
                pl.BlockSpec((None, None, block, ranks, d_rank), lambda i, t: (t[tick], 0, i, 0, 0)),
            ],
            out_specs=pl.BlockSpec((rows, f_rank), whole),
            scratch_shapes=[
                pltpu.VMEM((d_rank, rows), jnp.bfloat16),
                pltpu.VMEM((ranks, rows), jnp.float32),
                pltpu.VMEM((f_rank, rows), jnp.float32),
            ],
        ),
        out_shape=jax.ShapeDtypeStruct((rows, f_rank), jnp.bfloat16),
        cost_estimate=pl.CostEstimate(
            flops=2 * rows * f_rank * ranks * d_rank,
            bytes_accessed=2 * f_rank * ranks * d_rank + 6 * rows * total,
            transcendentals=rows * experts,
        ),
        name="core",
    )(table, own, square, *sent, *squares, expert, core_tensor)


def advance_body(pieces, table, h_ref, *rest):
    ranked, ups, out_ref = rest[:pieces], rest[pieces : 2 * pieces], rest[2 * pieces]
    value = h_ref[...].astype(jnp.float32)
    for left, right in zip(ranked, ups):
        value = value + jnp.dot(left[...], right[...], preferred_element_type=jnp.float32)
    out_ref[...] = value.astype(out_ref.dtype)


def advance(table, tick, h, row_block, ranked, up):
    pieces = len(ranked)
    rows, f_rank = ranked[0].shape
    features = up.shape[3]
    block = largest_divisor(features, 1024)

    def up_map(shift):
        def index(i, t):
            return (t[tick], 0, lax.rem(t[TICKS] + pieces - shift, pieces), i)

        return index

    return pl.pallas_call(
        functools.partial(advance_body, pieces),
        grid_spec=pltpu.PrefetchScalarGridSpec(
            num_scalar_prefetch=1,
            grid=(features // block,),
            in_specs=[pl.BlockSpec((rows, block), lambda i, t: (row_block, i))]
            + [pl.BlockSpec((rows, f_rank), lambda i, t: (0, 0))] * pieces
            + [pl.BlockSpec((None, None, f_rank, block), up_map(shift)) for shift in range(pieces)],
            out_specs=pl.BlockSpec((rows, block), lambda i, t: (0, i)),
        ),
        out_shape=jax.ShapeDtypeStruct((rows, features), jnp.bfloat16),
        cost_estimate=pl.CostEstimate(
            flops=2 * rows * f_rank * pieces * features,
            bytes_accessed=2 * f_rank * pieces * features + 4 * rows * features,
            transcendentals=0,
        ),
        name="advance",
    )(table, h, *ranked, *([up] * pieces))


def per_device(stream, down_factor, router, expert_factor, core_tensor, up_factor):
    section_id = lax.axis_index("section")
    sections = lax.axis_size("section")
    parts = lax.axis_size("tensor")
    front_edge = sections // 2
    ticks = jnp.arange(TICKS + 1, dtype=jnp.int32)
    laps = ((section_id - ticks) % sections < front_edge).astype(jnp.int32) + (section_id < ticks).astype(jnp.int32)
    table = jnp.where(ticks < TICKS, laps, lax.axis_index("tensor"))
    expert = jnp.swapaxes(expert_factor, 2, 3)
    width = stream.shape[2] * parts
    rows = stream.shape[1] // CHUNKS
    held = [(stream[0], at) for at in range(CHUNKS)]
    for tick in range(TICKS):
        projected = [project(table, tick, h, at, rows, down_factor, router) for h, at in held]
        if parts > 2:
            projected = [
                (lax.psum(own, "tensor"), sent, lax.psum(square, "tensor")) for own, sent, square in projected
            ]
        arrived = [
            [(from_behind(sent, "tensor", 1), from_behind(square, "tensor", 1))] if parts == 2 else []
            for _, sent, square in projected
        ]
        ranked = [
            core(
                table, tick, own, square, [sent for sent, _ in other], [squares for _, squares in other],
                expert, core_tensor, width,
            )
            for (own, _, square), other in zip(projected, arrived)
        ]
        if parts > 2:
            gathered = [[lax.all_gather(piece, "tensor", axis=1, tiled=True)] for piece in ranked]
        else:
            gathered = [[piece] + [from_behind(piece, "tensor", 1)] * (parts - 1) for piece in ranked]
        advanced = [
            advance(table, tick, h, at, pieces, up_factor) for (h, at), pieces in zip(held, gathered)
        ]
        held = [(from_behind(value, "section", 1), 0) for value in advanced]
    return jnp.concatenate([value for value, _ in held], axis=0).astype(jnp.float32)[None]


def solution(mesh):
    return jax.shard_map(
        per_device,
        mesh=mesh,
        in_specs=(
            P("section", None, "tensor"),
            P(None, "section", "tensor", None),
            P(None, "section", "tensor", None),
            P(None, "section", None, None),
            P(None, "section", "tensor", None, None),
            P(None, "section", None, "tensor"),
        ),
        out_specs=P("section", None, "tensor"),
        check_vma=False,
    )
```

time: 1200 us -> 637 us (0.53)
  waiting for transfers between devices: 731 us -> 242 us
  Pallas kernels: 0 us -> 303 us
  matrix products: 242 us -> 0 us
  blocking collectives: 125 us -> 0 us
  starting transfers between devices: 2.49 us -> 54.9 us
  local copies, waits for them, and re-layouts: 61.4 us -> 24.2 us
  other arithmetic: 19.4 us -> 5.01 us
  between operations: 14.5 us -> 0.51 us
    ppermute x6 -> x48, waiting for transfers between devices: 573 us -> 242 us  [from_behind(): return lax.ppermute(value, axis, pairs)]
    pallas_call x0 -> x36, Pallas kernels: none -> 303 us  [the longest x12 117 us: core(): pl.pallas_call(functools.partial(core_body, others, width, d_rank), grid_...]
    dot_general x30 -> x0, matrix products: 242 us -> none  [the longest x6 107 us: core_rows(): lax.dot_general(reduced, flattened, (((1,), (1,)), ((), ())), preferred_e...]
    reduce_scatter x12 -> x0, waiting for transfers between devices: 157 us -> none  [the longest x6 84.2 us: per_device(): lax.psum_scatter(projected, 'tensor', scatter_dimension=0, tiled=True)]
    all_gather x18 -> x0, blocking collectives: 125 us -> none  [the longest x12 79.1 us: per_device(): pieces = lax.all_gather((reduced, mixing), 'tensor', axis=0, tiled=True)]
    ppermute x6 -> x48, starting transfers between devices: 0.35 us -> 54.9 us  [from_behind(): return lax.ppermute(value, axis, pairs)]
    dynamic_slice x1 -> x0, local copies, waits for them, and re-layouts: 36.3 us -> none  [select_lap(): return lax.dynamic_index_in_dim(stacked[:, 0], lap_id, 0, keepdims=False)]
    unnamed x45 -> x94, local copies, waits for them, and re-layouts: 25.1 us -> 24.2 us
  transfers between devices with their start and end apart: 24 -> 48, of which waited for: 16 -> 18; matrix products, arithmetic and copies ran while one was open for 12% -> 0% of each run, Pallas kernels for 0% -> 47%
where the time goes in v1:
time: 637 us; the launch traced here: 629 us
  Pallas kernels  303 us (48%)
  waiting for transfers between devices  242 us (38%)
  starting transfers between devices  54.9 us (9%)
  local copies, waits for them, and re-layouts  24.2 us (4%)
    ppermute x48, waiting for transfers between devices, from_behind(): return lax.ppermute(value, axis, pairs)  242 us
    pallas_call x12, Pallas kernels, core(): pl.pallas_call(functools.partial(core_body, others, width, d_rank), grid_...  117 us
    pallas_call x12, Pallas kernels, project(): pl.pallas_call(functools.partial(project_body, d_tiles), grid_spec=pltpu....  109 us
    pallas_call x12, Pallas kernels, advance(): pl.pallas_call(functools.partial(advance_body, pieces), grid_spec=pltpu.P...  76.7 us
    ppermute x48, starting transfers between devices, from_behind(): return lax.ppermute(value, axis, pairs)  54.9 us
    unnamed x94, local copies, waits for them, and re-layouts  24.2 us
  transfers between devices with their start and end apart: 48, of which 18 were waited for; matrix products, arithmetic and copies ran while one was open for 0% of the time, Pallas kernels for 47%

profile of v1, /device:TPU:0, one launch (start us, length us, event | category | flops | bytes accessed | tf_op | source)
XLA Modules:
  0.0 628.8 jit_solution(13940761593797654203)
XLA Ops:
  0.5 9.7 %project.18 = (f32[256,1024]{1,0:T(8,128)}, bf16[256,1024]{1,0:T(8,128)(2,1)}, f32[1,256]{1,0:T(1,128)}) custom-call(s32[7]{0:T(128)} %compare_select_fusion.2.table, f32[512,4096]{1,0:T(8,128)} %bitcast.4, bf16[2,1,4096,512]{3,2,1,0:T(8,128)(2,1)} %down_ref.23, bf16[2,1,4096,512]{3,2,1,0:T(8,128)(2,1)} %router_ref.23), custom_call_target="tpu_custom_call" | custom-call | flops 2147483648 | bytes 12058624 | tf_op jit(solution)/shard_map/project/pallas_call | solution.py:62
  13.3 9.8 %project.12 = (f32[256,1024]{1,0:T(8,128)}, bf16[256,1024]{1,0:T(8,128)(2,1)}, f32[1,256]{1,0:T(1,128)}) custom-call(s32[7]{0:T(128)} %compare_select_fusion.2.table, f32[512,4096]{1,0:T(8,128)} %bitcast.5, bf16[2,1,4096,512]{3,2,1,0:T(8,128)(2,1)} %down_ref.23, bf16[2,1,4096,512]{3,2,1,0:T(8,128)(2,1)} %router_ref.23), custom_call_target="tpu_custom_call" | custom-call | flops 2147483648 | bytes 12058624 | tf_op jit(solution)/shard_map/project/pallas_call | solution.py:62
  25.1 11.6 %collective-permute-done.25.rest_1_ = f32[1,256]{1,0:T(1,128)S(1)} collective-permute-done((f32[1,256]{1,0:T(1,128)S(1)}, f32[1,256]{1,0:T(1,128)S(1)}, u32[]{:S(2)}, u32[]{:S(2)}) %collective-permute-start.25) | collective-permute-done | bytes 1056 | tf_op jit(solution)/shard_map/ppermute | solution.py:18
  37.5 9.7 %core.18.rest_0_ = bf16[256,256]{1,0:T(8,128)(2,1)} custom-call(s32[7]{0:T(128)} %compare_select_fusion.2.table, f32[256,1024]{1,0:T(8,128)} %get-tuple-element.59.own_ref, f32[1,256]{1,0:T(1,128)} %get-tuple-element.60.square_ref, bf16[256,1024]{1,0:T(8,128)(2,1)} %copy-done.16, f32[1,256]{1,0:T(1,128)} %copy-done.41, bf16[2,1,32,512]{3,2,1,0:T(8,128)(2,1)} %bitcast.8, ...), custom_call_target="tpu_custom_call" | custom-call | flops 2147483648 | bytes 9961472 | tf_op jit(solution)/shard_map/core/pallas_call | solution.py:145
  49.8 9.7 %core.12.rest_0_ = bf16[256,256]{1,0:T(8,128)(2,1)} custom-call(s32[7]{0:T(128)} %compare_select_fusion.2.table, f32[256,1024]{1,0:T(8,128)} %get-tuple-element.41.own_ref, f32[1,256]{1,0:T(1,128)} %get-tuple-element.42.square_ref, bf16[256,1024]{1,0:T(8,128)(2,1)} %copy-done.5, f32[1,256]{1,0:T(1,128)} %copy-done.35, bf16[2,1,32,512]{3,2,1,0:T(8,128)(2,1)} %bitcast.9, ...), custom_call_target="tpu_custom_call" | custom-call | flops 2147483648 | bytes 9961472 | tf_op jit(solution)/shard_map/core/pallas_call | solution.py:145
  60.5 6.7 %advance.18 = bf16[256,4096]{1,0:T(8,128)(2,1)} custom-call(s32[7]{0:T(128)} %compare_select_fusion.2.table, f32[512,4096]{1,0:T(8,128)} %bitcast.6, bf16[256,256]{1,0:T(8,128)(2,1)} %core.18.rest_0_, bf16[256,256]{1,0:T(8,128)(2,1)} %copy-done.22, bf16[2,1,512,4096]{3,2,1,0:T(8,128)(2,1)} %rest_3_.47, bf16[2,1,512,4096]{3,2,1,0:T(8,128)(2,1)} %rest_3_.47), custom_call_target="tpu_custom_call" | custom-call | flops 1073741824 | bytes 8388608 | tf_op jit(solution)/shard_map/advance/pallas_call | solution.py:194
  67.9 6.8 %advance.12 = bf16[256,4096]{1,0:T(8,128)(2,1)} custom-call(s32[7]{0:T(128)} %compare_select_fusion.2.table, f32[512,4096]{1,0:T(8,128)} %bitcast.7, bf16[256,256]{1,0:T(8,128)(2,1)} %core.12.rest_0_, bf16[256,256]{1,0:T(8,128)(2,1)} %copy-done.28, bf16[2,1,512,4096]{3,2,1,0:T(8,128)(2,1)} %rest_3_.47, bf16[2,1,512,4096]{3,2,1,0:T(8,128)(2,1)} %rest_3_.47), custom_call_target="tpu_custom_call" | custom-call | flops 1073741824 | bytes 8388608 | tf_op jit(solution)/shard_map/advance/pallas_call | solution.py:194
  76.8 18.9 %collective-permute-done.27.h_ref = bf16[256,4096]{1,0:T(8,128)(2,1)} collective-permute-done((bf16[256,4096]{1,0:T(8,128)(2,1)}, bf16[256,4096]{1,0:T(8,128)(2,1)}, u32[]{:S(2)}, u32[]{:S(2)}) %collective-permute-start.27) | collective-permute-done | bytes 2097184 | tf_op jit(solution)/shard_map/ppermute | solution.py:18
  95.7 8.9 %project.19 = (f32[256,1024]{1,0:T(8,128)}, bf16[256,1024]{1,0:T(8,128)(2,1)}, f32[1,256]{1,0:T(1,128)}) custom-call(s32[7]{0:T(128)} %compare_select_fusion.2.table, bf16[256,4096]{1,0:T(8,128)(2,1)} %collective-permute-done.27.h_ref, bf16[2,1,4096,512]{3,2,1,0:T(8,128)(2,1)} %down_ref.23, bf16[2,1,4096,512]{3,2,1,0:T(8,128)(2,1)} %router_ref.23), custom_call_target="tpu_custom_call" | custom-call | flops 2147483648 | bytes 12058624 | tf_op jit(solution)/shard_map/project/pallas_call | solution.py:62
  106.4 11.6 %collective-permute-done.3.h_ref = bf16[256,4096]{1,0:T(8,128)(2,1)S(1)} collective-permute-done((bf16[256,4096]{1,0:T(8,128)(2,1)}, bf16[256,4096]{1,0:T(8,128)(2,1)S(1)}, u32[]{:S(2)}, u32[]{:S(2)}) %collective-permute-start.3) | collective-permute-done | bytes 2097184 | tf_op jit(solution)/shard_map/ppermute | solution.py:18
  119.4 9.0 %project.13 = (f32[256,1024]{1,0:T(8,128)}, bf16[256,1024]{1,0:T(8,128)(2,1)}, f32[1,256]{1,0:T(1,128)}) custom-call(s32[7]{0:T(128)} %compare_select_fusion.2.table, bf16[256,4096]{1,0:T(8,128)(2,1)} %copy-done.1, bf16[2,1,4096,512]{3,2,1,0:T(8,128)(2,1)} %down_ref.23, bf16[2,1,4096,512]{3,2,1,0:T(8,128)(2,1)} %router_ref.23), custom_call_target="tpu_custom_call" | custom-call | flops 2147483648 | bytes 12058624 | tf_op jit(solution)/shard_map/project/pallas_call | solution.py:62
  132.1 7.1 %collective-permute-done.29.rest_1_ = f32[1,256]{1,0:T(1,128)S(1)} collective-permute-done((f32[1,256]{1,0:T(1,128)S(1)}, f32[1,256]{1,0:T(1,128)S(1)}, u32[]{:S(2)}, u32[]{:S(2)}) %collective-permute-start.29) | collective-permute-done | bytes 1056 | tf_op jit(solution)/shard_map/ppermute | solution.py:18
  140.0 9.7 %core.19.rest_0_ = bf16[256,256]{1,0:T(8,128)(2,1)} custom-call(s32[7]{0:T(128)} %compare_select_fusion.2.table, f32[256,1024]{1,0:T(8,128)} %get-tuple-element.62.own_ref, f32[1,256]{1,0:T(1,128)} %get-tuple-element.63.square_ref, bf16[256,1024]{1,0:T(8,128)(2,1)} %copy-done.11, f32[1,256]{1,0:T(1,128)} %copy-done.42, bf16[2,1,32,512]{3,2,1,0:T(8,128)(2,1)} %bitcast.10, ...), custom_call_target="tpu_custom_call" | custom-call | flops 2147483648 | bytes 9961472 | tf_op jit(solution)/shard_map/core/pallas_call | solution.py:145
  152.1 9.7 %core.13.rest_0_ = bf16[256,256]{1,0:T(8,128)(2,1)} custom-call(s32[7]{0:T(128)} %compare_select_fusion.2.table, f32[256,1024]{1,0:T(8,128)} %get-tuple-element.44.own_ref, f32[1,256]{1,0:T(1,128)} %get-tuple-element.45.square_ref, bf16[256,1024]{1,0:T(8,128)(2,1)} %copy-done.6, f32[1,256]{1,0:T(1,128)} %copy-done.36, bf16[2,1,32,512]{3,2,1,0:T(8,128)(2,1)} %bitcast.11, ...), custom_call_target="tpu_custom_call" | custom-call | flops 2147483648 | bytes 9961472 | tf_op jit(solution)/shard_map/core/pallas_call | solution.py:145
  169.9 6.4 %advance.13 = bf16[256,4096]{1,0:T(8,128)(2,1)} custom-call(s32[7]{0:T(128)} %compare_select_fusion.2.table, bf16[256,4096]{1,0:T(8,128)(2,1)} %copy-done.1, bf16[256,256]{1,0:T(8,128)(2,1)} %core.13.rest_0_, bf16[256,256]{1,0:T(8,128)(2,1)} %copy-done.24, bf16[2,1,512,4096]{3,2,1,0:T(8,128)(2,1)} %rest_3_.47, bf16[2,1,512,4096]{3,2,1,0:T(8,128)(2,1)} %rest_3_.47), custom_call_target="tpu_custom_call" | custom-call | flops 1073741824 | bytes 8388608 | tf_op jit(solution)/shard_map/advance/pallas_call | solution.py:194
  178.5 19.1 %collective-permute-done.31.h_ref = bf16[256,4096]{1,0:T(8,128)(2,1)S(1)} collective-permute-done((bf16[256,4096]{1,0:T(8,128)(2,1)}, bf16[256,4096]{1,0:T(8,128)(2,1)S(1)}, u32[]{:S(2)}, u32[]{:S(2)}) %collective-permute-start.31) | collective-permute-done | bytes 2097184 | tf_op jit(solution)/shard_map/ppermute | solution.py:18
  199.0 9.0 %project.20 = (f32[256,1024]{1,0:T(8,128)}, bf16[256,1024]{1,0:T(8,128)(2,1)}, f32[1,256]{1,0:T(1,128)}) custom-call(s32[7]{0:T(128)} %compare_select_fusion.2.table, bf16[256,4096]{1,0:T(8,128)(2,1)} %copy-done.2, bf16[2,1,4096,512]{3,2,1,0:T(8,128)(2,1)} %down_ref.23, bf16[2,1,4096,512]{3,2,1,0:T(8,128)(2,1)} %router_ref.23), custom_call_target="tpu_custom_call" | custom-call | flops 2147483648 | bytes 12058624 | tf_op jit(solution)/shard_map/project/pallas_call | solution.py:62
  209.5 10.7 %collective-permute-done.7.h_ref = bf16[256,4096]{1,0:T(8,128)(2,1)} collective-permute-done((bf16[256,4096]{1,0:T(8,128)(2,1)}, bf16[256,4096]{1,0:T(8,128)(2,1)}, u32[]{:S(2)}, u32[]{:S(2)}) %collective-permute-start.7) | collective-permute-done | bytes 2097184 | tf_op jit(solution)/shard_map/ppermute | solution.py:18
  220.2 9.0 %project.14 = (f32[256,1024]{1,0:T(8,128)}, bf16[256,1024]{1,0:T(8,128)(2,1)}, f32[1,256]{1,0:T(1,128)}) custom-call(s32[7]{0:T(128)} %compare_select_fusion.2.table, bf16[256,4096]{1,0:T(8,128)(2,1)} %collective-permute-done.7.h_ref, bf16[2,1,4096,512]{3,2,1,0:T(8,128)(2,1)} %down_ref.23, bf16[2,1,4096,512]{3,2,1,0:T(8,128)(2,1)} %router_ref.23), custom_call_target="tpu_custom_call" | custom-call | flops 2147483648 | bytes 12058624 | tf_op jit(solution)/shard_map/project/pallas_call | solution.py:62
  232.8 7.0 %collective-permute-done.33.rest_1_ = f32[1,256]{1,0:T(1,128)S(1)} collective-permute-done((f32[1,256]{1,0:T(1,128)S(1)}, f32[1,256]{1,0:T(1,128)S(1)}, u32[]{:S(2)}, u32[]{:S(2)}) %collective-permute-start.33) | collective-permute-done | bytes 1056 | tf_op jit(solution)/shard_map/ppermute | solution.py:18
  240.7 9.7 %core.20.rest_0_ = bf16[256,256]{1,0:T(8,128)(2,1)} custom-call(s32[7]{0:T(128)} %compare_select_fusion.2.table, f32[256,1024]{1,0:T(8,128)} %get-tuple-element.65.own_ref, f32[1,256]{1,0:T(1,128)} %get-tuple-element.66.square_ref, bf16[256,1024]{1,0:T(8,128)(2,1)} %copy-done.12, f32[1,256]{1,0:T(1,128)} %copy-done.43, bf16[2,1,32,512]{3,2,1,0:T(8,128)(2,1)} %bitcast.12, ...), custom_call_target="tpu_custom_call" | custom-call | flops 2147483648 | bytes 9961472 | tf_op jit(solution)/shard_map/core/pallas_call | solution.py:145
  252.7 9.7 %core.14.rest_0_ = bf16[256,256]{1,0:T(8,128)(2,1)} custom-call(s32[7]{0:T(128)} %compare_select_fusion.2.table, f32[256,1024]{1,0:T(8,128)} %get-tuple-element.47.own_ref, f32[1,256]{1,0:T(1,128)} %get-tuple-element.48.square_ref, bf16[256,1024]{1,0:T(8,128)(2,1)} %copy-done.7, f32[1,256]{1,0:T(1,128)} %copy-done.37, bf16[2,1,32,512]{3,2,1,0:T(8,128)(2,1)} %bitcast.13, ...), custom_call_target="tpu_custom_call" | custom-call | flops 2147483648 | bytes 9961472 | tf_op jit(solution)/shard_map/core/pallas_call | solution.py:145
  263.6 6.4 %advance.20 = bf16[256,4096]{1,0:T(8,128)(2,1)} custom-call(s32[7]{0:T(128)} %compare_select_fusion.2.table, bf16[256,4096]{1,0:T(8,128)(2,1)} %copy-done.2, bf16[256,256]{1,0:T(8,128)(2,1)} %core.20.rest_0_, bf16[256,256]{1,0:T(8,128)(2,1)} %copy-done.18, bf16[2,1,512,4096]{3,2,1,0:T(8,128)(2,1)} %rest_3_.47, bf16[2,1,512,4096]{3,2,1,0:T(8,128)(2,1)} %rest_3_.47), custom_call_target="tpu_custom_call" | custom-call | flops 1073741824 | bytes 8388608 | tf_op jit(solution)/shard_map/advance/pallas_call | solution.py:194
  278.7 19.6 %collective-permute-done.35.h_ref = bf16[256,4096]{1,0:T(8,128)(2,1)S(1)} collective-permute-done((bf16[256,4096]{1,0:T(8,128)(2,1)}, bf16[256,4096]{1,0:T(8,128)(2,1)S(1)}, u32[]{:S(2)}, u32[]{:S(2)}) %collective-permute-start.35) | collective-permute-done | bytes 2097184 | tf_op jit(solution)/shard_map/ppermute | solution.py:18
  299.6 9.0 %project.21 = (f32[256,1024]{1,0:T(8,128)}, bf16[256,1024]{1,0:T(8,128)(2,1)}, f32[1,256]{1,0:T(1,128)}) custom-call(s32[7]{0:T(128)} %compare_select_fusion.2.table, bf16[256,4096]{1,0:T(8,128)(2,1)} %copy-done.3, bf16[2,1,4096,512]{3,2,1,0:T(8,128)(2,1)} %down_ref.23, bf16[2,1,4096,512]{3,2,1,0:T(8,128)(2,1)} %router_ref.23), custom_call_target="tpu_custom_call" | custom-call | flops 2147483648 | bytes 12058624 | tf_op jit(solution)/shard_map/project/pallas_call | solution.py:62
  310.2 10.7 %collective-permute-done.11.h_ref = bf16[256,4096]{1,0:T(8,128)(2,1)} collective-permute-done((bf16[256,4096]{1,0:T(8,128)(2,1)}, bf16[256,4096]{1,0:T(8,128)(2,1)}, u32[]{:S(2)}, u32[]{:S(2)}) %collective-permute-start.11) | collective-permute-done | bytes 2097184 | tf_op jit(solution)/shard_map/ppermute | solution.py:18
  320.9 9.0 %project.15 = (f32[256,1024]{1,0:T(8,128)}, bf16[256,1024]{1,0:T(8,128)(2,1)}, f32[1,256]{1,0:T(1,128)}) custom-call(s32[7]{0:T(128)} %compare_select_fusion.2.table, bf16[256,4096]{1,0:T(8,128)(2,1)} %collective-permute-done.11.h_ref, bf16[2,1,4096,512]{3,2,1,0:T(8,128)(2,1)} %down_ref.23, bf16[2,1,4096,512]{3,2,1,0:T(8,128)(2,1)} %router_ref.23), custom_call_target="tpu_custom_call" | custom-call | flops 2147483648 | bytes 12058624 | tf_op jit(solution)/shard_map/project/pallas_call | solution.py:62
  333.5 7.0 %collective-permute-done.37.rest_1_ = f32[1,256]{1,0:T(1,128)S(1)} collective-permute-done((f32[1,256]{1,0:T(1,128)S(1)}, f32[1,256]{1,0:T(1,128)S(1)}, u32[]{:S(2)}, u32[]{:S(2)}) %collective-permute-start.37) | collective-permute-done | bytes 1056 | tf_op jit(solution)/shard_map/ppermute | solution.py:18
  341.3 9.7 %core.21.rest_0_ = bf16[256,256]{1,0:T(8,128)(2,1)} custom-call(s32[7]{0:T(128)} %compare_select_fusion.2.table, f32[256,1024]{1,0:T(8,128)} %get-tuple-element.68.own_ref, f32[1,256]{1,0:T(1,128)} %get-tuple-element.69.square_ref, bf16[256,1024]{1,0:T(8,128)(2,1)} %copy-done.13, f32[1,256]{1,0:T(1,128)} %copy-done.44, bf16[2,1,32,512]{3,2,1,0:T(8,128)(2,1)} %bitcast.14, ...), custom_call_target="tpu_custom_call" | custom-call | flops 2147483648 | bytes 9961472 | tf_op jit(solution)/shard_map/core/pallas_call | solution.py:145
  353.4 9.7 %core.15.rest_0_ = bf16[256,256]{1,0:T(8,128)(2,1)} custom-call(s32[7]{0:T(128)} %compare_select_fusion.2.table, f32[256,1024]{1,0:T(8,128)} %get-tuple-element.50.own_ref, f32[1,256]{1,0:T(1,128)} %get-tuple-element.51.square_ref, bf16[256,1024]{1,0:T(8,128)(2,1)} %copy-done.8, f32[1,256]{1,0:T(1,128)} %copy-done.38, bf16[2,1,32,512]{3,2,1,0:T(8,128)(2,1)} %bitcast.15, ...), custom_call_target="tpu_custom_call" | custom-call | flops 2147483648 | bytes 9961472 | tf_op jit(solution)/shard_map/core/pallas_call | solution.py:145
  364.3 6.4 %advance.21 = bf16[256,4096]{1,0:T(8,128)(2,1)} custom-call(s32[7]{0:T(128)} %compare_select_fusion.2.table, bf16[256,4096]{1,0:T(8,128)(2,1)} %copy-done.3, bf16[256,256]{1,0:T(8,128)(2,1)} %core.21.rest_0_, bf16[256,256]{1,0:T(8,128)(2,1)} %copy-done.19, bf16[2,1,512,4096]{3,2,1,0:T(8,128)(2,1)} %rest_3_.47, bf16[2,1,512,4096]{3,2,1,0:T(8,128)(2,1)} %rest_3_.47), custom_call_target="tpu_custom_call" | custom-call | flops 1073741824 | bytes 8388608 | tf_op jit(solution)/shard_map/advance/pallas_call | solution.py:194
  379.5 19.5 %collective-permute-done.39.h_ref = bf16[256,4096]{1,0:T(8,128)(2,1)S(1)} collective-permute-done((bf16[256,4096]{1,0:T(8,128)(2,1)}, bf16[256,4096]{1,0:T(8,128)(2,1)S(1)}, u32[]{:S(2)}, u32[]{:S(2)}) %collective-permute-start.39) | collective-permute-done | bytes 2097184 | tf_op jit(solution)/shard_map/ppermute | solution.py:18
  400.3 9.0 %project.22 = (f32[256,1024]{1,0:T(8,128)}, bf16[256,1024]{1,0:T(8,128)(2,1)}, f32[1,256]{1,0:T(1,128)}) custom-call(s32[7]{0:T(128)} %compare_select_fusion.2.table, bf16[256,4096]{1,0:T(8,128)(2,1)} %copy-done.4, bf16[2,1,4096,512]{3,2,1,0:T(8,128)(2,1)} %down_ref.23, bf16[2,1,4096,512]{3,2,1,0:T(8,128)(2,1)} %router_ref.23), custom_call_target="tpu_custom_call" | custom-call | flops 2147483648 | bytes 12058624 | tf_op jit(solution)/shard_map/project/pallas_call | solution.py:62
  410.8 10.7 %collective-permute-done.15.h_ref = bf16[256,4096]{1,0:T(8,128)(2,1)} collective-permute-done((bf16[256,4096]{1,0:T(8,128)(2,1)}, bf16[256,4096]{1,0:T(8,128)(2,1)}, u32[]{:S(2)}, u32[]{:S(2)}) %collective-permute-start.15) | collective-permute-done | bytes 2097184 | tf_op jit(solution)/shard_map/ppermute | solution.py:18
  421.6 9.0 %project.16 = (f32[256,1024]{1,0:T(8,128)}, bf16[256,1024]{1,0:T(8,128)(2,1)}, f32[1,256]{1,0:T(1,128)}) custom-call(s32[7]{0:T(128)} %compare_select_fusion.2.table, bf16[256,4096]{1,0:T(8,128)(2,1)} %collective-permute-done.15.h_ref, bf16[2,1,4096,512]{3,2,1,0:T(8,128)(2,1)} %down_ref.23, bf16[2,1,4096,512]{3,2,1,0:T(8,128)(2,1)} %router_ref.23), custom_call_target="tpu_custom_call" | custom-call | flops 2147483648 | bytes 12058624 | tf_op jit(solution)/shard_map/project/pallas_call | solution.py:62
  434.2 7.0 %collective-permute-done.41.rest_1_ = f32[1,256]{1,0:T(1,128)S(1)} collective-permute-done((f32[1,256]{1,0:T(1,128)S(1)}, f32[1,256]{1,0:T(1,128)S(1)}, u32[]{:S(2)}, u32[]{:S(2)}) %collective-permute-start.41) | collective-permute-done | bytes 1056 | tf_op jit(solution)/shard_map/ppermute | solution.py:18
  442.1 9.7 %core.22.rest_0_ = bf16[256,256]{1,0:T(8,128)(2,1)} custom-call(s32[7]{0:T(128)} %compare_select_fusion.2.table, f32[256,1024]{1,0:T(8,128)} %get-tuple-element.71.own_ref, f32[1,256]{1,0:T(1,128)} %get-tuple-element.72.square_ref, bf16[256,1024]{1,0:T(8,128)(2,1)} %copy-done.14, f32[1,256]{1,0:T(1,128)} %copy-done.45, bf16[2,1,32,512]{3,2,1,0:T(8,128)(2,1)} %bitcast.16, ...), custom_call_target="tpu_custom_call" | custom-call | flops 2147483648 | bytes 9961472 | tf_op jit(solution)/shard_map/core/pallas_call | solution.py:145
  454.1 9.7 %core.16.rest_0_ = bf16[256,256]{1,0:T(8,128)(2,1)} custom-call(s32[7]{0:T(128)} %compare_select_fusion.2.table, f32[256,1024]{1,0:T(8,128)} %get-tuple-element.53.own_ref, f32[1,256]{1,0:T(1,128)} %get-tuple-element.54.square_ref, bf16[256,1024]{1,0:T(8,128)(2,1)} %copy-done.9, f32[1,256]{1,0:T(1,128)} %copy-done.39, bf16[2,1,32,512]{3,2,1,0:T(8,128)(2,1)} %bitcast.17, ...), custom_call_target="tpu_custom_call" | custom-call | flops 2147483648 | bytes 9961472 | tf_op jit(solution)/shard_map/core/pallas_call | solution.py:145
  465.0 6.4 %advance.22 = bf16[256,4096]{1,0:T(8,128)(2,1)} custom-call(s32[7]{0:T(128)} %compare_select_fusion.2.table, bf16[256,4096]{1,0:T(8,128)(2,1)} %copy-done.4, bf16[256,256]{1,0:T(8,128)(2,1)} %core.22.rest_0_, bf16[256,256]{1,0:T(8,128)(2,1)} %copy-done.20, bf16[2,1,512,4096]{3,2,1,0:T(8,128)(2,1)} %rest_3_.47, bf16[2,1,512,4096]{3,2,1,0:T(8,128)(2,1)} %rest_3_.47), custom_call_target="tpu_custom_call" | custom-call | flops 1073741824 | bytes 8388608 | tf_op jit(solution)/shard_map/advance/pallas_call | solution.py:194
  480.1 19.7 %collective-permute-done.43.h_ref = bf16[256,4096]{1,0:T(8,128)(2,1)} collective-permute-done((bf16[256,4096]{1,0:T(8,128)(2,1)}, bf16[256,4096]{1,0:T(8,128)(2,1)}, u32[]{:S(2)}, u32[]{:S(2)}) %collective-permute-start.43) | collective-permute-done | bytes 2097184 | tf_op jit(solution)/shard_map/ppermute | solution.py:18
  499.8 9.0 %project.23 = (f32[256,1024]{1,0:T(8,128)}, bf16[256,1024]{1,0:T(8,128)(2,1)}, f32[1,256]{1,0:T(1,128)}) custom-call(s32[7]{0:T(128)} %compare_select_fusion.2.table, bf16[256,4096]{1,0:T(8,128)(2,1)} %collective-permute-done.43.h_ref, bf16[2,1,4096,512]{3,2,1,0:T(8,128)(2,1)} %down_ref.23, bf16[2,1,4096,512]{3,2,1,0:T(8,128)(2,1)} %router_ref.23), custom_call_target="tpu_custom_call" | custom-call | flops 2147483648 | bytes 12058624 | tf_op jit(solution)/shard_map/project/pallas_call | solution.py:62
  510.4 11.8 %collective-permute-done.19.h_ref = bf16[256,4096]{1,0:T(8,128)(2,1)S(1)} collective-permute-done((bf16[256,4096]{1,0:T(8,128)(2,1)}, bf16[256,4096]{1,0:T(8,128)(2,1)S(1)}, u32[]{:S(2)}, u32[]{:S(2)}) %collective-permute-start.19) | collective-permute-done | bytes 2097184 | tf_op jit(solution)/shard_map/ppermute | solution.py:18
  523.5 8.9 %project.17 = (f32[256,1024]{1,0:T(8,128)}, bf16[256,1024]{1,0:T(8,128)(2,1)}, f32[1,256]{1,0:T(1,128)}) custom-call(s32[7]{0:T(128)} %compare_select_fusion.2.table, bf16[256,4096]{1,0:T(8,128)(2,1)} %copy-done, bf16[2,1,4096,512]{3,2,1,0:T(8,128)(2,1)} %down_ref.23, bf16[2,1,4096,512]{3,2,1,0:T(8,128)(2,1)} %router_ref.23), custom_call_target="tpu_custom_call" | custom-call | flops 2147483648 | bytes 12058624 | tf_op jit(solution)/shard_map/project/pallas_call | solution.py:62
  536.1 7.1 %collective-permute-done.45.rest_1_ = f32[1,256]{1,0:T(1,128)S(1)} collective-permute-done((f32[1,256]{1,0:T(1,128)S(1)}, f32[1,256]{1,0:T(1,128)S(1)}, u32[]{:S(2)}, u32[]{:S(2)}) %collective-permute-start.45) | collective-permute-done | bytes 1056 | tf_op jit(solution)/shard_map/ppermute | solution.py:18
  544.0 9.7 %core.23.rest_0_ = bf16[256,256]{1,0:T(8,128)(2,1)} custom-call(s32[7]{0:T(128)} %compare_select_fusion.2.table, f32[256,1024]{1,0:T(8,128)} %get-tuple-element.74.own_ref, f32[1,256]{1,0:T(1,128)} %get-tuple-element.75.square_ref, bf16[256,1024]{1,0:T(8,128)(2,1)} %copy-done.15, f32[1,256]{1,0:T(1,128)} %copy-done.46, bf16[2,1,32,512]{3,2,1,0:T(8,128)(2,1)} %bitcast.18, ...), custom_call_target="tpu_custom_call" | custom-call | flops 2147483648 | bytes 9961472 | tf_op jit(solution)/shard_map/core/pallas_call | solution.py:145
  556.0 9.7 %core.17.rest_0_ = bf16[256,256]{1,0:T(8,128)(2,1)} custom-call(s32[7]{0:T(128)} %compare_select_fusion.2.table, f32[256,1024]{1,0:T(8,128)} %get-tuple-element.56.own_ref, f32[1,256]{1,0:T(1,128)} %get-tuple-element.57.square_ref, bf16[256,1024]{1,0:T(8,128)(2,1)} %copy-done.10, f32[1,256]{1,0:T(1,128)} %copy-done.40, bf16[2,1,32,512]{3,2,1,0:T(8,128)(2,1)} %bitcast.19, ...), custom_call_target="tpu_custom_call" | custom-call | flops 2147483648 | bytes 9961472 | tf_op jit(solution)/shard_map/core/pallas_call | solution.py:145
  581.8 19.7 %collective-permute-done.47 = bf16[256,4096]{1,0:T(8,128)(2,1)S(1)} collective-permute-done((bf16[256,4096]{1,0:T(8,128)(2,1)}, bf16[256,4096]{1,0:T(8,128)(2,1)S(1)}, u32[]{:S(2)}, u32[]{:S(2)}) %collective-permute-start.47) | collective-permute-done | bytes 2097184 | tf_op jit(solution)/shard_map/ppermute | solution.py:18
  601.6 22.5 %collective-permute-done.23 = bf16[256,4096]{1,0:T(8,128)(2,1)S(1)} collective-permute-done((bf16[256,4096]{1,0:T(8,128)(2,1)}, bf16[256,4096]{1,0:T(8,128)(2,1)S(1)}, u32[]{:S(2)}, u32[]{:S(2)}) %collective-permute-start.23) | collective-permute-done | bytes 2097184 | tf_op jit(solution)/shard_map/ppermute | solution.py:18
  (180 shorter events, 122.0 us)
Async XLA Ops:
  10.2 26.5 %collective-permute-start.24 = (bf16[256,1024]{1,0:T(8,128)(2,1)}, bf16[256,1024]{1,0:T(8,128)(2,1)S(1)}, u32[]{:S(2)}, u32[]{:S(2)}) collective-permute-start(bf16[256,1024]{1,0:T(8,128)(2,1)} %get-tuple-element.61), channel_id=1, source_target_pairs={{0,1},{1,0},{2,3},{3,2},{4,5},{5,4},{6,7},{7,6},{8,9},{9,8},{10,11... | collective-permute-start | bytes 1572872 | tf_op jit(solution)/shard_map/ppermute | solution.py:18
  23.0 26.0 %collective-permute-start = (bf16[256,1024]{1,0:T(8,128)(2,1)}, bf16[256,1024]{1,0:T(8,128)(2,1)S(1)}, u32[]{:S(2)}, u32[]{:S(2)}) collective-permute-start(bf16[256,1024]{1,0:T(8,128)(2,1)} %get-tuple-element.43), channel_id=1, source_target_pairs={{0,1},{1,0},{2,3},{3,2},{4,5},{5,4},{6,7},{7,6},{8,9},{9,8},{10,11... | collective-permute-start | bytes 1572872 | tf_op jit(solution)/shard_map/ppermute | solution.py:18
  23.0 13.7 %collective-permute-start.25 = (f32[1,256]{1,0:T(1,128)S(1)}, f32[1,256]{1,0:T(1,128)S(1)}, u32[]{:S(2)}, u32[]{:S(2)}) collective-permute-start(f32[1,256]{1,0:T(1,128)S(1)} %copy-done.34), channel_id=1, source_target_pairs={{0,1},{1,0},{2,3},{3,2},{4,5},{5,4},{6,7},{7,6},{8,9},{9,8},{10,11... | collective-permute-start | bytes 3080 | tf_op jit(solution)/shard_map/ppermute | solution.py:18
  25.0 23.9 %collective-permute-start.1 = (f32[1,256]{1,0:T(1,128)}, f32[1,256]{1,0:T(1,128)S(1)}, u32[]{:S(2)}, u32[]{:S(2)}) collective-permute-start(f32[1,256]{1,0:T(1,128)} %get-tuple-element.42.square_ref), channel_id=1, source_target_pairs={{0,1},{1,0},{2,3},{3,2},{4,5},{5,4},{6,7},{7,6},{8,9},{9,8},{10,11... | collective-permute-start | bytes 3080 | tf_op jit(solution)/shard_map/ppermute | solution.py:18
  47.2 12.6 %collective-permute-start.26 = (bf16[256,256]{1,0:T(8,128)(2,1)}, bf16[256,256]{1,0:T(8,128)(2,1)S(1)}, u32[]{:S(2)}, u32[]{:S(2)}) collective-permute-start(bf16[256,256]{1,0:T(8,128)(2,1)} %core.18.rest_0_), channel_id=1, source_target_pairs={{0,1},{1,0},{2,3},{3,2},{4,5},{5,4},{6,7},{7,6},{8,9},{9,8},{10,11... | collective-permute-start | bytes 393224 | tf_op jit(solution)/shard_map/ppermute | solution.py:18
  59.5 7.7 %collective-permute-start.2 = (bf16[256,256]{1,0:T(8,128)(2,1)}, bf16[256,256]{1,0:T(8,128)(2,1)S(1)}, u32[]{:S(2)}, u32[]{:S(2)}) collective-permute-start(bf16[256,256]{1,0:T(8,128)(2,1)} %core.12.rest_0_), channel_id=1, source_target_pairs={{0,1},{1,0},{2,3},{3,2},{4,5},{5,4},{6,7},{7,6},{8,9},{9,8},{10,11... | collective-permute-start | bytes 393224 | tf_op jit(solution)/shard_map/ppermute | solution.py:18
  67.2 28.5 %collective-permute-start.27 = (bf16[256,4096]{1,0:T(8,128)(2,1)}, bf16[256,4096]{1,0:T(8,128)(2,1)}, u32[]{:S(2)}, u32[]{:S(2)}) collective-permute-start(bf16[256,4096]{1,0:T(8,128)(2,1)} %advance.18), channel_id=1, source_target_pairs={{0,2},{2,4},{4,6},{6,8},{8,10},{10,12},{12,14},{14,16},{16,18},{18... | collective-permute-start | bytes 6291464 | tf_op jit(solution)/shard_map/ppermute | solution.py:18
  74.7 43.4 %collective-permute-start.3 = (bf16[256,4096]{1,0:T(8,128)(2,1)}, bf16[256,4096]{1,0:T(8,128)(2,1)S(1)}, u32[]{:S(2)}, u32[]{:S(2)}) collective-permute-start(bf16[256,4096]{1,0:T(8,128)(2,1)} %advance.12), channel_id=1, source_target_pairs={{0,2},{2,4},{4,6},{6,8},{8,10},{10,12},{12,14},{14,16},{16,18},{18... | collective-permute-start | bytes 6291464 | tf_op jit(solution)/shard_map/ppermute | solution.py:18
  104.6 34.6 %collective-permute-start.28 = (bf16[256,1024]{1,0:T(8,128)(2,1)}, bf16[256,1024]{1,0:T(8,128)(2,1)S(1)}, u32[]{:S(2)}, u32[]{:S(2)}) collective-permute-start(bf16[256,1024]{1,0:T(8,128)(2,1)} %get-tuple-element.64), channel_id=1, source_target_pairs={{0,1},{1,0},{2,3},{3,2},{4,5},{5,4},{6,7},{7,6},{8,9},{9,8},{10,11... | collective-permute-start | bytes 1572872 | tf_op jit(solution)/shard_map/ppermute | solution.py:18
  128.4 22.9 %collective-permute-start.4 = (bf16[256,1024]{1,0:T(8,128)(2,1)}, bf16[256,1024]{1,0:T(8,128)(2,1)S(1)}, u32[]{:S(2)}, u32[]{:S(2)}) collective-permute-start(bf16[256,1024]{1,0:T(8,128)(2,1)} %get-tuple-element.46), channel_id=1, source_target_pairs={{0,1},{1,0},{2,3},{3,2},{4,5},{5,4},{6,7},{7,6},{8,9},{9,8},{10,11... | collective-permute-start | bytes 1572872 | tf_op jit(solution)/shard_map/ppermute | solution.py:18
  130.1 9.1 %collective-permute-start.29 = (f32[1,256]{1,0:T(1,128)S(1)}, f32[1,256]{1,0:T(1,128)S(1)}, u32[]{:S(2)}, u32[]{:S(2)}) collective-permute-start(f32[1,256]{1,0:T(1,128)S(1)} %copy-done.29), channel_id=1, source_target_pairs={{0,1},{1,0},{2,3},{3,2},{4,5},{5,4},{6,7},{7,6},{8,9},{9,8},{10,11... | collective-permute-start | bytes 3080 | tf_op jit(solution)/shard_map/ppermute | solution.py:18
  130.4 20.9 %collective-permute-start.5 = (f32[1,256]{1,0:T(1,128)}, f32[1,256]{1,0:T(1,128)S(1)}, u32[]{:S(2)}, u32[]{:S(2)}) collective-permute-start(f32[1,256]{1,0:T(1,128)} %get-tuple-element.45.square_ref), channel_id=1, source_target_pairs={{0,1},{1,0},{2,3},{3,2},{4,5},{5,4},{6,7},{7,6},{8,9},{9,8},{10,11... | collective-permute-start | bytes 3080 | tf_op jit(solution)/shard_map/ppermute | solution.py:18
  149.8 12.6 %collective-permute-start.30 = (bf16[256,256]{1,0:T(8,128)(2,1)}, bf16[256,256]{1,0:T(8,128)(2,1)S(1)}, u32[]{:S(2)}, u32[]{:S(2)}) collective-permute-start(bf16[256,256]{1,0:T(8,128)(2,1)} %core.19.rest_0_), channel_id=1, source_target_pairs={{0,1},{1,0},{2,3},{3,2},{4,5},{5,4},{6,7},{7,6},{8,9},{9,8},{10,11... | collective-permute-start | bytes 393224 | tf_op jit(solution)/shard_map/ppermute | solution.py:18
  161.8 7.5 %collective-permute-start.6 = (bf16[256,256]{1,0:T(8,128)(2,1)}, bf16[256,256]{1,0:T(8,128)(2,1)S(1)}, u32[]{:S(2)}, u32[]{:S(2)}) collective-permute-start(bf16[256,256]{1,0:T(8,128)(2,1)} %core.13.rest_0_), channel_id=1, source_target_pairs={{0,1},{1,0},{2,3},{3,2},{4,5},{5,4},{6,7},{7,6},{8,9},{9,8},{10,11... | collective-permute-start | bytes 393224 | tf_op jit(solution)/shard_map/ppermute | solution.py:18
  169.3 28.4 %collective-permute-start.31 = (bf16[256,4096]{1,0:T(8,128)(2,1)}, bf16[256,4096]{1,0:T(8,128)(2,1)S(1)}, u32[]{:S(2)}, u32[]{:S(2)}) collective-permute-start(bf16[256,4096]{1,0:T(8,128)(2,1)} %advance.19), channel_id=1, source_target_pairs={{0,2},{2,4},{4,6},{6,8},{8,10},{10,12},{12,14},{14,16},{16,18},{18... | collective-permute-start | bytes 6291464 | tf_op jit(solution)/shard_map/ppermute | solution.py:18
  176.3 43.9 %collective-permute-start.7 = (bf16[256,4096]{1,0:T(8,128)(2,1)}, bf16[256,4096]{1,0:T(8,128)(2,1)}, u32[]{:S(2)}, u32[]{:S(2)}) collective-permute-start(bf16[256,4096]{1,0:T(8,128)(2,1)} %advance.13), channel_id=1, source_target_pairs={{0,2},{2,4},{4,6},{6,8},{8,10},{10,12},{12,14},{14,16},{16,18},{18... | collective-permute-start | bytes 6291464 | tf_op jit(solution)/shard_map/ppermute | solution.py:18
  208.0 31.9 %collective-permute-start.32 = (bf16[256,1024]{1,0:T(8,128)(2,1)}, bf16[256,1024]{1,0:T(8,128)(2,1)S(1)}, u32[]{:S(2)}, u32[]{:S(2)}) collective-permute-start(bf16[256,1024]{1,0:T(8,128)(2,1)} %get-tuple-element.67), channel_id=1, source_target_pairs={{0,1},{1,0},{2,3},{3,2},{4,5},{5,4},{6,7},{7,6},{8,9},{9,8},{10,11... | collective-permute-start | bytes 1572872 | tf_op jit(solution)/shard_map/ppermute | solution.py:18
  229.2 22.7 %collective-permute-start.8 = (bf16[256,1024]{1,0:T(8,128)(2,1)}, bf16[256,1024]{1,0:T(8,128)(2,1)S(1)}, u32[]{:S(2)}, u32[]{:S(2)}) collective-permute-start(bf16[256,1024]{1,0:T(8,128)(2,1)} %get-tuple-element.49), channel_id=1, source_target_pairs={{0,1},{1,0},{2,3},{3,2},{4,5},{5,4},{6,7},{7,6},{8,9},{9,8},{10,11... | collective-permute-start | bytes 1572872 | tf_op jit(solution)/shard_map/ppermute | solution.py:18
  230.8 9.1 %collective-permute-start.33 = (f32[1,256]{1,0:T(1,128)S(1)}, f32[1,256]{1,0:T(1,128)S(1)}, u32[]{:S(2)}, u32[]{:S(2)}) collective-permute-start(f32[1,256]{1,0:T(1,128)S(1)} %copy-done.30), channel_id=1, source_target_pairs={{0,1},{1,0},{2,3},{3,2},{4,5},{5,4},{6,7},{7,6},{8,9},{9,8},{10,11... | collective-permute-start | bytes 3080 | tf_op jit(solution)/shard_map/ppermute | solution.py:18
  231.3 20.6 %collective-permute-start.9 = (f32[1,256]{1,0:T(1,128)}, f32[1,256]{1,0:T(1,128)S(1)}, u32[]{:S(2)}, u32[]{:S(2)}) collective-permute-start(f32[1,256]{1,0:T(1,128)} %get-tuple-element.48.square_ref), channel_id=1, source_target_pairs={{0,1},{1,0},{2,3},{3,2},{4,5},{5,4},{6,7},{7,6},{8,9},{9,8},{10,11... | collective-permute-start | bytes 3080 | tf_op jit(solution)/shard_map/ppermute | solution.py:18
  250.4 12.6 %collective-permute-start.34 = (bf16[256,256]{1,0:T(8,128)(2,1)}, bf16[256,256]{1,0:T(8,128)(2,1)S(1)}, u32[]{:S(2)}, u32[]{:S(2)}) collective-permute-start(bf16[256,256]{1,0:T(8,128)(2,1)} %core.20.rest_0_), channel_id=1, source_target_pairs={{0,1},{1,0},{2,3},{3,2},{4,5},{5,4},{6,7},{7,6},{8,9},{9,8},{10,11... | collective-permute-start | bytes 393224 | tf_op jit(solution)/shard_map/ppermute | solution.py:18
  262.4 7.5 %collective-permute-start.10 = (bf16[256,256]{1,0:T(8,128)(2,1)}, bf16[256,256]{1,0:T(8,128)(2,1)S(1)}, u32[]{:S(2)}, u32[]{:S(2)}) collective-permute-start(bf16[256,256]{1,0:T(8,128)(2,1)} %core.14.rest_0_), channel_id=1, source_target_pairs={{0,1},{1,0},{2,3},{3,2},{4,5},{5,4},{6,7},{7,6},{8,9},{9,8},{10,11... | collective-permute-start | bytes 393224 | tf_op jit(solution)/shard_map/ppermute | solution.py:18
  269.9 28.4 %collective-permute-start.35 = (bf16[256,4096]{1,0:T(8,128)(2,1)}, bf16[256,4096]{1,0:T(8,128)(2,1)S(1)}, u32[]{:S(2)}, u32[]{:S(2)}) collective-permute-start(bf16[256,4096]{1,0:T(8,128)(2,1)} %advance.20), channel_id=1, source_target_pairs={{0,2},{2,4},{4,6},{6,8},{8,10},{10,12},{12,14},{14,16},{16,18},{18... | collective-permute-start | bytes 6291464 | tf_op jit(solution)/shard_map/ppermute | solution.py:18
  276.9 44.0 %collective-permute-start.11 = (bf16[256,4096]{1,0:T(8,128)(2,1)}, bf16[256,4096]{1,0:T(8,128)(2,1)}, u32[]{:S(2)}, u32[]{:S(2)}) collective-permute-start(bf16[256,4096]{1,0:T(8,128)(2,1)} %advance.14), channel_id=1, source_target_pairs={{0,2},{2,4},{4,6},{6,8},{8,10},{10,12},{12,14},{14,16},{16,18},{18... | collective-permute-start | bytes 6291464 | tf_op jit(solution)/shard_map/ppermute | solution.py:18
  308.6 31.9 %collective-permute-start.36 = (bf16[256,1024]{1,0:T(8,128)(2,1)}, bf16[256,1024]{1,0:T(8,128)(2,1)S(1)}, u32[]{:S(2)}, u32[]{:S(2)}) collective-permute-start(bf16[256,1024]{1,0:T(8,128)(2,1)} %get-tuple-element.70), channel_id=1, source_target_pairs={{0,1},{1,0},{2,3},{3,2},{4,5},{5,4},{6,7},{7,6},{8,9},{9,8},{10,11... | collective-permute-start | bytes 1572872 | tf_op jit(solution)/shard_map/ppermute | solution.py:18
  329.9 22.7 %collective-permute-start.12 = (bf16[256,1024]{1,0:T(8,128)(2,1)}, bf16[256,1024]{1,0:T(8,128)(2,1)S(1)}, u32[]{:S(2)}, u32[]{:S(2)}) collective-permute-start(bf16[256,1024]{1,0:T(8,128)(2,1)} %get-tuple-element.52), channel_id=1, source_target_pairs={{0,1},{1,0},{2,3},{3,2},{4,5},{5,4},{6,7},{7,6},{8,9},{9,8},{10,11... | collective-permute-start | bytes 1572872 | tf_op jit(solution)/shard_map/ppermute | solution.py:18
  331.5 9.0 %collective-permute-start.37 = (f32[1,256]{1,0:T(1,128)S(1)}, f32[1,256]{1,0:T(1,128)S(1)}, u32[]{:S(2)}, u32[]{:S(2)}) collective-permute-start(f32[1,256]{1,0:T(1,128)S(1)} %copy-done.31), channel_id=1, source_target_pairs={{0,1},{1,0},{2,3},{3,2},{4,5},{5,4},{6,7},{7,6},{8,9},{9,8},{10,11... | collective-permute-start | bytes 3080 | tf_op jit(solution)/shard_map/ppermute | solution.py:18
  332.0 20.6 %collective-permute-start.13 = (f32[1,256]{1,0:T(1,128)}, f32[1,256]{1,0:T(1,128)S(1)}, u32[]{:S(2)}, u32[]{:S(2)}) collective-permute-start(f32[1,256]{1,0:T(1,128)} %get-tuple-element.51.square_ref), channel_id=1, source_target_pairs={{0,1},{1,0},{2,3},{3,2},{4,5},{5,4},{6,7},{7,6},{8,9},{9,8},{10,11... | collective-permute-start | bytes 3080 | tf_op jit(solution)/shard_map/ppermute | solution.py:18
  351.1 12.6 %collective-permute-start.38 = (bf16[256,256]{1,0:T(8,128)(2,1)}, bf16[256,256]{1,0:T(8,128)(2,1)S(1)}, u32[]{:S(2)}, u32[]{:S(2)}) collective-permute-start(bf16[256,256]{1,0:T(8,128)(2,1)} %core.21.rest_0_), channel_id=1, source_target_pairs={{0,1},{1,0},{2,3},{3,2},{4,5},{5,4},{6,7},{7,6},{8,9},{9,8},{10,11... | collective-permute-start | bytes 393224 | tf_op jit(solution)/shard_map/ppermute | solution.py:18
  363.1 7.5 %collective-permute-start.14 = (bf16[256,256]{1,0:T(8,128)(2,1)}, bf16[256,256]{1,0:T(8,128)(2,1)S(1)}, u32[]{:S(2)}, u32[]{:S(2)}) collective-permute-start(bf16[256,256]{1,0:T(8,128)(2,1)} %core.15.rest_0_), channel_id=1, source_target_pairs={{0,1},{1,0},{2,3},{3,2},{4,5},{5,4},{6,7},{7,6},{8,9},{9,8},{10,11... | collective-permute-start | bytes 393224 | tf_op jit(solution)/shard_map/ppermute | solution.py:18
  370.6 28.4 %collective-permute-start.39 = (bf16[256,4096]{1,0:T(8,128)(2,1)}, bf16[256,4096]{1,0:T(8,128)(2,1)S(1)}, u32[]{:S(2)}, u32[]{:S(2)}) collective-permute-start(bf16[256,4096]{1,0:T(8,128)(2,1)} %advance.21), channel_id=1, source_target_pairs={{0,2},{2,4},{4,6},{6,8},{8,10},{10,12},{12,14},{14,16},{16,18},{18... | collective-permute-start | bytes 6291464 | tf_op jit(solution)/shard_map/ppermute | solution.py:18
  377.6 44.0 %collective-permute-start.15 = (bf16[256,4096]{1,0:T(8,128)(2,1)}, bf16[256,4096]{1,0:T(8,128)(2,1)}, u32[]{:S(2)}, u32[]{:S(2)}) collective-permute-start(bf16[256,4096]{1,0:T(8,128)(2,1)} %advance.15), channel_id=1, source_target_pairs={{0,2},{2,4},{4,6},{6,8},{8,10},{10,12},{12,14},{14,16},{16,18},{18... | collective-permute-start | bytes 6291464 | tf_op jit(solution)/shard_map/ppermute | solution.py:18
  409.3 31.9 %collective-permute-start.40 = (bf16[256,1024]{1,0:T(8,128)(2,1)}, bf16[256,1024]{1,0:T(8,128)(2,1)S(1)}, u32[]{:S(2)}, u32[]{:S(2)}) collective-permute-start(bf16[256,1024]{1,0:T(8,128)(2,1)} %get-tuple-element.73), channel_id=1, source_target_pairs={{0,1},{1,0},{2,3},{3,2},{4,5},{5,4},{6,7},{7,6},{8,9},{9,8},{10,11... | collective-permute-start | bytes 1572872 | tf_op jit(solution)/shard_map/ppermute | solution.py:18
  430.6 22.8 %collective-permute-start.16 = (bf16[256,1024]{1,0:T(8,128)(2,1)}, bf16[256,1024]{1,0:T(8,128)(2,1)S(1)}, u32[]{:S(2)}, u32[]{:S(2)}) collective-permute-start(bf16[256,1024]{1,0:T(8,128)(2,1)} %get-tuple-element.55), channel_id=1, source_target_pairs={{0,1},{1,0},{2,3},{3,2},{4,5},{5,4},{6,7},{7,6},{8,9},{9,8},{10,11... | collective-permute-start | bytes 1572872 | tf_op jit(solution)/shard_map/ppermute | solution.py:18
  432.2 9.1 %collective-permute-start.41 = (f32[1,256]{1,0:T(1,128)S(1)}, f32[1,256]{1,0:T(1,128)S(1)}, u32[]{:S(2)}, u32[]{:S(2)}) collective-permute-start(f32[1,256]{1,0:T(1,128)S(1)} %copy-done.32), channel_id=1, source_target_pairs={{0,1},{1,0},{2,3},{3,2},{4,5},{5,4},{6,7},{7,6},{8,9},{9,8},{10,11... | collective-permute-start | bytes 3080 | tf_op jit(solution)/shard_map/ppermute | solution.py:18
  432.7 20.7 %collective-permute-start.17 = (f32[1,256]{1,0:T(1,128)}, f32[1,256]{1,0:T(1,128)S(1)}, u32[]{:S(2)}, u32[]{:S(2)}) collective-permute-start(f32[1,256]{1,0:T(1,128)} %get-tuple-element.54.square_ref), channel_id=1, source_target_pairs={{0,1},{1,0},{2,3},{3,2},{4,5},{5,4},{6,7},{7,6},{8,9},{9,8},{10,11... | collective-permute-start | bytes 3080 | tf_op jit(solution)/shard_map/ppermute | solution.py:18
  451.8 12.6 %collective-permute-start.42 = (bf16[256,256]{1,0:T(8,128)(2,1)}, bf16[256,256]{1,0:T(8,128)(2,1)S(1)}, u32[]{:S(2)}, u32[]{:S(2)}) collective-permute-start(bf16[256,256]{1,0:T(8,128)(2,1)} %core.22.rest_0_), channel_id=1, source_target_pairs={{0,1},{1,0},{2,3},{3,2},{4,5},{5,4},{6,7},{7,6},{8,9},{9,8},{10,11... | collective-permute-start | bytes 393224 | tf_op jit(solution)/shard_map/ppermute | solution.py:18
  463.9 7.5 %collective-permute-start.18 = (bf16[256,256]{1,0:T(8,128)(2,1)}, bf16[256,256]{1,0:T(8,128)(2,1)S(1)}, u32[]{:S(2)}, u32[]{:S(2)}) collective-permute-start(bf16[256,256]{1,0:T(8,128)(2,1)} %core.16.rest_0_), channel_id=1, source_target_pairs={{0,1},{1,0},{2,3},{3,2},{4,5},{5,4},{6,7},{7,6},{8,9},{9,8},{10,11... | collective-permute-start | bytes 393224 | tf_op jit(solution)/shard_map/ppermute | solution.py:18
  471.4 28.5 %collective-permute-start.43 = (bf16[256,4096]{1,0:T(8,128)(2,1)}, bf16[256,4096]{1,0:T(8,128)(2,1)}, u32[]{:S(2)}, u32[]{:S(2)}) collective-permute-start(bf16[256,4096]{1,0:T(8,128)(2,1)} %advance.22), channel_id=1, source_target_pairs={{0,2},{2,4},{4,6},{6,8},{8,10},{10,12},{12,14},{14,16},{16,18},{18... | collective-permute-start | bytes 6291464 | tf_op jit(solution)/shard_map/ppermute | solution.py:18
  478.3 43.9 %collective-permute-start.19 = (bf16[256,4096]{1,0:T(8,128)(2,1)}, bf16[256,4096]{1,0:T(8,128)(2,1)S(1)}, u32[]{:S(2)}, u32[]{:S(2)}) collective-permute-start(bf16[256,4096]{1,0:T(8,128)(2,1)} %advance.16), channel_id=1, source_target_pairs={{0,2},{2,4},{4,6},{6,8},{8,10},{10,12},{12,14},{14,16},{16,18},{18... | collective-permute-start | bytes 6291464 | tf_op jit(solution)/shard_map/ppermute | solution.py:18
  508.8 34.4 %collective-permute-start.44 = (bf16[256,1024]{1,0:T(8,128)(2,1)}, bf16[256,1024]{1,0:T(8,128)(2,1)S(1)}, u32[]{:S(2)}, u32[]{:S(2)}) collective-permute-start(bf16[256,1024]{1,0:T(8,128)(2,1)} %get-tuple-element.76), channel_id=1, source_target_pairs={{0,1},{1,0},{2,3},{3,2},{4,5},{5,4},{6,7},{7,6},{8,9},{9,8},{10,11... | collective-permute-start | bytes 1572872 | tf_op jit(solution)/shard_map/ppermute | solution.py:18
  532.5 22.8 %collective-permute-start.20 = (bf16[256,1024]{1,0:T(8,128)(2,1)}, bf16[256,1024]{1,0:T(8,128)(2,1)S(1)}, u32[]{:S(2)}, u32[]{:S(2)}) collective-permute-start(bf16[256,1024]{1,0:T(8,128)(2,1)} %get-tuple-element.58), channel_id=1, source_target_pairs={{0,1},{1,0},{2,3},{3,2},{4,5},{5,4},{6,7},{7,6},{8,9},{9,8},{10,11... | collective-permute-start | bytes 1572872 | tf_op jit(solution)/shard_map/ppermute | solution.py:18
  534.0 9.1 %collective-permute-start.45 = (f32[1,256]{1,0:T(1,128)S(1)}, f32[1,256]{1,0:T(1,128)S(1)}, u32[]{:S(2)}, u32[]{:S(2)}) collective-permute-start(f32[1,256]{1,0:T(1,128)S(1)} %copy-done.33), channel_id=1, source_target_pairs={{0,1},{1,0},{2,3},{3,2},{4,5},{5,4},{6,7},{7,6},{8,9},{9,8},{10,11... | collective-permute-start | bytes 3080 | tf_op jit(solution)/shard_map/ppermute | solution.py:18
  534.5 20.7 %collective-permute-start.21 = (f32[1,256]{1,0:T(1,128)}, f32[1,256]{1,0:T(1,128)S(1)}, u32[]{:S(2)}, u32[]{:S(2)}) collective-permute-start(f32[1,256]{1,0:T(1,128)} %get-tuple-element.57.square_ref), channel_id=1, source_target_pairs={{0,1},{1,0},{2,3},{3,2},{4,5},{5,4},{6,7},{7,6},{8,9},{9,8},{10,11... | collective-permute-start | bytes 3080 | tf_op jit(solution)/shard_map/ppermute | solution.py:18
  553.7 12.6 %collective-permute-start.46 = (bf16[256,256]{1,0:T(8,128)(2,1)}, bf16[256,256]{1,0:T(8,128)(2,1)S(1)}, u32[]{:S(2)}, u32[]{:S(2)}) collective-permute-start(bf16[256,256]{1,0:T(8,128)(2,1)} %core.23.rest_0_), channel_id=1, source_target_pairs={{0,1},{1,0},{2,3},{3,2},{4,5},{5,4},{6,7},{7,6},{8,9},{9,8},{10,11... | collective-permute-start | bytes 393224 | tf_op jit(solution)/shard_map/ppermute | solution.py:18
  565.7 7.5 %collective-permute-start.22 = (bf16[256,256]{1,0:T(8,128)(2,1)}, bf16[256,256]{1,0:T(8,128)(2,1)S(1)}, u32[]{:S(2)}, u32[]{:S(2)}) collective-permute-start(bf16[256,256]{1,0:T(8,128)(2,1)} %core.17.rest_0_), channel_id=1, source_target_pairs={{0,1},{1,0},{2,3},{3,2},{4,5},{5,4},{6,7},{7,6},{8,9},{9,8},{10,11... | collective-permute-start | bytes 393224 | tf_op jit(solution)/shard_map/ppermute | solution.py:18
  573.2 28.4 %collective-permute-start.47 = (bf16[256,4096]{1,0:T(8,128)(2,1)}, bf16[256,4096]{1,0:T(8,128)(2,1)S(1)}, u32[]{:S(2)}, u32[]{:S(2)}) collective-permute-start(bf16[256,4096]{1,0:T(8,128)(2,1)} %advance.23), channel_id=1, source_target_pairs={{0,2},{2,4},{4,6},{6,8},{8,10},{10,12},{12,14},{14,16},{16,18},{18... | collective-permute-start | bytes 6291464 | tf_op jit(solution)/shard_map/ppermute | solution.py:18
  580.2 43.8 %collective-permute-start.23 = (bf16[256,4096]{1,0:T(8,128)(2,1)}, bf16[256,4096]{1,0:T(8,128)(2,1)S(1)}, u32[]{:S(2)}, u32[]{:S(2)}) collective-permute-start(bf16[256,4096]{1,0:T(8,128)(2,1)} %advance.17), channel_id=1, source_target_pairs={{0,2},{2,4},{4,6},{6,8},{8,10},{10,12},{12,14},{14,16},{16,18},{18... | collective-permute-start | bytes 6291464 | tf_op jit(solution)/shard_map/ppermute | solution.py:18
  (47 other events, 163.0 us)

commit v2 on v0

v2 whole, which is shorter than its diff:
```python
import functools

import jax
import jax.numpy as jnp
from jax import lax
from jax.experimental import pallas as pl
from jax.experimental.pallas import tpu as pltpu
from jax.sharding import PartitionSpec as P


TICKS = 6
CHUNKS = 4
LEAD = 2
PIECES = 4
EPSILON = 1e-05
LANES = 128

IN_VMEM = pl.BlockSpec(memory_space=pltpu.VMEM)
IN_HBM = pl.BlockSpec(memory_space=pltpu.HBM)
IN_SMEM = pl.BlockSpec(memory_space=pltpu.SMEM)
ANYWHERE = pl.BlockSpec(memory_space=pl.ANY)


def from_behind(value, axis, steps):
    count = lax.axis_size(axis)
    pairs = [(source, (source + steps) % count) for source in range(count)]
    return lax.ppermute(value, axis, pairs)


def largest_divisor(extent, limit):
    size = min(extent, limit)
    while extent % size:
        size -= 1
    return size


def params():
    return pltpu.CompilerParams(vmem_limit_bytes=10 << 20)


def fetch_copies(sources, targets, semaphores, places):
    copies = []
    for at, (source, target, place) in enumerate(zip(sources, targets, places)):
        extent = target.shape[0] // PIECES
        for piece in range(PIECES):
            copies.append(
                pltpu.make_async_copy(
                    source.at[(*place[:-1], pl.ds(place[-1] + piece * extent, extent))],
                    target.at[pl.ds(piece * extent, extent)],
                    semaphores.at[at, piece],
                )
            )
    return copies


def fetch_body(count, tick, first, table_ref, stream_ref, *refs):
    sources, h_ref, targets, semaphores = refs[:count], refs[count], refs[count + 1 : -1], refs[-1]
    lap = table_ref[tick]
    copies = fetch_copies(
        (stream_ref, *sources), (h_ref, *targets), semaphores, [(0, first)] + [(lap, 0, 0)] * count
    )
    for copy in copies:
        copy.start()
    for copy in copies:
        copy.wait()


def fetch(table, tick, stream, first, rows, stacked):
    count = len(stacked)
    features = stream.shape[2]
    return pl.pallas_call(
        functools.partial(fetch_body, count, tick, first),
        in_specs=[IN_SMEM] + [IN_HBM] * (1 + count),
        out_specs=[IN_VMEM] * (1 + count),
        out_shape=[pltpu.VMEM((rows, features), stream.dtype)]
        + [pltpu.VMEM(value.shape[2:], value.dtype) for value in stacked],
        scratch_shapes=[pltpu.SemaphoreType.DMA((1 + count, PIECES))],
        compiler_params=params(),
        cost_estimate=pl.CostEstimate(
            flops=0, transcendentals=0, bytes_accessed=sum(value.size * value.dtype.itemsize for value in stacked)
        ),
        name="fetch",
    )(table, stream, *stacked)


def refresh_body(count, tick, table_ref, *refs):
    sources = refs[:count]
    targets, semaphores = refs[-1 - count : -1], refs[-1]

    @pl.when(table_ref[tick] != table_ref[tick - 1])
    def _():
        copies = fetch_copies(sources, targets, semaphores, [(table_ref[tick], 0, 0)] * count)
        for copy in copies:
            copy.start()
        for copy in copies:
            copy.wait()


def refresh(table, tick, stacked, resident, after):
    count = len(stacked)
    return pl.pallas_call(
        functools.partial(refresh_body, count, tick),
        in_specs=[IN_SMEM] + [IN_HBM] * count + [IN_VMEM] * count + [ANYWHERE] * len(after),
        out_specs=[IN_VMEM] * count,
        out_shape=[pltpu.VMEM(value.shape, value.dtype) for value in resident],
        input_output_aliases={1 + count + at: at for at in range(count)},
        scratch_shapes=[pltpu.SemaphoreType.DMA((count, PIECES))],
        compiler_params=params(),
        cost_estimate=pl.CostEstimate(flops=0, transcendentals=0, bytes_accessed=0),
        name="refresh",
    )(table, *stacked, *resident, *after)


def project_body(h_ref, down_ref, router_ref, *rest):
    own_ref, square_ref, sent_ref = rest[-3:]
    rows, features = h_ref.shape
    partial = jnp.zeros((rows, LANES), jnp.float32)
    for at in range(0, features, LANES):
        wide = h_ref[:, at : at + LANES].astype(jnp.float32)
        partial = partial + wide * wide
    square = jnp.broadcast_to(jnp.sum(partial, axis=1, keepdims=True), (rows, LANES))
    square_ref[...] = square
    upper = square.astype(jnp.bfloat16)
    lower = (square - upper.astype(jnp.float32)).astype(jnp.bfloat16)
    lane = lax.broadcasted_iota(jnp.int32, (rows, LANES), 1)
    start = 0
    for weight_ref in (down_ref, router_ref):
        extent = weight_ref.shape[1]
        block = largest_divisor(extent, 256)
        for at in range(0, extent, block):
            value = jnp.dot(
                h_ref[...].astype(jnp.bfloat16), weight_ref[:, at : at + block], preferred_element_type=jnp.float32
            )
            own_ref[:, start + at : start + at + block] = value
            sent_ref[:, start + at : start + at + block] = value.astype(jnp.bfloat16)
        start += extent
    sent_ref[:, start:] = jnp.where(
        lane < LANES // 2, upper.astype(jnp.float32), lower.astype(jnp.float32)
    ).astype(jnp.bfloat16)


def project(h, down, router, after):
    rows, features = h.shape
    total = down.shape[1] + router.shape[1]
    return pl.pallas_call(
        project_body,
        in_specs=[IN_VMEM] * 3 + [ANYWHERE] * len(after),
        out_specs=[IN_VMEM] * 3,
        out_shape=[
            jax.ShapeDtypeStruct((rows, total), jnp.float32),
            jax.ShapeDtypeStruct((rows, LANES), jnp.float32),
            jax.ShapeDtypeStruct((rows, total + LANES), jnp.bfloat16),
        ],
        compiler_params=params(),
        cost_estimate=pl.CostEstimate(
            flops=2 * rows * features * total, bytes_accessed=6 * rows * total, transcendentals=0
        ),
        name="project",
    )(h, down, router, *after)


def core_body(others, width, tick, table_ref, own_ref, square_ref, *rest):
    sent_refs = rest[:others]
    expert_ref, core_ref = rest[others : others + 2]
    out_ref, reduced_ref, mixing_ref, ranked_ref = rest[-4:]
    d_rank, rows = reduced_ref.shape
    experts = expert_ref.shape[2]
    lap = table_ref[tick]
    square = square_ref[...]
    tail = d_rank + experts
    for other in sent_refs:
        pair = other[:, tail:].astype(jnp.float32)
        square = square + pair[:, :1] + pair[:, LANES // 2 : LANES // 2 + 1]
    factor = lax.rsqrt(square / width + EPSILON)

    def total(at):
        value = own_ref[:, at : at + LANES]
        for other in sent_refs:
            value = value + other[:, at : at + LANES].astype(jnp.float32)
        return value

    for at in range(0, d_rank, LANES):
        reduced_ref[at : at + LANES, :] = (total(at) * factor).astype(jnp.bfloat16).T
    mixing = jnp.zeros(mixing_ref.shape, jnp.float32)
    for at in range(0, experts, LANES):
        gating = jax.nn.sigmoid(total(d_rank + at) * factor).astype(jnp.bfloat16)
        mixing = mixing + lax.dot_general(
            expert_ref[lap, :, at : at + LANES],
            gating,
            (((1,), (1,)), ((), ())),
            preferred_element_type=jnp.float32,
        )
    mixing_ref[...] = mixing.astype(jnp.bfloat16).astype(jnp.float32)

    f_rank, ranks, depth = core_ref.shape
    group = largest_divisor(f_rank, 32)
    for at in range(0, f_rank, group):
        part = core_ref[at : at + group].reshape(group * ranks, depth)
        value = jnp.dot(part, reduced_ref[...], preferred_element_type=jnp.float32)
        value = value.reshape(group, ranks, rows) * mixing_ref[...][None]
        ranked_ref[at : at + group, :] = jnp.sum(value, axis=1)
    out_ref[...] = ranked_ref[...].T.astype(jnp.bfloat16)


def core(table, tick, own, square, sent, expert, core_tensor, width, after):
    rows = own.shape[0]
    f_rank, ranks, d_rank = core_tensor.shape
    others = len(sent)
    return pl.pallas_call(
        functools.partial(core_body, others, width, tick),
        in_specs=[IN_SMEM] + [IN_VMEM] * (4 + others) + [ANYWHERE] * len(after),
        out_specs=IN_VMEM,
        out_shape=jax.ShapeDtypeStruct((rows, f_rank), jnp.bfloat16),
        scratch_shapes=[
            pltpu.VMEM((d_rank, rows), jnp.bfloat16),
            pltpu.VMEM((ranks, rows), jnp.float32),
            pltpu.VMEM((f_rank, rows), jnp.float32),
        ],
        compiler_params=params(),
        cost_estimate=pl.CostEstimate(
            flops=2 * rows * f_rank * ranks * d_rank, bytes_accessed=6 * rows * d_rank, transcendentals=rows * d_rank
        ),
        name="core",
    )(table, own, square, *sent, expert, core_tensor, *after)


def advance_body(pieces, table_ref, h_ref, *rest):
    ranked, up_ref, out_ref = rest[:pieces], rest[pieces], rest[-1]
    features = h_ref.shape[1]
    extent = ranked[0].shape[1]
    block = largest_divisor(features, 512)
    for at in range(0, features, block):
        value = h_ref[:, at : at + block].astype(jnp.float32)
        for shift, piece in enumerate(ranked):
            row = pl.multiple_of(lax.rem(table_ref[TICKS] + pieces - shift, pieces) * extent, extent)
            value = value + jnp.dot(
                piece[...], up_ref[pl.ds(row, extent), at : at + block], preferred_element_type=jnp.float32
            )
        out_ref[:, at : at + block] = value.astype(jnp.bfloat16)


def advance(table, h, ranked, up, after):
    pieces = len(ranked)
    rows, features = h.shape
    return pl.pallas_call(
        functools.partial(advance_body, pieces),
        in_specs=[IN_SMEM] + [IN_VMEM] * (2 + pieces) + [ANYWHERE] * len(after),
        out_specs=IN_VMEM,
        out_shape=jax.ShapeDtypeStruct((rows, features), jnp.bfloat16),
        compiler_params=params(),
        cost_estimate=pl.CostEstimate(
            flops=2 * rows * up.shape[0] * features, bytes_accessed=4 * rows * features, transcendentals=0
        ),
        name="advance",
    )(table, h, *ranked, up, *after)


def store_body(first, *refs):
    h_ref, (out_ref, wide_ref, semaphores) = refs[0], refs[-3:]
    rows = h_ref.shape[0]
    extent = rows // PIECES
    copies = []
    for piece in range(PIECES):
        part = pl.ds(piece * extent, extent)
        wide_ref[part, :] = h_ref[part, :].astype(wide_ref.dtype)
        copy = pltpu.make_async_copy(
            wide_ref.at[part], out_ref.at[0, pl.ds(first + piece * extent, extent)], semaphores.at[piece]
        )
        copy.start()
        copies.append(copy)
    for copy in copies:
        copy.wait()


def store(h, first, shape, dtype, out):
    held = [] if out is None else [out]
    return pl.pallas_call(
        functools.partial(store_body, first),
        in_specs=[IN_VMEM] + [ANYWHERE] * len(held),
        out_specs=ANYWHERE,
        out_shape=jax.ShapeDtypeStruct(shape, dtype),
        input_output_aliases={1: 0} if held else {},
        scratch_shapes=[pltpu.VMEM(h.shape, dtype), pltpu.SemaphoreType.DMA((PIECES,))],
        compiler_params=params(),
        cost_estimate=pl.CostEstimate(flops=0, transcendentals=0, bytes_accessed=6 * h.size),
        name="store",
    )(h, *held)


def per_device(stream, down_factor, router, expert_factor, core_tensor, up_factor):
    section_id = lax.axis_index("section")
    sections = lax.axis_size("section")
    parts = lax.axis_size("tensor")
    front_edge = sections // 2
    ticks = jnp.arange(TICKS + 1, dtype=jnp.int32)
    laps = ((section_id - ticks) % sections < front_edge).astype(jnp.int32) + (section_id < ticks).astype(jnp.int32)
    table = jnp.where(ticks < TICKS, laps, lax.axis_index("tensor"))
    expert = jnp.swapaxes(expert_factor[:, 0], 1, 2)
    width = stream.shape[2] * parts
    rows = stream.shape[1] // CHUNKS
    stream, *stacked = [
        pltpu.with_memory_space_constraint(value, pltpu.HBM)
        for value in (stream, down_factor, router, core_tensor, up_factor)
    ]
    held, resident = [], []
    for chunk in range(CHUNKS):
        share = stacked[:2] if chunk == 0 else stacked[2:] if chunk == 1 else []
        h, *fetched = fetch(table, 0, stream, chunk * rows, rows, share)
        held.append(h)
        resident += fetched
    early, late = resident[:2], resident[2:]

    def exchange(own, square, sent):
        if parts == 2:
            return own, square, [from_behind(sent, "tensor", 1)]
        if parts > 2:
            return lax.psum(own, "tensor"), lax.psum(square, "tensor"), []
        return own, square, []

    def gather(piece):
        if parts > 2:
            return [lax.all_gather(piece, "tensor", axis=1, tiled=True)]
        return [piece] + [from_behind(piece, "tensor", 1)] * (parts - 1)

    steps = TICKS * CHUNKS
    projected = [exchange(*project(held[at], *early, [])) for at in range(LEAD)]
    piece = core(table, 0, *projected[0], expert, late[0], width, [])
    for step in range(steps):
        tick, chunk = divmod(step, CHUNKS)
        order = []
        if step + LEAD < steps:
            ahead_tick, ahead = divmod(step + LEAD, CHUNKS)
            own, square, sent = project(held[ahead], *early, [piece])
            order = [sent]
            if ahead == CHUNKS - 1 and ahead_tick + 1 < TICKS:
                early = refresh(table, ahead_tick + 1, stacked[:2], early, order)
                order = order + [early[0]]
            projected.append(exchange(own, square, sent))
        pieces = gather(piece)
        value = advance(table, held[chunk], pieces, late[1], order)
        held[chunk] = from_behind(value, "section", 1)
        if step + 1 < steps:
            if chunk == CHUNKS - 1:
                late = refresh(table, tick + 1, stacked[2:], late, [value])
            piece = core(
                table, (step + 1) // CHUNKS, *projected[step + 1], expert, late[0], width, [value]
            )
    out = None
    for chunk, h in enumerate(held):
        out = store(h, chunk * rows, stream.shape, stream.dtype, out)
    return out


def solution(mesh):
    return jax.shard_map(
        per_device,
        mesh=mesh,
        in_specs=(
            P("section", None, "tensor"),
            P(None, "section", "tensor", None),
            P(None, "section", "tensor", None),
            P(None, "section", None, None),
            P(None, "section", "tensor", None, None),
            P(None, "section", None, "tensor"),
        ),
        out_specs=P("section", None, "tensor"),
        check_vma=False,
    )
```

time: 1200 us -> 403 us (0.34)
  waiting for transfers between devices: 731 us -> 162 us
  matrix products: 242 us -> 0 us
  Pallas kernels: 0 us -> 166 us
  blocking collectives: 125 us -> 0 us
  starting transfers between devices: 2.49 us -> 66.1 us
  local copies, waits for them, and re-layouts: 61.4 us -> 0.01 us
  other arithmetic: 19.4 us -> 0.01 us
  between operations: 14.5 us -> 0.97 us
    ppermute x6 -> x72, waiting for transfers between devices: 573 us -> 162 us  [from_behind(): return lax.ppermute(value, axis, pairs)]
    dot_general x30 -> x0, matrix products: 242 us -> none  [the longest x6 107 us: core_rows(): lax.dot_general(reduced, flattened, (((1,), (1,)), ((), ())), preferred_e...]
    pallas_call x0 -> x90, Pallas kernels: none -> 166 us  [the longest x24 76.8 us: core(): pl.pallas_call(functools.partial(core_body, others, width, tick), in_spec...]
    reduce_scatter x12 -> x0, waiting for transfers between devices: 157 us -> none  [the longest x6 84.2 us: per_device(): lax.psum_scatter(projected, 'tensor', scatter_dimension=0, tiled=True)]
    all_gather x18 -> x0, blocking collectives: 125 us -> none  [the longest x12 79.1 us: per_device(): pieces = lax.all_gather((reduced, mixing), 'tensor', axis=0, tiled=True)]
    ppermute x6 -> x72, starting transfers between devices: 0.35 us -> 66.1 us  [from_behind(): return lax.ppermute(value, axis, pairs)]
    dynamic_slice x1 -> x0, local copies, waits for them, and re-layouts: 36.3 us -> none  [select_lap(): return lax.dynamic_index_in_dim(stacked[:, 0], lap_id, 0, keepdims=False)]
    unnamed x45 -> x2, local copies, waits for them, and re-layouts: 25.1 us -> 0.01 us
  transfers between devices with their start and end apart: 24 -> 72, of which waited for: 16 -> 38; matrix products, arithmetic and copies ran while one was open for 12% -> 0% of each run, Pallas kernels for 0% -> 39%
where the time goes in v2:
time: 403 us; the launch traced here: 396 us
  Pallas kernels  166 us (41%)
  waiting for transfers between devices  162 us (40%)
  starting transfers between devices  66.1 us (16%)
    ppermute x72, waiting for transfers between devices, from_behind(): return lax.ppermute(value, axis, pairs)  162 us
    pallas_call x24, Pallas kernels, core(): pl.pallas_call(functools.partial(core_body, others, width, tick), in_spec...  76.8 us
    ppermute x72, starting transfers between devices, from_behind(): return lax.ppermute(value, axis, pairs)  66.1 us
    pallas_call x24, Pallas kernels, project(): pl.pallas_call(project_body, in_specs=[IN_VMEM] * 3 + [ANYWHERE] * len(af...  32.4 us
    pallas_call x24, Pallas kernels, advance(): pl.pallas_call(functools.partial(advance_body, pieces), in_specs=[IN_SMEM...  30.5 us
    pallas_call x4, Pallas kernels, fetch(): pl.pallas_call(functools.partial(fetch_body, count, tick, first), in_spec...  14.7 us
  transfers between devices with their start and end apart: 72, of which 38 were waited for; matrix products, arithmetic and copies ran while one was open for 0% of the time, Pallas kernels for 39%

profile of v2, /device:TPU:0, one launch (start us, length us, event | category | flops | bytes accessed | tf_op | source)
XLA Modules:
  0.0 395.6 jit_solution(18360242268880054033)
XLA Ops:
  0.0 4.7 %fetch.5 = (f32[128,4096]{1,0:T(8,128)S(1)}, bf16[4096,512]{1,0:T(8,128)(2,1)S(1)}, bf16[4096,512]{1,0:T(8,128)(2,1)S(1)}) custom-call(s32[7]{0:T(128)S(1)} %compare_select_fusion.2.table_ref, f32[1,512,4096]{2,1,0:T(8,128)} %stream_ref.7, bf16[2,1,4096,512]{3,2,1,0:T(8,128)(2,1)} %refs_0_.22, bf16[2,1,4096,512]{3,2,1,0:T(8,128)(2,1)} %refs_1_.22), custom_call_target="tpu_custom_call" | custom-call | bytes 16777216 | tf_op jit(solution)/shard_map/fetch/pallas_call | solution.py:71
  6.0 3.0 collective-permute-start.1
  9.1 5.8 %fetch.6 = (f32[128,4096]{1,0:T(8,128)S(1)}, bf16[256,32,512]{2,1,0:T(8,128)(2,1)S(1)}, bf16[512,4096]{1,0:T(8,128)(2,1)S(1)}) custom-call(s32[7]{0:T(128)S(1)} %compare_select_fusion.2.table_ref, f32[1,512,4096]{2,1,0:T(8,128)} %stream_ref.7, bf16[2,1,256,32,512]{4,3,2,1,0:T(8,128)(2,1)} %refs_0_.23, bf16[2,1,512,4096]{3,2,1,0:T(8,128)(2,1)} %refs_1_.23), custom_call_target="tpu_custom_call" | custom-call | bytes 25165824 | tf_op jit(solution)/shard_map/fetch/pallas_call | solution.py:71
  18.4 3.2 core.24.rest_0_
  29.6 3.2 core.25.rest_0_
  42.0 7.9 %collective-permute-done.4.rest_0_ = bf16[128,1152]{1,0:T(8,128)(2,1)S(1)} collective-permute-done((bf16[128,1152]{1,0:T(8,128)(2,1)S(1)}, bf16[128,1152]{1,0:T(8,128)(2,1)S(1)}, u32[]{:S(2)}, u32[]{:S(2)}) %collective-permute-start.4) | collective-permute-done | bytes 294944 | tf_op jit(solution)/shard_map/ppermute | solution.py:27
  49.9 3.2 core.26.rest_0_
  58.9 3.2 core.27.rest_0_
  71.4 7.2 %collective-permute-done.12.rest_0_ = bf16[128,1152]{1,0:T(8,128)(2,1)S(1)} collective-permute-done((bf16[128,1152]{1,0:T(8,128)(2,1)S(1)}, bf16[128,1152]{1,0:T(8,128)(2,1)S(1)}, u32[]{:S(2)}, u32[]{:S(2)}) %collective-permute-start.12) | collective-permute-done | bytes 294944 | tf_op jit(solution)/shard_map/ppermute | solution.py:27
  78.6 3.2 core.28.rest_0_
  87.7 3.2 core.29.rest_0_
  99.6 7.4 %collective-permute-done.16.rest_0_ = bf16[128,1152]{1,0:T(8,128)(2,1)S(1)} collective-permute-done((bf16[128,1152]{1,0:T(8,128)(2,1)S(1)}, bf16[128,1152]{1,0:T(8,128)(2,1)S(1)}, u32[]{:S(2)}, u32[]{:S(2)}) %collective-permute-start.16) | collective-permute-done | bytes 294944 | tf_op jit(solution)/shard_map/ppermute | solution.py:27
  107.0 3.2 core.30.rest_0_
  116.7 3.2 core.31.rest_0_
  129.3 7.2 %collective-permute-done.24.rest_0_ = bf16[128,1152]{1,0:T(8,128)(2,1)S(1)} collective-permute-done((bf16[128,1152]{1,0:T(8,128)(2,1)S(1)}, bf16[128,1152]{1,0:T(8,128)(2,1)S(1)}, u32[]{:S(2)}, u32[]{:S(2)}) %collective-permute-start.24) | collective-permute-done | bytes 294944 | tf_op jit(solution)/shard_map/ppermute | solution.py:27
  136.5 3.2 core.32.rest_0_
  145.4 3.2 core.33.rest_0_
  154.2 2.8 collective-permute-start.33
  159.1 7.6 %collective-permute-done.28.rest_0_ = bf16[128,1152]{1,0:T(8,128)(2,1)S(1)} collective-permute-done((bf16[128,1152]{1,0:T(8,128)(2,1)S(1)}, bf16[128,1152]{1,0:T(8,128)(2,1)S(1)}, u32[]{:S(2)}, u32[]{:S(2)}) %collective-permute-start.28) | collective-permute-done | bytes 294944 | tf_op jit(solution)/shard_map/ppermute | solution.py:27
  166.7 3.2 core.34.rest_0_
  171.8 2.8 collective-permute-done.30.rest_1_
  176.0 3.2 core.35.rest_0_
  181.0 2.6 collective-permute-done.32.rest_1_
  188.5 7.2 %collective-permute-done.36.rest_0_ = bf16[128,1152]{1,0:T(8,128)(2,1)S(1)} collective-permute-done((bf16[128,1152]{1,0:T(8,128)(2,1)S(1)}, bf16[128,1152]{1,0:T(8,128)(2,1)S(1)}, u32[]{:S(2)}, u32[]{:S(2)}) %collective-permute-start.36) | collective-permute-done | bytes 294944 | tf_op jit(solution)/shard_map/ppermute | solution.py:27
  195.7 3.2 core.36.rest_0_
  204.6 3.2 core.37.rest_0_
  217.9 7.6 %collective-permute-done.40.rest_0_ = bf16[128,1152]{1,0:T(8,128)(2,1)S(1)} collective-permute-done((bf16[128,1152]{1,0:T(8,128)(2,1)S(1)}, bf16[128,1152]{1,0:T(8,128)(2,1)S(1)}, u32[]{:S(2)}, u32[]{:S(2)}) %collective-permute-start.40) | collective-permute-done | bytes 294944 | tf_op jit(solution)/shard_map/ppermute | solution.py:27
  225.6 3.2 core.38.rest_0_
  230.7 2.8 collective-permute-done.42.rest_1_
  234.9 3.2 core.39.rest_0_
  247.5 6.7 %collective-permute-done.48.rest_0_ = bf16[128,1152]{1,0:T(8,128)(2,1)S(1)} collective-permute-done((bf16[128,1152]{1,0:T(8,128)(2,1)S(1)}, bf16[128,1152]{1,0:T(8,128)(2,1)S(1)}, u32[]{:S(2)}, u32[]{:S(2)}) %collective-permute-start.48) | collective-permute-done | bytes 294944 | tf_op jit(solution)/shard_map/ppermute | solution.py:27
  254.2 3.2 core.40.rest_0_
  259.3 3.0 collective-permute-done.49.rest_1_
  263.9 3.2 core.41.rest_0_
  276.1 7.9 %collective-permute-done.52.rest_0_ = bf16[128,1152]{1,0:T(8,128)(2,1)S(1)} collective-permute-done((bf16[128,1152]{1,0:T(8,128)(2,1)S(1)}, bf16[128,1152]{1,0:T(8,128)(2,1)S(1)}, u32[]{:S(2)}, u32[]{:S(2)}) %collective-permute-start.52) | collective-permute-done | bytes 294944 | tf_op jit(solution)/shard_map/ppermute | solution.py:27
  283.9 3.2 core.42.rest_0_
  293.0 3.2 core.43.rest_0_
  298.0 3.0 collective-permute-done.56.rest_1_
  305.5 7.1 %collective-permute-done.60.rest_0_ = bf16[128,1152]{1,0:T(8,128)(2,1)S(1)} collective-permute-done((bf16[128,1152]{1,0:T(8,128)(2,1)S(1)}, bf16[128,1152]{1,0:T(8,128)(2,1)S(1)}, u32[]{:S(2)}, u32[]{:S(2)}) %collective-permute-start.60) | collective-permute-done | bytes 294944 | tf_op jit(solution)/shard_map/ppermute | solution.py:27
  312.6 3.2 core.44.rest_0_
  321.7 3.2 core.45.rest_0_
  330.9 3.2 core.46.rest_0_
  334.2 4.2 %collective-permute-done.66.rest_1_ = bf16[128,256]{1,0:T(8,128)(2,1)S(1)} collective-permute-done((bf16[128,256]{1,0:T(8,128)(2,1)S(1)}, bf16[128,256]{1,0:T(8,128)(2,1)S(1)}, u32[]{:S(2)}, u32[]{:S(2)}) %collective-permute-start.66) | collective-permute-done | bytes 65568 | tf_op jit(solution)/shard_map/ppermute | solution.py:27
  339.8 3.4 core.47.rest_0_
  348.9 11.4 %collective-permute-done.71.refs_0_ = bf16[128,4096]{1,0:T(8,128)(2,1)S(1)} collective-permute-done((bf16[128,4096]{1,0:T(8,128)(2,1)S(1)}, bf16[128,4096]{1,0:T(8,128)(2,1)S(1)}, u32[]{:S(2)}, u32[]{:S(2)}) %collective-permute-start.71) | collective-permute-done | bytes 1048608 | tf_op jit(solution)/shard_map/ppermute | solution.py:27
  361.6 9.8 %collective-permute-done.70.refs_0_ = bf16[128,4096]{1,0:T(8,128)(2,1)S(1)} collective-permute-done((bf16[128,4096]{1,0:T(8,128)(2,1)S(1)}, bf16[128,4096]{1,0:T(8,128)(2,1)S(1)}, u32[]{:S(2)}, u32[]{:S(2)}) %collective-permute-start.70) | collective-permute-done | bytes 1048608 | tf_op jit(solution)/shard_map/ppermute | solution.py:27
  372.9 9.8 %collective-permute-done.69.refs_0_ = bf16[128,4096]{1,0:T(8,128)(2,1)S(1)} collective-permute-done((bf16[128,4096]{1,0:T(8,128)(2,1)S(1)}, bf16[128,4096]{1,0:T(8,128)(2,1)S(1)}, u32[]{:S(2)}, u32[]{:S(2)}) %collective-permute-start.69) | collective-permute-done | bytes 1048608 | tf_op jit(solution)/shard_map/ppermute | solution.py:27
  384.1 9.8 %collective-permute-done.68.refs_0_ = bf16[128,4096]{1,0:T(8,128)(2,1)S(1)} collective-permute-done((bf16[128,4096]{1,0:T(8,128)(2,1)S(1)}, bf16[128,4096]{1,0:T(8,128)(2,1)S(1)}, u32[]{:S(2)}, u32[]{:S(2)}) %collective-permute-start.68) | collective-permute-done | bytes 1048608 | tf_op jit(solution)/shard_map/ppermute | solution.py:27
  (189 shorter events, 168.2 us)
Async XLA Ops:
  6.0 12.4 %collective-permute-start.1 = (bf16[128,1152]{1,0:T(8,128)(2,1)S(1)}, bf16[128,1152]{1,0:T(8,128)(2,1)S(1)}, u32[]{:S(2)}, u32[]{:S(2)}) collective-permute-start(bf16[128,1152]{1,0:T(8,128)(2,1)S(1)} %get-tuple-element.113), channel_id=1, source_target_pairs={{0,1},{1,0},{2,3},{3,2},{4,5},{5,4},{6,7},{7,6},{8,9},{9,8},{10,11... | collective-permute-start | bytes 884744 | tf_op jit(solution)/shard_map/ppermute | solution.py:27
  16.2 13.4 %collective-permute-start = (bf16[128,1152]{1,0:T(8,128)(2,1)S(1)}, bf16[128,1152]{1,0:T(8,128)(2,1)S(1)}, u32[]{:S(2)}, u32[]{:S(2)}) collective-permute-start(bf16[128,1152]{1,0:T(8,128)(2,1)S(1)} %get-tuple-element.108), channel_id=1, source_target_pairs={{0,1},{1,0},{2,3},{3,2},{4,5},{5,4},{6,7},{7,6},{8,9},{9,8},{10,11... | collective-permute-start | bytes 884744 | tf_op jit(solution)/shard_map/ppermute | solution.py:27
  27.4 27.3 %collective-permute-start.7 = (bf16[128,4096]{1,0:T(8,128)(2,1)S(1)}, bf16[128,4096]{1,0:T(8,128)(2,1)S(1)}, u32[]{:S(2)}, u32[]{:S(2)}) collective-permute-start(bf16[128,4096]{1,0:T(8,128)(2,1)S(1)} %advance.24.rest_3_), channel_id=1, source_target_pairs={{0,2},{2,4},{4,6},{6,8},{8,10},{10,12},{12,14},{14,16},{16,18},{18... | collective-permute-start | bytes 3145736 | tf_op jit(solution)/shard_map/ppermute | solution.py:27
  38.4 25.3 %collective-permute-start.9 = (bf16[128,4096]{1,0:T(8,128)(2,1)S(1)}, bf16[128,4096]{1,0:T(8,128)(2,1)S(1)}, u32[]{:S(2)}, u32[]{:S(2)}) collective-permute-start(bf16[128,4096]{1,0:T(8,128)(2,1)S(1)} %advance.25.rest_3_), channel_id=1, source_target_pairs={{0,2},{2,4},{4,6},{6,8},{8,10},{10,12},{12,14},{14,16},{16,18},{18... | collective-permute-start | bytes 3145736 | tf_op jit(solution)/shard_map/ppermute | solution.py:27
  40.0 9.9 %collective-permute-start.4 = (bf16[128,1152]{1,0:T(8,128)(2,1)S(1)}, bf16[128,1152]{1,0:T(8,128)(2,1)S(1)}, u32[]{:S(2)}, u32[]{:S(2)}) collective-permute-start(bf16[128,1152]{1,0:T(8,128)(2,1)S(1)} %get-tuple-element.115.rest_3_), channel_id=1, source_target_pairs={{0,1},{1,0},{2,3},{3,2},{4,5},{5,4},{6,7},{7,6},{8,9},{9,8},{10,11... | collective-permute-start | bytes 884744 | tf_op jit(solution)/shard_map/ppermute | solution.py:27
  41.6 17.3 %collective-permute-start.3 = (bf16[128,1152]{1,0:T(8,128)(2,1)S(1)}, bf16[128,1152]{1,0:T(8,128)(2,1)S(1)}, u32[]{:S(2)}, u32[]{:S(2)}) collective-permute-start(bf16[128,1152]{1,0:T(8,128)(2,1)S(1)} %get-tuple-element.118.refs_4_.rest_3_), channel_id=1, source_target_pairs={{0,1},{1,0},{2,3},{3,2},{4,5},{5,4},{6,7},{7,6},{8,9},{9,8},{10,11... | collective-permute-start | bytes 884744 | tf_op jit(solution)/shard_map/ppermute | solution.py:27
  58.8 24.6 %collective-permute-start.14 = (bf16[128,4096]{1,0:T(8,128)(2,1)S(1)}, bf16[128,4096]{1,0:T(8,128)(2,1)S(1)}, u32[]{:S(2)}, u32[]{:S(2)}) collective-permute-start(bf16[128,4096]{1,0:T(8,128)(2,1)S(1)} %advance.26.rest_3_), channel_id=1, source_target_pairs={{0,2},{2,4},{4,6},{6,8},{8,10},{10,12},{12,14},{14,16},{16,18},{18... | collective-permute-start | bytes 3145736 | tf_op jit(solution)/shard_map/ppermute | solution.py:27
  67.7 24.8 %collective-permute-start.10 = (bf16[128,4096]{1,0:T(8,128)(2,1)S(1)}, bf16[128,4096]{1,0:T(8,128)(2,1)S(1)}, u32[]{:S(2)}, u32[]{:S(2)}) collective-permute-start(bf16[128,4096]{1,0:T(8,128)(2,1)S(1)} %advance.27.refs_4_.rest_3_), channel_id=1, source_target_pairs={{0,2},{2,4},{4,6},{6,8},{8,10},{10,12},{12,14},{14,16},{16,18},{18... | collective-permute-start | bytes 3145736 | tf_op jit(solution)/shard_map/ppermute | solution.py:27
  68.8 9.9 %collective-permute-start.12 = (bf16[128,1152]{1,0:T(8,128)(2,1)S(1)}, bf16[128,1152]{1,0:T(8,128)(2,1)S(1)}, u32[]{:S(2)}, u32[]{:S(2)}) collective-permute-start(bf16[128,1152]{1,0:T(8,128)(2,1)S(1)} %get-tuple-element.123.rest_3_), channel_id=1, source_target_pairs={{0,1},{1,0},{2,3},{3,2},{4,5},{5,4},{6,7},{7,6},{8,9},{9,8},{10,11... | collective-permute-start | bytes 884744 | tf_op jit(solution)/shard_map/ppermute | solution.py:27
  70.3 17.4 %collective-permute-start.11 = (bf16[128,1152]{1,0:T(8,128)(2,1)S(1)}, bf16[128,1152]{1,0:T(8,128)(2,1)S(1)}, u32[]{:S(2)}, u32[]{:S(2)}) collective-permute-start(bf16[128,1152]{1,0:T(8,128)(2,1)S(1)} %get-tuple-element.124.rest_3_), channel_id=1, source_target_pairs={{0,1},{1,0},{2,3},{3,2},{4,5},{5,4},{6,7},{7,6},{8,9},{9,8},{10,11... | collective-permute-start | bytes 884744 | tf_op jit(solution)/shard_map/ppermute | solution.py:27
  87.6 24.4 %collective-permute-start.19 = (bf16[128,4096]{1,0:T(8,128)(2,1)S(1)}, bf16[128,4096]{1,0:T(8,128)(2,1)S(1)}, u32[]{:S(2)}, u32[]{:S(2)}) collective-permute-start(bf16[128,4096]{1,0:T(8,128)(2,1)S(1)} %advance.28.rest_3_), channel_id=1, source_target_pairs={{0,2},{2,4},{4,6},{6,8},{8,10},{10,12},{12,14},{14,16},{16,18},{18... | collective-permute-start | bytes 3145736 | tf_op jit(solution)/shard_map/ppermute | solution.py:27
  96.5 24.8 %collective-permute-start.21 = (bf16[128,4096]{1,0:T(8,128)(2,1)S(1)}, bf16[128,4096]{1,0:T(8,128)(2,1)S(1)}, u32[]{:S(2)}, u32[]{:S(2)}) collective-permute-start(bf16[128,4096]{1,0:T(8,128)(2,1)S(1)} %advance.29.rest_3_), channel_id=1, source_target_pairs={{0,2},{2,4},{4,6},{6,8},{8,10},{10,12},{12,14},{14,16},{16,18},{18... | collective-permute-start | bytes 3145736 | tf_op jit(solution)/shard_map/ppermute | solution.py:27
  97.6 9.4 %collective-permute-start.16 = (bf16[128,1152]{1,0:T(8,128)(2,1)S(1)}, bf16[128,1152]{1,0:T(8,128)(2,1)S(1)}, u32[]{:S(2)}, u32[]{:S(2)}) collective-permute-start(bf16[128,1152]{1,0:T(8,128)(2,1)S(1)} %get-tuple-element.131.rest_3_), channel_id=1, source_target_pairs={{0,1},{1,0},{2,3},{3,2},{4,5},{5,4},{6,7},{7,6},{8,9},{9,8},{10,11... | collective-permute-start | bytes 884744 | tf_op jit(solution)/shard_map/ppermute | solution.py:27
  99.1 17.6 %collective-permute-start.15 = (bf16[128,1152]{1,0:T(8,128)(2,1)S(1)}, bf16[128,1152]{1,0:T(8,128)(2,1)S(1)}, u32[]{:S(2)}, u32[]{:S(2)}) collective-permute-start(bf16[128,1152]{1,0:T(8,128)(2,1)S(1)} %get-tuple-element.134.refs_4_.rest_3_), channel_id=1, source_target_pairs={{0,1},{1,0},{2,3},{3,2},{4,5},{5,4},{6,7},{7,6},{8,9},{9,8},{10,11... | collective-permute-start | bytes 884744 | tf_op jit(solution)/shard_map/ppermute | solution.py:27
  116.5 24.7 %collective-permute-start.26 = (bf16[128,4096]{1,0:T(8,128)(2,1)S(1)}, bf16[128,4096]{1,0:T(8,128)(2,1)S(1)}, u32[]{:S(2)}, u32[]{:S(2)}) collective-permute-start(bf16[128,4096]{1,0:T(8,128)(2,1)S(1)} %advance.30.rest_3_), channel_id=1, source_target_pairs={{0,2},{2,4},{4,6},{6,8},{8,10},{10,12},{12,14},{14,16},{16,18},{18... | collective-permute-start | bytes 3145736 | tf_op jit(solution)/shard_map/ppermute | solution.py:27
  125.8 24.2 %collective-permute-start.22 = (bf16[128,4096]{1,0:T(8,128)(2,1)S(1)}, bf16[128,4096]{1,0:T(8,128)(2,1)S(1)}, u32[]{:S(2)}, u32[]{:S(2)}) collective-permute-start(bf16[128,4096]{1,0:T(8,128)(2,1)S(1)} %advance.31.refs_4_.rest_3_), channel_id=1, source_target_pairs={{0,2},{2,4},{4,6},{6,8},{8,10},{10,12},{12,14},{14,16},{16,18},{18... | collective-permute-start | bytes 3145736 | tf_op jit(solution)/shard_map/ppermute | solution.py:27
  126.6 9.9 %collective-permute-start.24 = (bf16[128,1152]{1,0:T(8,128)(2,1)S(1)}, bf16[128,1152]{1,0:T(8,128)(2,1)S(1)}, u32[]{:S(2)}, u32[]{:S(2)}) collective-permute-start(bf16[128,1152]{1,0:T(8,128)(2,1)S(1)} %get-tuple-element.139.rest_3_), channel_id=1, source_target_pairs={{0,1},{1,0},{2,3},{3,2},{4,5},{5,4},{6,7},{7,6},{8,9},{9,8},{10,11... | collective-permute-start | bytes 884744 | tf_op jit(solution)/shard_map/ppermute | solution.py:27
  128.0 17.4 %collective-permute-start.23 = (bf16[128,1152]{1,0:T(8,128)(2,1)S(1)}, bf16[128,1152]{1,0:T(8,128)(2,1)S(1)}, u32[]{:S(2)}, u32[]{:S(2)}) collective-permute-start(bf16[128,1152]{1,0:T(8,128)(2,1)S(1)} %get-tuple-element.140.rest_3_), channel_id=1, source_target_pairs={{0,1},{1,0},{2,3},{3,2},{4,5},{5,4},{6,7},{7,6},{8,9},{9,8},{10,11... | collective-permute-start | bytes 884744 | tf_op jit(solution)/shard_map/ppermute | solution.py:27
  145.3 25.2 %collective-permute-start.31 = (bf16[128,4096]{1,0:T(8,128)(2,1)S(1)}, bf16[128,4096]{1,0:T(8,128)(2,1)S(1)}, u32[]{:S(2)}, u32[]{:S(2)}) collective-permute-start(bf16[128,4096]{1,0:T(8,128)(2,1)S(1)} %advance.32.rest_3_), channel_id=1, source_target_pairs={{0,2},{2,4},{4,6},{6,8},{8,10},{10,12},{12,14},{14,16},{16,18},{18... | collective-permute-start | bytes 3145736 | tf_op jit(solution)/shard_map/ppermute | solution.py:27
  154.2 25.5 %collective-permute-start.33 = (bf16[128,4096]{1,0:T(8,128)(2,1)S(1)}, bf16[128,4096]{1,0:T(8,128)(2,1)S(1)}, u32[]{:S(2)}, u32[]{:S(2)}) collective-permute-start(bf16[128,4096]{1,0:T(8,128)(2,1)S(1)} %advance.33.rest_3_), channel_id=1, source_target_pairs={{0,2},{2,4},{4,6},{6,8},{8,10},{10,12},{12,14},{14,16},{16,18},{18... | collective-permute-start | bytes 3145736 | tf_op jit(solution)/shard_map/ppermute | solution.py:27
  157.0 9.6 %collective-permute-start.28 = (bf16[128,1152]{1,0:T(8,128)(2,1)S(1)}, bf16[128,1152]{1,0:T(8,128)(2,1)S(1)}, u32[]{:S(2)}, u32[]{:S(2)}) collective-permute-start(bf16[128,1152]{1,0:T(8,128)(2,1)S(1)} %get-tuple-element.147.rest_3_), channel_id=1, source_target_pairs={{0,1},{1,0},{2,3},{3,2},{4,5},{5,4},{6,7},{7,6},{8,9},{9,8},{10,11... | collective-permute-start | bytes 884744 | tf_op jit(solution)/shard_map/ppermute | solution.py:27
  157.4 18.5 %collective-permute-start.27 = (bf16[128,1152]{1,0:T(8,128)(2,1)S(1)}, bf16[128,1152]{1,0:T(8,128)(2,1)S(1)}, u32[]{:S(2)}, u32[]{:S(2)}) collective-permute-start(bf16[128,1152]{1,0:T(8,128)(2,1)S(1)} %get-tuple-element.150.refs_4_.rest_3_), channel_id=1, source_target_pairs={{0,1},{1,0},{2,3},{3,2},{4,5},{5,4},{6,7},{7,6},{8,9},{9,8},{10,11... | collective-permute-start | bytes 884744 | tf_op jit(solution)/shard_map/ppermute | solution.py:27
  175.9 23.5 %collective-permute-start.38 = (bf16[128,4096]{1,0:T(8,128)(2,1)S(1)}, bf16[128,4096]{1,0:T(8,128)(2,1)S(1)}, u32[]{:S(2)}, u32[]{:S(2)}) collective-permute-start(bf16[128,4096]{1,0:T(8,128)(2,1)S(1)} %advance.34.rest_3_), channel_id=1, source_target_pairs={{0,2},{2,4},{4,6},{6,8},{8,10},{10,12},{12,14},{14,16},{16,18},{18... | collective-permute-start | bytes 3145736 | tf_op jit(solution)/shard_map/ppermute | solution.py:27
  184.9 23.4 %collective-permute-start.34 = (bf16[128,4096]{1,0:T(8,128)(2,1)S(1)}, bf16[128,4096]{1,0:T(8,128)(2,1)S(1)}, u32[]{:S(2)}, u32[]{:S(2)}) collective-permute-start(bf16[128,4096]{1,0:T(8,128)(2,1)S(1)} %advance.35.refs_4_.rest_3_), channel_id=1, source_target_pairs={{0,2},{2,4},{4,6},{6,8},{8,10},{10,12},{12,14},{14,16},{16,18},{18... | collective-permute-start | bytes 3145736 | tf_op jit(solution)/shard_map/ppermute | solution.py:27
  185.8 9.9 %collective-permute-start.36 = (bf16[128,1152]{1,0:T(8,128)(2,1)S(1)}, bf16[128,1152]{1,0:T(8,128)(2,1)S(1)}, u32[]{:S(2)}, u32[]{:S(2)}) collective-permute-start(bf16[128,1152]{1,0:T(8,128)(2,1)S(1)} %get-tuple-element.155.rest_3_), channel_id=1, source_target_pairs={{0,1},{1,0},{2,3},{3,2},{4,5},{5,4},{6,7},{7,6},{8,9},{9,8},{10,11... | collective-permute-start | bytes 884744 | tf_op jit(solution)/shard_map/ppermute | solution.py:27
  186.2 18.3 %collective-permute-start.35 = (bf16[128,1152]{1,0:T(8,128)(2,1)S(1)}, bf16[128,1152]{1,0:T(8,128)(2,1)S(1)}, u32[]{:S(2)}, u32[]{:S(2)}) collective-permute-start(bf16[128,1152]{1,0:T(8,128)(2,1)S(1)} %get-tuple-element.156.rest_3_), channel_id=1, source_target_pairs={{0,1},{1,0},{2,3},{3,2},{4,5},{5,4},{6,7},{7,6},{8,9},{9,8},{10,11... | collective-permute-start | bytes 884744 | tf_op jit(solution)/shard_map/ppermute | solution.py:27
  204.5 24.8 %collective-permute-start.43 = (bf16[128,4096]{1,0:T(8,128)(2,1)S(1)}, bf16[128,4096]{1,0:T(8,128)(2,1)S(1)}, u32[]{:S(2)}, u32[]{:S(2)}) collective-permute-start(bf16[128,4096]{1,0:T(8,128)(2,1)S(1)} %advance.36.rest_3_), channel_id=1, source_target_pairs={{0,2},{2,4},{4,6},{6,8},{8,10},{10,12},{12,14},{14,16},{16,18},{18... | collective-permute-start | bytes 3145736 | tf_op jit(solution)/shard_map/ppermute | solution.py:27
  213.4 25.2 %collective-permute-start.45 = (bf16[128,4096]{1,0:T(8,128)(2,1)S(1)}, bf16[128,4096]{1,0:T(8,128)(2,1)S(1)}, u32[]{:S(2)}, u32[]{:S(2)}) collective-permute-start(bf16[128,4096]{1,0:T(8,128)(2,1)S(1)} %advance.37.rest_3_), channel_id=1, source_target_pairs={{0,2},{2,4},{4,6},{6,8},{8,10},{10,12},{12,14},{14,16},{16,18},{18... | collective-permute-start | bytes 3145736 | tf_op jit(solution)/shard_map/ppermute | solution.py:27
  215.9 9.7 %collective-permute-start.40 = (bf16[128,1152]{1,0:T(8,128)(2,1)S(1)}, bf16[128,1152]{1,0:T(8,128)(2,1)S(1)}, u32[]{:S(2)}, u32[]{:S(2)}) collective-permute-start(bf16[128,1152]{1,0:T(8,128)(2,1)S(1)} %get-tuple-element.163.rest_3_), channel_id=1, source_target_pairs={{0,1},{1,0},{2,3},{3,2},{4,5},{5,4},{6,7},{7,6},{8,9},{9,8},{10,11... | collective-permute-start | bytes 884744 | tf_op jit(solution)/shard_map/ppermute | solution.py:27
  216.4 18.5 %collective-permute-start.39 = (bf16[128,1152]{1,0:T(8,128)(2,1)S(1)}, bf16[128,1152]{1,0:T(8,128)(2,1)S(1)}, u32[]{:S(2)}, u32[]{:S(2)}) collective-permute-start(bf16[128,1152]{1,0:T(8,128)(2,1)S(1)} %get-tuple-element.166.refs_4_.rest_3_), channel_id=1, source_target_pairs={{0,1},{1,0},{2,3},{3,2},{4,5},{5,4},{6,7},{7,6},{8,9},{9,8},{10,11... | collective-permute-start | bytes 884744 | tf_op jit(solution)/shard_map/ppermute | solution.py:27
  234.8 23.2 %collective-permute-start.50 = (bf16[128,4096]{1,0:T(8,128)(2,1)S(1)}, bf16[128,4096]{1,0:T(8,128)(2,1)S(1)}, u32[]{:S(2)}, u32[]{:S(2)}) collective-permute-start(bf16[128,4096]{1,0:T(8,128)(2,1)S(1)} %advance.38.rest_3_), channel_id=1, source_target_pairs={{0,2},{2,4},{4,6},{6,8},{8,10},{10,12},{12,14},{14,16},{16,18},{18... | collective-permute-start | bytes 3145736 | tf_op jit(solution)/shard_map/ppermute | solution.py:27
  243.7 24.0 %collective-permute-start.46 = (bf16[128,4096]{1,0:T(8,128)(2,1)S(1)}, bf16[128,4096]{1,0:T(8,128)(2,1)S(1)}, u32[]{:S(2)}, u32[]{:S(2)}) collective-permute-start(bf16[128,4096]{1,0:T(8,128)(2,1)S(1)} %advance.39.refs_4_.rest_3_), channel_id=1, source_target_pairs={{0,2},{2,4},{4,6},{6,8},{8,10},{10,12},{12,14},{14,16},{16,18},{18... | collective-permute-start | bytes 3145736 | tf_op jit(solution)/shard_map/ppermute | solution.py:27
  244.8 9.4 %collective-permute-start.48 = (bf16[128,1152]{1,0:T(8,128)(2,1)S(1)}, bf16[128,1152]{1,0:T(8,128)(2,1)S(1)}, u32[]{:S(2)}, u32[]{:S(2)}) collective-permute-start(bf16[128,1152]{1,0:T(8,128)(2,1)S(1)} %get-tuple-element.171.rest_3_), channel_id=1, source_target_pairs={{0,1},{1,0},{2,3},{3,2},{4,5},{5,4},{6,7},{7,6},{8,9},{9,8},{10,11... | collective-permute-start | bytes 884744 | tf_op jit(solution)/shard_map/ppermute | solution.py:27
  245.3 18.6 %collective-permute-start.47 = (bf16[128,1152]{1,0:T(8,128)(2,1)S(1)}, bf16[128,1152]{1,0:T(8,128)(2,1)S(1)}, u32[]{:S(2)}, u32[]{:S(2)}) collective-permute-start(bf16[128,1152]{1,0:T(8,128)(2,1)S(1)} %get-tuple-element.172.rest_3_), channel_id=1, source_target_pairs={{0,1},{1,0},{2,3},{3,2},{4,5},{5,4},{6,7},{7,6},{8,9},{9,8},{10,11... | collective-permute-start | bytes 884744 | tf_op jit(solution)/shard_map/ppermute | solution.py:27
  263.6 24.1 %collective-permute-start.55 = (bf16[128,4096]{1,0:T(8,128)(2,1)S(1)}, bf16[128,4096]{1,0:T(8,128)(2,1)S(1)}, u32[]{:S(2)}, u32[]{:S(2)}) collective-permute-start(bf16[128,4096]{1,0:T(8,128)(2,1)S(1)} %advance.40.rest_3_), channel_id=1, source_target_pairs={{0,2},{2,4},{4,6},{6,8},{8,10},{10,12},{12,14},{14,16},{16,18},{18... | collective-permute-start | bytes 3145736 | tf_op jit(solution)/shard_map/ppermute | solution.py:27
  273.2 23.5 %collective-permute-start.57 = (bf16[128,4096]{1,0:T(8,128)(2,1)S(1)}, bf16[128,4096]{1,0:T(8,128)(2,1)S(1)}, u32[]{:S(2)}, u32[]{:S(2)}) collective-permute-start(bf16[128,4096]{1,0:T(8,128)(2,1)S(1)} %advance.41.rest_3_), channel_id=1, source_target_pairs={{0,2},{2,4},{4,6},{6,8},{8,10},{10,12},{12,14},{14,16},{16,18},{18... | collective-permute-start | bytes 3145736 | tf_op jit(solution)/shard_map/ppermute | solution.py:27
  274.0 9.9 %collective-permute-start.52 = (bf16[128,1152]{1,0:T(8,128)(2,1)S(1)}, bf16[128,1152]{1,0:T(8,128)(2,1)S(1)}, u32[]{:S(2)}, u32[]{:S(2)}) collective-permute-start(bf16[128,1152]{1,0:T(8,128)(2,1)S(1)} %get-tuple-element.179.rest_3_), channel_id=1, source_target_pairs={{0,1},{1,0},{2,3},{3,2},{4,5},{5,4},{6,7},{7,6},{8,9},{9,8},{10,11... | collective-permute-start | bytes 884744 | tf_op jit(solution)/shard_map/ppermute | solution.py:27
  274.5 18.4 %collective-permute-start.51 = (bf16[128,1152]{1,0:T(8,128)(2,1)S(1)}, bf16[128,1152]{1,0:T(8,128)(2,1)S(1)}, u32[]{:S(2)}, u32[]{:S(2)}) collective-permute-start(bf16[128,1152]{1,0:T(8,128)(2,1)S(1)} %get-tuple-element.182.refs_4_.rest_3_), channel_id=1, source_target_pairs={{0,1},{1,0},{2,3},{3,2},{4,5},{5,4},{6,7},{7,6},{8,9},{9,8},{10,11... | collective-permute-start | bytes 884744 | tf_op jit(solution)/shard_map/ppermute | solution.py:27
  292.9 23.4 %collective-permute-start.62 = (bf16[128,4096]{1,0:T(8,128)(2,1)S(1)}, bf16[128,4096]{1,0:T(8,128)(2,1)S(1)}, u32[]{:S(2)}, u32[]{:S(2)}) collective-permute-start(bf16[128,4096]{1,0:T(8,128)(2,1)S(1)} %advance.42.rest_3_), channel_id=1, source_target_pairs={{0,2},{2,4},{4,6},{6,8},{8,10},{10,12},{12,14},{14,16},{16,18},{18... | collective-permute-start | bytes 3145736 | tf_op jit(solution)/shard_map/ppermute | solution.py:27
  302.3 23.1 %collective-permute-start.58 = (bf16[128,4096]{1,0:T(8,128)(2,1)S(1)}, bf16[128,4096]{1,0:T(8,128)(2,1)S(1)}, u32[]{:S(2)}, u32[]{:S(2)}) collective-permute-start(bf16[128,4096]{1,0:T(8,128)(2,1)S(1)} %advance.43.refs_4_.rest_3_), channel_id=1, source_target_pairs={{0,2},{2,4},{4,6},{6,8},{8,10},{10,12},{12,14},{14,16},{16,18},{18... | collective-permute-start | bytes 3145736 | tf_op jit(solution)/shard_map/ppermute | solution.py:27
  302.8 9.8 %collective-permute-start.60 = (bf16[128,1152]{1,0:T(8,128)(2,1)S(1)}, bf16[128,1152]{1,0:T(8,128)(2,1)S(1)}, u32[]{:S(2)}, u32[]{:S(2)}) collective-permute-start(bf16[128,1152]{1,0:T(8,128)(2,1)S(1)} %get-tuple-element.187.rest_3_), channel_id=1, source_target_pairs={{0,1},{1,0},{2,3},{3,2},{4,5},{5,4},{6,7},{7,6},{8,9},{9,8},{10,11... | collective-permute-start | bytes 884744 | tf_op jit(solution)/shard_map/ppermute | solution.py:27
  303.2 18.5 %collective-permute-start.59 = (bf16[128,1152]{1,0:T(8,128)(2,1)S(1)}, bf16[128,1152]{1,0:T(8,128)(2,1)S(1)}, u32[]{:S(2)}, u32[]{:S(2)}) collective-permute-start(bf16[128,1152]{1,0:T(8,128)(2,1)S(1)} %get-tuple-element.188.rest_3_), channel_id=1, source_target_pairs={{0,1},{1,0},{2,3},{3,2},{4,5},{5,4},{6,7},{7,6},{8,9},{9,8},{10,11... | collective-permute-start | bytes 884744 | tf_op jit(solution)/shard_map/ppermute | solution.py:27
  317.6 13.3 %collective-permute-start.64 = (bf16[128,1152]{1,0:T(8,128)(2,1)S(1)}, bf16[128,1152]{1,0:T(8,128)(2,1)S(1)}, u32[]{:S(2)}, u32[]{:S(2)}) collective-permute-start(bf16[128,1152]{1,0:T(8,128)(2,1)S(1)} %get-tuple-element.195.rest_3_), channel_id=1, source_target_pairs={{0,1},{1,0},{2,3},{3,2},{4,5},{5,4},{6,7},{7,6},{8,9},{9,8},{10,11... | collective-permute-start | bytes 884744 | tf_op jit(solution)/shard_map/ppermute | solution.py:27
  326.8 13.0 %collective-permute-start.63 = (bf16[128,1152]{1,0:T(8,128)(2,1)S(1)}, bf16[128,1152]{1,0:T(8,128)(2,1)S(1)}, u32[]{:S(2)}, u32[]{:S(2)}) collective-permute-start(bf16[128,1152]{1,0:T(8,128)(2,1)S(1)} %get-tuple-element.198.rest_3_), channel_id=1, source_target_pairs={{0,1},{1,0},{2,3},{3,2},{4,5},{5,4},{6,7},{7,6},{8,9},{9,8},{10,11... | collective-permute-start | bytes 884744 | tf_op jit(solution)/shard_map/ppermute | solution.py:27
  343.3 17.0 %collective-permute-start.71 = (bf16[128,4096]{1,0:T(8,128)(2,1)S(1)}, bf16[128,4096]{1,0:T(8,128)(2,1)S(1)}, u32[]{:S(2)}, u32[]{:S(2)}) collective-permute-start(bf16[128,4096]{1,0:T(8,128)(2,1)S(1)} %advance.44.rest_3_), channel_id=1, source_target_pairs={{0,2},{2,4},{4,6},{6,8},{8,10},{10,12},{12,14},{14,16},{16,18},{18... | collective-permute-start | bytes 3145736 | tf_op jit(solution)/shard_map/ppermute | solution.py:27
  343.3 28.1 %collective-permute-start.70 = (bf16[128,4096]{1,0:T(8,128)(2,1)S(1)}, bf16[128,4096]{1,0:T(8,128)(2,1)S(1)}, u32[]{:S(2)}, u32[]{:S(2)}) collective-permute-start(bf16[128,4096]{1,0:T(8,128)(2,1)S(1)} %advance.45.rest_3_), channel_id=1, source_target_pairs={{0,2},{2,4},{4,6},{6,8},{8,10},{10,12},{12,14},{14,16},{16,18},{18... | collective-permute-start | bytes 3145736 | tf_op jit(solution)/shard_map/ppermute | solution.py:27
  345.3 37.4 %collective-permute-start.69 = (bf16[128,4096]{1,0:T(8,128)(2,1)S(1)}, bf16[128,4096]{1,0:T(8,128)(2,1)S(1)}, u32[]{:S(2)}, u32[]{:S(2)}) collective-permute-start(bf16[128,4096]{1,0:T(8,128)(2,1)S(1)} %advance.46.rest_3_), channel_id=1, source_target_pairs={{0,2},{2,4},{4,6},{6,8},{8,10},{10,12},{12,14},{14,16},{16,18},{18... | collective-permute-start | bytes 3145736 | tf_op jit(solution)/shard_map/ppermute | solution.py:27
  348.8 45.2 %collective-permute-start.68 = (bf16[128,4096]{1,0:T(8,128)(2,1)S(1)}, bf16[128,4096]{1,0:T(8,128)(2,1)S(1)}, u32[]{:S(2)}, u32[]{:S(2)}) collective-permute-start(bf16[128,4096]{1,0:T(8,128)(2,1)S(1)} %advance.47), channel_id=1, source_target_pairs={{0,2},{2,4},{4,6},{6,8},{8,10},{10,12},{12,14},{14,16},{16,18},{18... | collective-permute-start | bytes 3145736 | tf_op jit(solution)/shard_map/ppermute | solution.py:27
  (25 other events, 111.1 us)

commit v3 on v2

--- a/solution.py
+++ b/solution.py
@@ -9,7 +9,8 @@
 
 
 TICKS = 6
-CHUNKS = 4
+SHARES = (4, 4, 4, 4)
+CHUNKS = len(SHARES)
 LEAD = 2
 PIECES = 4
 EPSILON = 1e-05
@@ -53,11 +54,14 @@
     return copies
 
 
-def fetch_body(count, tick, first, table_ref, stream_ref, *refs):
-    sources, h_ref, targets, semaphores = refs[:count], refs[count], refs[count + 1 : -1], refs[-1]
+def fetch_body(count, tick, blocks, table_ref, stream_ref, *refs):
+    sources, targets, semaphores = refs[:count], refs[-1 - count - len(blocks) : -1], refs[-1]
     lap = table_ref[tick]
     copies = fetch_copies(
-        (stream_ref, *sources), (h_ref, *targets), semaphores, [(0, first)] + [(lap, 0, 0)] * count
+        (*sources, *([stream_ref] * len(blocks))),
+        targets,
+        semaphores,
+        [(lap, 0, 0)] * count + [(0, first) for first, _ in blocks],
     )
     for copy in copies:
         copy.start()
@@ -65,22 +69,22 @@
         copy.wait()
 
 
-def fetch(table, tick, stream, first, rows, stacked):
+def fetch(table, tick, stream, blocks, stacked, after):
     count = len(stacked)
     features = stream.shape[2]
     return pl.pallas_call(
-        functools.partial(fetch_body, count, tick, first),
-        in_specs=[IN_SMEM] + [IN_HBM] * (1 + count),
-        out_specs=[IN_VMEM] * (1 + count),
-        out_shape=[pltpu.VMEM((rows, features), stream.dtype)]
-        + [pltpu.VMEM(value.shape[2:], value.dtype) for value in stacked],
-        scratch_shapes=[pltpu.SemaphoreType.DMA((1 + count, PIECES))],
+        functools.partial(fetch_body, count, tick, blocks),
+        in_specs=[IN_SMEM] + [IN_HBM] * (1 + count) + [ANYWHERE] * len(after),
+        out_specs=[IN_VMEM] * (count + len(blocks)),
+        out_shape=[pltpu.VMEM(value.shape[2:], value.dtype) for value in stacked]
+        + [pltpu.VMEM((rows, features), stream.dtype) for _, rows in blocks],
+        scratch_shapes=[pltpu.SemaphoreType.DMA((count + len(blocks), PIECES))],
         compiler_params=params(),
         cost_estimate=pl.CostEstimate(
             flops=0, transcendentals=0, bytes_accessed=sum(value.size * value.dtype.itemsize for value in stacked)
         ),
         name="fetch",
-    )(table, stream, *stacked)
+    )(table, stream, *stacked, *after)
 
 
 def refresh_body(count, tick, table_ref, *refs):
@@ -297,18 +301,18 @@
     table = jnp.where(ticks < TICKS, laps, lax.axis_index("tensor"))
     expert = jnp.swapaxes(expert_factor[:, 0], 1, 2)
     width = stream.shape[2] * parts
-    rows = stream.shape[1] // CHUNKS
     stream, *stacked = [
         pltpu.with_memory_space_constraint(value, pltpu.HBM)
         for value in (stream, down_factor, router, core_tensor, up_factor)
     ]
-    held, resident = [], []
-    for chunk in range(CHUNKS):
-        share = stacked[:2] if chunk == 0 else stacked[2:] if chunk == 1 else []
-        h, *fetched = fetch(table, 0, stream, chunk * rows, rows, share)
-        held.append(h)
-        resident += fetched
-    early, late = resident[:2], resident[2:]
+    blocks, start = [], 0
+    for share in SHARES:
+        rows = stream.shape[1] * share // sum(SHARES)
+        blocks.append((start, rows))
+        start += rows
+    *early, front = fetch(table, 0, stream, blocks[:1], stacked[:2], [])
+    *late, back = fetch(table, 0, stream, blocks[1:2], stacked[2:], [])
+    held = [front, back]
 
     def exchange(own, square, sent):
         if parts == 2:
@@ -325,6 +329,7 @@
     steps = TICKS * CHUNKS
     projected = [exchange(*project(held[at], *early, [])) for at in range(LEAD)]
     piece = core(table, 0, *projected[0], expert, late[0], width, [])
+    held += fetch(table, 0, stream, blocks[2:], [], [piece])
     for step in range(steps):
         tick, chunk = divmod(step, CHUNKS)
         order = []
@@ -346,8 +351,8 @@
                 table, (step + 1) // CHUNKS, *projected[step + 1], expert, late[0], width, [value]
             )
     out = None
-    for chunk, h in enumerate(held):
-        out = store(h, chunk * rows, stream.shape, stream.dtype, out)
+    for h, (first, _) in zip(held, blocks):
+        out = store(h, first, stream.shape, stream.dtype, out)
     return out
 
 

time: 403 us -> 401 us (level)
    ppermute x72, waiting for transfers between devices: 162 us -> 158 us  [from_behind(): return lax.ppermute(value, axis, pairs)]
    pallas_call x4 -> x3, Pallas kernels: 14.7 us -> 13.2 us  [fetch(): pl.pallas_call(functools.partial(fetch_body, count, tick, blocks), in_spe...]
where the time goes in v3:
time: 401 us; the launch traced here: 393 us
  Pallas kernels  165 us (41%)
  waiting for transfers between devices  158 us (39%)
  starting transfers between devices  69.9 us (17%)
    ppermute x72, waiting for transfers between devices, from_behind(): return lax.ppermute(value, axis, pairs)  158 us
    pallas_call x24, Pallas kernels, core(): pl.pallas_call(functools.partial(core_body, others, width, tick), in_spec...  76.8 us
    ppermute x72, starting transfers between devices, from_behind(): return lax.ppermute(value, axis, pairs)  69.9 us
    pallas_call x24, Pallas kernels, project(): pl.pallas_call(project_body, in_specs=[IN_VMEM] * 3 + [ANYWHERE] * len(af...  32.4 us
    pallas_call x24, Pallas kernels, advance(): pl.pallas_call(functools.partial(advance_body, pieces), in_specs=[IN_SMEM...  30.6 us
    pallas_call x3, Pallas kernels, fetch(): pl.pallas_call(functools.partial(fetch_body, count, tick, blocks), in_spe...  13.2 us
  transfers between devices with their start and end apart: 72, of which 38 were waited for; matrix products, arithmetic and copies ran while one was open for 0% of the time, Pallas kernels for 39%

profile of v3, /device:TPU:0, one launch (start us, length us, event | category | flops | bytes accessed | tf_op | source)
XLA Modules:
  0.0 393.5 jit_solution(13660672569479300994)
XLA Ops:
  0.0 4.7 %fetch.3 = (bf16[4096,512]{1,0:T(8,128)(2,1)S(1)}, bf16[4096,512]{1,0:T(8,128)(2,1)S(1)}, f32[128,4096]{1,0:T(8,128)S(1)}) custom-call(s32[7]{0:T(128)S(1)} %compare_select_fusion.2.table_ref, f32[1,512,4096]{2,1,0:T(8,128)} %stream_ref.5, bf16[2,1,4096,512]{3,2,1,0:T(8,128)(2,1)} %refs_0_.22, bf16[2,1,4096,512]{3,2,1,0:T(8,128)(2,1)} %refs_1_.22), custom_call_target="tpu_custom_call" | custom-call | bytes 16777216 | tf_op jit(solution)/shard_map/fetch/pallas_call | solution.py:75
  6.0 3.0 collective-permute-start
  9.1 5.8 %fetch.4 = (bf16[256,32,512]{2,1,0:T(8,128)(2,1)S(1)}, bf16[512,4096]{1,0:T(8,128)(2,1)S(1)}, f32[128,4096]{1,0:T(8,128)S(1)}) custom-call(s32[7]{0:T(128)S(1)} %compare_select_fusion.2.table_ref, f32[1,512,4096]{2,1,0:T(8,128)} %stream_ref.5, bf16[2,1,256,32,512]{4,3,2,1,0:T(8,128)(2,1)} %refs_0_.23, bf16[2,1,512,4096]{3,2,1,0:T(8,128)(2,1)} %refs_1_.23), custom_call_target="tpu_custom_call" | custom-call | bytes 25165824 | tf_op jit(solution)/shard_map/fetch/pallas_call | solution.py:75
  16.3 3.2 core.24.refs_0_.rest_0_
  21.5 2.8 fetch.5
  27.5 3.2 core.25.rest_0_
  39.7 7.9 %collective-permute-done.4.rest_0_ = bf16[128,1152]{1,0:T(8,128)(2,1)S(1)} collective-permute-done((bf16[128,1152]{1,0:T(8,128)(2,1)S(1)}, bf16[128,1152]{1,0:T(8,128)(2,1)S(1)}, u32[]{:S(2)}, u32[]{:S(2)}) %collective-permute-start.4) | collective-permute-done | bytes 294944 | tf_op jit(solution)/shard_map/ppermute | solution.py:28
  47.6 3.2 core.26.rest_0_
  52.6 2.5 collective-permute-done.6.rest_1_
  56.5 3.2 core.27.rest_0_
  61.6 2.4 collective-permute-done.8.rest_1_
  69.0 7.2 %collective-permute-done.12.rest_0_ = bf16[128,1152]{1,0:T(8,128)(2,1)S(1)} collective-permute-done((bf16[128,1152]{1,0:T(8,128)(2,1)S(1)}, bf16[128,1152]{1,0:T(8,128)(2,1)S(1)}, u32[]{:S(2)}, u32[]{:S(2)}) %collective-permute-start.12) | collective-permute-done | bytes 294944 | tf_op jit(solution)/shard_map/ppermute | solution.py:28
  76.2 3.2 core.28.rest_0_
  81.4 2.6 collective-permute-done.13.rest_1_
  85.3 3.2 core.29.rest_0_
  97.2 7.6 %collective-permute-done.16.rest_0_ = bf16[128,1152]{1,0:T(8,128)(2,1)S(1)} collective-permute-done((bf16[128,1152]{1,0:T(8,128)(2,1)S(1)}, bf16[128,1152]{1,0:T(8,128)(2,1)S(1)}, u32[]{:S(2)}, u32[]{:S(2)}) %collective-permute-start.16) | collective-permute-done | bytes 294944 | tf_op jit(solution)/shard_map/ppermute | solution.py:28
  104.9 3.2 core.30.rest_0_
  109.8 3.0 collective-permute-done.18.rest_1_
  114.2 3.2 core.31.rest_0_
  126.8 7.2 %collective-permute-done.24.rest_0_ = bf16[128,1152]{1,0:T(8,128)(2,1)S(1)} collective-permute-done((bf16[128,1152]{1,0:T(8,128)(2,1)S(1)}, bf16[128,1152]{1,0:T(8,128)(2,1)S(1)}, u32[]{:S(2)}, u32[]{:S(2)}) %collective-permute-start.24) | collective-permute-done | bytes 294944 | tf_op jit(solution)/shard_map/ppermute | solution.py:28
  134.0 3.2 core.32.rest_0_
  142.9 3.2 core.33.rest_0_
  155.6 7.8 %collective-permute-done.28.rest_0_ = bf16[128,1152]{1,0:T(8,128)(2,1)S(1)} collective-permute-done((bf16[128,1152]{1,0:T(8,128)(2,1)S(1)}, bf16[128,1152]{1,0:T(8,128)(2,1)S(1)}, u32[]{:S(2)}, u32[]{:S(2)}) %collective-permute-start.28) | collective-permute-done | bytes 294944 | tf_op jit(solution)/shard_map/ppermute | solution.py:28
  163.4 3.2 core.34.rest_0_
  172.6 3.2 core.35.rest_0_
  185.1 7.2 %collective-permute-done.36.rest_0_ = bf16[128,1152]{1,0:T(8,128)(2,1)S(1)} collective-permute-done((bf16[128,1152]{1,0:T(8,128)(2,1)S(1)}, bf16[128,1152]{1,0:T(8,128)(2,1)S(1)}, u32[]{:S(2)}, u32[]{:S(2)}) %collective-permute-start.36) | collective-permute-done | bytes 294944 | tf_op jit(solution)/shard_map/ppermute | solution.py:28
  192.3 3.2 core.36.rest_0_
  201.3 3.2 core.37.rest_0_
  210.1 2.5 collective-permute-start.45
  214.6 7.6 %collective-permute-done.40.rest_0_ = bf16[128,1152]{1,0:T(8,128)(2,1)S(1)} collective-permute-done((bf16[128,1152]{1,0:T(8,128)(2,1)S(1)}, bf16[128,1152]{1,0:T(8,128)(2,1)S(1)}, u32[]{:S(2)}, u32[]{:S(2)}) %collective-permute-start.40) | collective-permute-done | bytes 294944 | tf_op jit(solution)/shard_map/ppermute | solution.py:28
  222.3 3.2 core.38.rest_0_
  231.6 3.2 core.39.rest_0_
  244.2 6.7 %collective-permute-done.48.rest_0_ = bf16[128,1152]{1,0:T(8,128)(2,1)S(1)} collective-permute-done((bf16[128,1152]{1,0:T(8,128)(2,1)S(1)}, bf16[128,1152]{1,0:T(8,128)(2,1)S(1)}, u32[]{:S(2)}, u32[]{:S(2)}) %collective-permute-start.48) | collective-permute-done | bytes 294944 | tf_op jit(solution)/shard_map/ppermute | solution.py:28
  250.9 3.2 core.40.rest_0_
  260.6 3.2 core.41.rest_0_
  272.8 7.9 %collective-permute-done.52.rest_0_ = bf16[128,1152]{1,0:T(8,128)(2,1)S(1)} collective-permute-done((bf16[128,1152]{1,0:T(8,128)(2,1)S(1)}, bf16[128,1152]{1,0:T(8,128)(2,1)S(1)}, u32[]{:S(2)}, u32[]{:S(2)}) %collective-permute-start.52) | collective-permute-done | bytes 294944 | tf_op jit(solution)/shard_map/ppermute | solution.py:28
  280.6 3.2 core.42.rest_0_
  289.6 3.2 core.43.rest_0_
  302.1 7.0 %collective-permute-done.60.rest_0_ = bf16[128,1152]{1,0:T(8,128)(2,1)S(1)} collective-permute-done((bf16[128,1152]{1,0:T(8,128)(2,1)S(1)}, bf16[128,1152]{1,0:T(8,128)(2,1)S(1)}, u32[]{:S(2)}, u32[]{:S(2)}) %collective-permute-start.60) | collective-permute-done | bytes 294944 | tf_op jit(solution)/shard_map/ppermute | solution.py:28
  309.2 3.2 core.44.rest_0_
  318.4 3.2 core.45.rest_0_
  327.2 3.2 core.46.rest_0_
  332.1 2.6 collective-permute-done.66.rest_1_
  336.0 3.4 core.47.rest_0_
  345.6 12.5 %collective-permute-done.71.refs_0_ = bf16[128,4096]{1,0:T(8,128)(2,1)S(1)} collective-permute-done((bf16[128,4096]{1,0:T(8,128)(2,1)S(1)}, bf16[128,4096]{1,0:T(8,128)(2,1)S(1)}, u32[]{:S(2)}, u32[]{:S(2)}) %collective-permute-start.71) | collective-permute-done | bytes 1048608 | tf_op jit(solution)/shard_map/ppermute | solution.py:28
  359.5 9.8 %collective-permute-done.70.refs_0_ = bf16[128,4096]{1,0:T(8,128)(2,1)S(1)} collective-permute-done((bf16[128,4096]{1,0:T(8,128)(2,1)S(1)}, bf16[128,4096]{1,0:T(8,128)(2,1)S(1)}, u32[]{:S(2)}, u32[]{:S(2)}) %collective-permute-start.70) | collective-permute-done | bytes 1048608 | tf_op jit(solution)/shard_map/ppermute | solution.py:28
  370.7 9.8 %collective-permute-done.69.refs_0_ = bf16[128,4096]{1,0:T(8,128)(2,1)S(1)} collective-permute-done((bf16[128,4096]{1,0:T(8,128)(2,1)S(1)}, bf16[128,4096]{1,0:T(8,128)(2,1)S(1)}, u32[]{:S(2)}, u32[]{:S(2)}) %collective-permute-start.69) | collective-permute-done | bytes 1048608 | tf_op jit(solution)/shard_map/ppermute | solution.py:28
  382.0 9.8 %collective-permute-done.68.refs_0_ = bf16[128,4096]{1,0:T(8,128)(2,1)S(1)} collective-permute-done((bf16[128,4096]{1,0:T(8,128)(2,1)S(1)}, bf16[128,4096]{1,0:T(8,128)(2,1)S(1)}, u32[]{:S(2)}, u32[]{:S(2)}) %collective-permute-start.68) | collective-permute-done | bytes 1048608 | tf_op jit(solution)/shard_map/ppermute | solution.py:28
  (188 shorter events, 167.6 us)
Async XLA Ops:
  6.0 10.2 %collective-permute-start = (bf16[128,1152]{1,0:T(8,128)(2,1)S(1)}, bf16[128,1152]{1,0:T(8,128)(2,1)S(1)}, u32[]{:S(2)}, u32[]{:S(2)}) collective-permute-start(bf16[128,1152]{1,0:T(8,128)(2,1)S(1)} %get-tuple-element.110), channel_id=1, source_target_pairs={{0,1},{1,0},{2,3},{3,2},{4,5},{5,4},{6,7},{7,6},{8,9},{9,8},{10,11... | collective-permute-start | bytes 884744 | tf_op jit(solution)/shard_map/ppermute | solution.py:28
  16.2 11.3 %collective-permute-start.1 = (bf16[128,1152]{1,0:T(8,128)(2,1)S(1)}, bf16[128,1152]{1,0:T(8,128)(2,1)S(1)}, u32[]{:S(2)}, u32[]{:S(2)}) collective-permute-start(bf16[128,1152]{1,0:T(8,128)(2,1)S(1)} %get-tuple-element.116), channel_id=1, source_target_pairs={{0,1},{1,0},{2,3},{3,2},{4,5},{5,4},{6,7},{7,6},{8,9},{9,8},{10,11... | collective-permute-start | bytes 884744 | tf_op jit(solution)/shard_map/ppermute | solution.py:28
  27.4 23.8 %collective-permute-start.7 = (bf16[128,4096]{1,0:T(8,128)(2,1)S(1)}, bf16[128,4096]{1,0:T(8,128)(2,1)S(1)}, u32[]{:S(2)}, u32[]{:S(2)}) collective-permute-start(bf16[128,4096]{1,0:T(8,128)(2,1)S(1)} %advance.24.rest_3_), channel_id=1, source_target_pairs={{0,2},{2,4},{4,6},{6,8},{8,10},{10,12},{12,14},{14,16},{16,18},{18... | collective-permute-start | bytes 3145736 | tf_op jit(solution)/shard_map/ppermute | solution.py:28
  36.4 23.9 %collective-permute-start.9 = (bf16[128,4096]{1,0:T(8,128)(2,1)S(1)}, bf16[128,4096]{1,0:T(8,128)(2,1)S(1)}, u32[]{:S(2)}, u32[]{:S(2)}) collective-permute-start(bf16[128,4096]{1,0:T(8,128)(2,1)S(1)} %advance.25.rest_3_), channel_id=1, source_target_pairs={{0,2},{2,4},{4,6},{6,8},{8,10},{10,12},{12,14},{14,16},{16,18},{18... | collective-permute-start | bytes 3145736 | tf_op jit(solution)/shard_map/ppermute | solution.py:28
  37.7 9.9 %collective-permute-start.4 = (bf16[128,1152]{1,0:T(8,128)(2,1)S(1)}, bf16[128,1152]{1,0:T(8,128)(2,1)S(1)}, u32[]{:S(2)}, u32[]{:S(2)}) collective-permute-start(bf16[128,1152]{1,0:T(8,128)(2,1)S(1)} %get-tuple-element.119.rest_3_), channel_id=1, source_target_pairs={{0,1},{1,0},{2,3},{3,2},{4,5},{5,4},{6,7},{7,6},{8,9},{9,8},{10,11... | collective-permute-start | bytes 884744 | tf_op jit(solution)/shard_map/ppermute | solution.py:28
  38.1 18.4 %collective-permute-start.3 = (bf16[128,1152]{1,0:T(8,128)(2,1)S(1)}, bf16[128,1152]{1,0:T(8,128)(2,1)S(1)}, u32[]{:S(2)}, u32[]{:S(2)}) collective-permute-start(bf16[128,1152]{1,0:T(8,128)(2,1)S(1)} %get-tuple-element.122.refs_4_.rest_3_), channel_id=1, source_target_pairs={{0,1},{1,0},{2,3},{3,2},{4,5},{5,4},{6,7},{7,6},{8,9},{9,8},{10,11... | collective-permute-start | bytes 884744 | tf_op jit(solution)/shard_map/ppermute | solution.py:28
  56.4 23.6 %collective-permute-start.14 = (bf16[128,4096]{1,0:T(8,128)(2,1)S(1)}, bf16[128,4096]{1,0:T(8,128)(2,1)S(1)}, u32[]{:S(2)}, u32[]{:S(2)}) collective-permute-start(bf16[128,4096]{1,0:T(8,128)(2,1)S(1)} %advance.26.rest_3_), channel_id=1, source_target_pairs={{0,2},{2,4},{4,6},{6,8},{8,10},{10,12},{12,14},{14,16},{16,18},{18... | collective-permute-start | bytes 3145736 | tf_op jit(solution)/shard_map/ppermute | solution.py:28
  65.3 23.9 %collective-permute-start.10 = (bf16[128,4096]{1,0:T(8,128)(2,1)S(1)}, bf16[128,4096]{1,0:T(8,128)(2,1)S(1)}, u32[]{:S(2)}, u32[]{:S(2)}) collective-permute-start(bf16[128,4096]{1,0:T(8,128)(2,1)S(1)} %advance.27.refs_4_.rest_3_), channel_id=1, source_target_pairs={{0,2},{2,4},{4,6},{6,8},{8,10},{10,12},{12,14},{14,16},{16,18},{18... | collective-permute-start | bytes 3145736 | tf_op jit(solution)/shard_map/ppermute | solution.py:28
  66.4 9.9 %collective-permute-start.12 = (bf16[128,1152]{1,0:T(8,128)(2,1)S(1)}, bf16[128,1152]{1,0:T(8,128)(2,1)S(1)}, u32[]{:S(2)}, u32[]{:S(2)}) collective-permute-start(bf16[128,1152]{1,0:T(8,128)(2,1)S(1)} %get-tuple-element.127.rest_3_), channel_id=1, source_target_pairs={{0,1},{1,0},{2,3},{3,2},{4,5},{5,4},{6,7},{7,6},{8,9},{9,8},{10,11... | collective-permute-start | bytes 884744 | tf_op jit(solution)/shard_map/ppermute | solution.py:28
  66.9 18.4 %collective-permute-start.11 = (bf16[128,1152]{1,0:T(8,128)(2,1)S(1)}, bf16[128,1152]{1,0:T(8,128)(2,1)S(1)}, u32[]{:S(2)}, u32[]{:S(2)}) collective-permute-start(bf16[128,1152]{1,0:T(8,128)(2,1)S(1)} %get-tuple-element.128.rest_3_), channel_id=1, source_target_pairs={{0,1},{1,0},{2,3},{3,2},{4,5},{5,4},{6,7},{7,6},{8,9},{9,8},{10,11... | collective-permute-start | bytes 884744 | tf_op jit(solution)/shard_map/ppermute | solution.py:28
  85.3 23.2 %collective-permute-start.19 = (bf16[128,4096]{1,0:T(8,128)(2,1)S(1)}, bf16[128,4096]{1,0:T(8,128)(2,1)S(1)}, u32[]{:S(2)}, u32[]{:S(2)}) collective-permute-start(bf16[128,4096]{1,0:T(8,128)(2,1)S(1)} %advance.28.rest_3_), channel_id=1, source_target_pairs={{0,2},{2,4},{4,6},{6,8},{8,10},{10,12},{12,14},{14,16},{16,18},{18... | collective-permute-start | bytes 3145736 | tf_op jit(solution)/shard_map/ppermute | solution.py:28
  94.1 24.0 %collective-permute-start.21 = (bf16[128,4096]{1,0:T(8,128)(2,1)S(1)}, bf16[128,4096]{1,0:T(8,128)(2,1)S(1)}, u32[]{:S(2)}, u32[]{:S(2)}) collective-permute-start(bf16[128,4096]{1,0:T(8,128)(2,1)S(1)} %advance.29.rest_3_), channel_id=1, source_target_pairs={{0,2},{2,4},{4,6},{6,8},{8,10},{10,12},{12,14},{14,16},{16,18},{18... | collective-permute-start | bytes 3145736 | tf_op jit(solution)/shard_map/ppermute | solution.py:28
  95.2 9.7 %collective-permute-start.16 = (bf16[128,1152]{1,0:T(8,128)(2,1)S(1)}, bf16[128,1152]{1,0:T(8,128)(2,1)S(1)}, u32[]{:S(2)}, u32[]{:S(2)}) collective-permute-start(bf16[128,1152]{1,0:T(8,128)(2,1)S(1)} %get-tuple-element.135.rest_3_), channel_id=1, source_target_pairs={{0,1},{1,0},{2,3},{3,2},{4,5},{5,4},{6,7},{7,6},{8,9},{9,8},{10,11... | collective-permute-start | bytes 884744 | tf_op jit(solution)/shard_map/ppermute | solution.py:28
  95.8 18.4 %collective-permute-start.15 = (bf16[128,1152]{1,0:T(8,128)(2,1)S(1)}, bf16[128,1152]{1,0:T(8,128)(2,1)S(1)}, u32[]{:S(2)}, u32[]{:S(2)}) collective-permute-start(bf16[128,1152]{1,0:T(8,128)(2,1)S(1)} %get-tuple-element.138.refs_4_.rest_3_), channel_id=1, source_target_pairs={{0,1},{1,0},{2,3},{3,2},{4,5},{5,4},{6,7},{7,6},{8,9},{9,8},{10,11... | collective-permute-start | bytes 884744 | tf_op jit(solution)/shard_map/ppermute | solution.py:28
  114.1 23.9 %collective-permute-start.26 = (bf16[128,4096]{1,0:T(8,128)(2,1)S(1)}, bf16[128,4096]{1,0:T(8,128)(2,1)S(1)}, u32[]{:S(2)}, u32[]{:S(2)}) collective-permute-start(bf16[128,4096]{1,0:T(8,128)(2,1)S(1)} %advance.30.rest_3_), channel_id=1, source_target_pairs={{0,2},{2,4},{4,6},{6,8},{8,10},{10,12},{12,14},{14,16},{16,18},{18... | collective-permute-start | bytes 3145736 | tf_op jit(solution)/shard_map/ppermute | solution.py:28
  123.2 23.7 %collective-permute-start.22 = (bf16[128,4096]{1,0:T(8,128)(2,1)S(1)}, bf16[128,4096]{1,0:T(8,128)(2,1)S(1)}, u32[]{:S(2)}, u32[]{:S(2)}) collective-permute-start(bf16[128,4096]{1,0:T(8,128)(2,1)S(1)} %advance.31.refs_4_.rest_3_), channel_id=1, source_target_pairs={{0,2},{2,4},{4,6},{6,8},{8,10},{10,12},{12,14},{14,16},{16,18},{18... | collective-permute-start | bytes 3145736 | tf_op jit(solution)/shard_map/ppermute | solution.py:28
  124.1 9.9 %collective-permute-start.24 = (bf16[128,1152]{1,0:T(8,128)(2,1)S(1)}, bf16[128,1152]{1,0:T(8,128)(2,1)S(1)}, u32[]{:S(2)}, u32[]{:S(2)}) collective-permute-start(bf16[128,1152]{1,0:T(8,128)(2,1)S(1)} %get-tuple-element.143.rest_3_), channel_id=1, source_target_pairs={{0,1},{1,0},{2,3},{3,2},{4,5},{5,4},{6,7},{7,6},{8,9},{9,8},{10,11... | collective-permute-start | bytes 884744 | tf_op jit(solution)/shard_map/ppermute | solution.py:28
  124.8 18.0 %collective-permute-start.23 = (bf16[128,1152]{1,0:T(8,128)(2,1)S(1)}, bf16[128,1152]{1,0:T(8,128)(2,1)S(1)}, u32[]{:S(2)}, u32[]{:S(2)}) collective-permute-start(bf16[128,1152]{1,0:T(8,128)(2,1)S(1)} %get-tuple-element.144.rest_3_), channel_id=1, source_target_pairs={{0,1},{1,0},{2,3},{3,2},{4,5},{5,4},{6,7},{7,6},{8,9},{9,8},{10,11... | collective-permute-start | bytes 884744 | tf_op jit(solution)/shard_map/ppermute | solution.py:28
  142.8 25.3 %collective-permute-start.31 = (bf16[128,4096]{1,0:T(8,128)(2,1)S(1)}, bf16[128,4096]{1,0:T(8,128)(2,1)S(1)}, u32[]{:S(2)}, u32[]{:S(2)}) collective-permute-start(bf16[128,4096]{1,0:T(8,128)(2,1)S(1)} %advance.32.rest_3_), channel_id=1, source_target_pairs={{0,2},{2,4},{4,6},{6,8},{8,10},{10,12},{12,14},{14,16},{16,18},{18... | collective-permute-start | bytes 3145736 | tf_op jit(solution)/shard_map/ppermute | solution.py:28
  151.7 25.7 %collective-permute-start.33 = (bf16[128,4096]{1,0:T(8,128)(2,1)S(1)}, bf16[128,4096]{1,0:T(8,128)(2,1)S(1)}, u32[]{:S(2)}, u32[]{:S(2)}) collective-permute-start(bf16[128,4096]{1,0:T(8,128)(2,1)S(1)} %advance.33.rest_3_), channel_id=1, source_target_pairs={{0,2},{2,4},{4,6},{6,8},{8,10},{10,12},{12,14},{14,16},{16,18},{18... | collective-permute-start | bytes 3145736 | tf_op jit(solution)/shard_map/ppermute | solution.py:28
  153.6 9.8 %collective-permute-start.28 = (bf16[128,1152]{1,0:T(8,128)(2,1)S(1)}, bf16[128,1152]{1,0:T(8,128)(2,1)S(1)}, u32[]{:S(2)}, u32[]{:S(2)}) collective-permute-start(bf16[128,1152]{1,0:T(8,128)(2,1)S(1)} %get-tuple-element.151.rest_3_), channel_id=1, source_target_pairs={{0,1},{1,0},{2,3},{3,2},{4,5},{5,4},{6,7},{7,6},{8,9},{9,8},{10,11... | collective-permute-start | bytes 884744 | tf_op jit(solution)/shard_map/ppermute | solution.py:28
  155.2 17.4 %collective-permute-start.27 = (bf16[128,1152]{1,0:T(8,128)(2,1)S(1)}, bf16[128,1152]{1,0:T(8,128)(2,1)S(1)}, u32[]{:S(2)}, u32[]{:S(2)}) collective-permute-start(bf16[128,1152]{1,0:T(8,128)(2,1)S(1)} %get-tuple-element.154.refs_4_.rest_3_), channel_id=1, source_target_pairs={{0,1},{1,0},{2,3},{3,2},{4,5},{5,4},{6,7},{7,6},{8,9},{9,8},{10,11... | collective-permute-start | bytes 884744 | tf_op jit(solution)/shard_map/ppermute | solution.py:28
  172.5 24.7 %collective-permute-start.38 = (bf16[128,4096]{1,0:T(8,128)(2,1)S(1)}, bf16[128,4096]{1,0:T(8,128)(2,1)S(1)}, u32[]{:S(2)}, u32[]{:S(2)}) collective-permute-start(bf16[128,4096]{1,0:T(8,128)(2,1)S(1)} %advance.34.rest_3_), channel_id=1, source_target_pairs={{0,2},{2,4},{4,6},{6,8},{8,10},{10,12},{12,14},{14,16},{16,18},{18... | collective-permute-start | bytes 3145736 | tf_op jit(solution)/shard_map/ppermute | solution.py:28
  181.4 24.6 %collective-permute-start.34 = (bf16[128,4096]{1,0:T(8,128)(2,1)S(1)}, bf16[128,4096]{1,0:T(8,128)(2,1)S(1)}, u32[]{:S(2)}, u32[]{:S(2)}) collective-permute-start(bf16[128,4096]{1,0:T(8,128)(2,1)S(1)} %advance.35.refs_4_.rest_3_), channel_id=1, source_target_pairs={{0,2},{2,4},{4,6},{6,8},{8,10},{10,12},{12,14},{14,16},{16,18},{18... | collective-permute-start | bytes 3145736 | tf_op jit(solution)/shard_map/ppermute | solution.py:28
  182.4 9.9 %collective-permute-start.36 = (bf16[128,1152]{1,0:T(8,128)(2,1)S(1)}, bf16[128,1152]{1,0:T(8,128)(2,1)S(1)}, u32[]{:S(2)}, u32[]{:S(2)}) collective-permute-start(bf16[128,1152]{1,0:T(8,128)(2,1)S(1)} %get-tuple-element.159.rest_3_), channel_id=1, source_target_pairs={{0,1},{1,0},{2,3},{3,2},{4,5},{5,4},{6,7},{7,6},{8,9},{9,8},{10,11... | collective-permute-start | bytes 884744 | tf_op jit(solution)/shard_map/ppermute | solution.py:28
  184.0 17.3 %collective-permute-start.35 = (bf16[128,1152]{1,0:T(8,128)(2,1)S(1)}, bf16[128,1152]{1,0:T(8,128)(2,1)S(1)}, u32[]{:S(2)}, u32[]{:S(2)}) collective-permute-start(bf16[128,1152]{1,0:T(8,128)(2,1)S(1)} %get-tuple-element.160.rest_3_), channel_id=1, source_target_pairs={{0,1},{1,0},{2,3},{3,2},{4,5},{5,4},{6,7},{7,6},{8,9},{9,8},{10,11... | collective-permute-start | bytes 884744 | tf_op jit(solution)/shard_map/ppermute | solution.py:28
  201.2 26.0 %collective-permute-start.43 = (bf16[128,4096]{1,0:T(8,128)(2,1)S(1)}, bf16[128,4096]{1,0:T(8,128)(2,1)S(1)}, u32[]{:S(2)}, u32[]{:S(2)}) collective-permute-start(bf16[128,4096]{1,0:T(8,128)(2,1)S(1)} %advance.36.rest_3_), channel_id=1, source_target_pairs={{0,2},{2,4},{4,6},{6,8},{8,10},{10,12},{12,14},{14,16},{16,18},{18... | collective-permute-start | bytes 3145736 | tf_op jit(solution)/shard_map/ppermute | solution.py:28
  210.1 26.2 %collective-permute-start.45 = (bf16[128,4096]{1,0:T(8,128)(2,1)S(1)}, bf16[128,4096]{1,0:T(8,128)(2,1)S(1)}, u32[]{:S(2)}, u32[]{:S(2)}) collective-permute-start(bf16[128,4096]{1,0:T(8,128)(2,1)S(1)} %advance.37.rest_3_), channel_id=1, source_target_pairs={{0,2},{2,4},{4,6},{6,8},{8,10},{10,12},{12,14},{14,16},{16,18},{18... | collective-permute-start | bytes 3145736 | tf_op jit(solution)/shard_map/ppermute | solution.py:28
  212.6 9.7 %collective-permute-start.40 = (bf16[128,1152]{1,0:T(8,128)(2,1)S(1)}, bf16[128,1152]{1,0:T(8,128)(2,1)S(1)}, u32[]{:S(2)}, u32[]{:S(2)}) collective-permute-start(bf16[128,1152]{1,0:T(8,128)(2,1)S(1)} %get-tuple-element.167.rest_3_), channel_id=1, source_target_pairs={{0,1},{1,0},{2,3},{3,2},{4,5},{5,4},{6,7},{7,6},{8,9},{9,8},{10,11... | collective-permute-start | bytes 884744 | tf_op jit(solution)/shard_map/ppermute | solution.py:28
  214.0 17.5 %collective-permute-start.39 = (bf16[128,1152]{1,0:T(8,128)(2,1)S(1)}, bf16[128,1152]{1,0:T(8,128)(2,1)S(1)}, u32[]{:S(2)}, u32[]{:S(2)}) collective-permute-start(bf16[128,1152]{1,0:T(8,128)(2,1)S(1)} %get-tuple-element.170.refs_4_.rest_3_), channel_id=1, source_target_pairs={{0,1},{1,0},{2,3},{3,2},{4,5},{5,4},{6,7},{7,6},{8,9},{9,8},{10,11... | collective-permute-start | bytes 884744 | tf_op jit(solution)/shard_map/ppermute | solution.py:28
  231.5 24.0 %collective-permute-start.50 = (bf16[128,4096]{1,0:T(8,128)(2,1)S(1)}, bf16[128,4096]{1,0:T(8,128)(2,1)S(1)}, u32[]{:S(2)}, u32[]{:S(2)}) collective-permute-start(bf16[128,4096]{1,0:T(8,128)(2,1)S(1)} %advance.38.rest_3_), channel_id=1, source_target_pairs={{0,2},{2,4},{4,6},{6,8},{8,10},{10,12},{12,14},{14,16},{16,18},{18... | collective-permute-start | bytes 3145736 | tf_op jit(solution)/shard_map/ppermute | solution.py:28
  240.4 24.9 %collective-permute-start.46 = (bf16[128,4096]{1,0:T(8,128)(2,1)S(1)}, bf16[128,4096]{1,0:T(8,128)(2,1)S(1)}, u32[]{:S(2)}, u32[]{:S(2)}) collective-permute-start(bf16[128,4096]{1,0:T(8,128)(2,1)S(1)} %advance.39.refs_4_.rest_3_), channel_id=1, source_target_pairs={{0,2},{2,4},{4,6},{6,8},{8,10},{10,12},{12,14},{14,16},{16,18},{18... | collective-permute-start | bytes 3145736 | tf_op jit(solution)/shard_map/ppermute | solution.py:28
  241.5 9.4 %collective-permute-start.48 = (bf16[128,1152]{1,0:T(8,128)(2,1)S(1)}, bf16[128,1152]{1,0:T(8,128)(2,1)S(1)}, u32[]{:S(2)}, u32[]{:S(2)}) collective-permute-start(bf16[128,1152]{1,0:T(8,128)(2,1)S(1)} %get-tuple-element.175.rest_3_), channel_id=1, source_target_pairs={{0,1},{1,0},{2,3},{3,2},{4,5},{5,4},{6,7},{7,6},{8,9},{9,8},{10,11... | collective-permute-start | bytes 884744 | tf_op jit(solution)/shard_map/ppermute | solution.py:28
  242.9 17.7 %collective-permute-start.47 = (bf16[128,1152]{1,0:T(8,128)(2,1)S(1)}, bf16[128,1152]{1,0:T(8,128)(2,1)S(1)}, u32[]{:S(2)}, u32[]{:S(2)}) collective-permute-start(bf16[128,1152]{1,0:T(8,128)(2,1)S(1)} %get-tuple-element.176.rest_3_), channel_id=1, source_target_pairs={{0,1},{1,0},{2,3},{3,2},{4,5},{5,4},{6,7},{7,6},{8,9},{9,8},{10,11... | collective-permute-start | bytes 884744 | tf_op jit(solution)/shard_map/ppermute | solution.py:28
  260.3 24.9 %collective-permute-start.55 = (bf16[128,4096]{1,0:T(8,128)(2,1)S(1)}, bf16[128,4096]{1,0:T(8,128)(2,1)S(1)}, u32[]{:S(2)}, u32[]{:S(2)}) collective-permute-start(bf16[128,4096]{1,0:T(8,128)(2,1)S(1)} %advance.40.rest_3_), channel_id=1, source_target_pairs={{0,2},{2,4},{4,6},{6,8},{8,10},{10,12},{12,14},{14,16},{16,18},{18... | collective-permute-start | bytes 3145736 | tf_op jit(solution)/shard_map/ppermute | solution.py:28
  269.9 24.5 %collective-permute-start.57 = (bf16[128,4096]{1,0:T(8,128)(2,1)S(1)}, bf16[128,4096]{1,0:T(8,128)(2,1)S(1)}, u32[]{:S(2)}, u32[]{:S(2)}) collective-permute-start(bf16[128,4096]{1,0:T(8,128)(2,1)S(1)} %advance.41.rest_3_), channel_id=1, source_target_pairs={{0,2},{2,4},{4,6},{6,8},{8,10},{10,12},{12,14},{14,16},{16,18},{18... | collective-permute-start | bytes 3145736 | tf_op jit(solution)/shard_map/ppermute | solution.py:28
  270.7 9.9 %collective-permute-start.52 = (bf16[128,1152]{1,0:T(8,128)(2,1)S(1)}, bf16[128,1152]{1,0:T(8,128)(2,1)S(1)}, u32[]{:S(2)}, u32[]{:S(2)}) collective-permute-start(bf16[128,1152]{1,0:T(8,128)(2,1)S(1)} %get-tuple-element.183.rest_3_), channel_id=1, source_target_pairs={{0,1},{1,0},{2,3},{3,2},{4,5},{5,4},{6,7},{7,6},{8,9},{9,8},{10,11... | collective-permute-start | bytes 884744 | tf_op jit(solution)/shard_map/ppermute | solution.py:28
  272.1 17.5 %collective-permute-start.51 = (bf16[128,1152]{1,0:T(8,128)(2,1)S(1)}, bf16[128,1152]{1,0:T(8,128)(2,1)S(1)}, u32[]{:S(2)}, u32[]{:S(2)}) collective-permute-start(bf16[128,1152]{1,0:T(8,128)(2,1)S(1)} %get-tuple-element.186.refs_4_.rest_3_), channel_id=1, source_target_pairs={{0,1},{1,0},{2,3},{3,2},{4,5},{5,4},{6,7},{7,6},{8,9},{9,8},{10,11... | collective-permute-start | bytes 884744 | tf_op jit(solution)/shard_map/ppermute | solution.py:28
  289.5 24.4 %collective-permute-start.62 = (bf16[128,4096]{1,0:T(8,128)(2,1)S(1)}, bf16[128,4096]{1,0:T(8,128)(2,1)S(1)}, u32[]{:S(2)}, u32[]{:S(2)}) collective-permute-start(bf16[128,4096]{1,0:T(8,128)(2,1)S(1)} %advance.42.rest_3_), channel_id=1, source_target_pairs={{0,2},{2,4},{4,6},{6,8},{8,10},{10,12},{12,14},{14,16},{16,18},{18... | collective-permute-start | bytes 3145736 | tf_op jit(solution)/shard_map/ppermute | solution.py:28
  298.8 24.3 %collective-permute-start.58 = (bf16[128,4096]{1,0:T(8,128)(2,1)S(1)}, bf16[128,4096]{1,0:T(8,128)(2,1)S(1)}, u32[]{:S(2)}, u32[]{:S(2)}) collective-permute-start(bf16[128,4096]{1,0:T(8,128)(2,1)S(1)} %advance.43.refs_4_.rest_3_), channel_id=1, source_target_pairs={{0,2},{2,4},{4,6},{6,8},{8,10},{10,12},{12,14},{14,16},{16,18},{18... | collective-permute-start | bytes 3145736 | tf_op jit(solution)/shard_map/ppermute | solution.py:28
  299.5 9.7 %collective-permute-start.60 = (bf16[128,1152]{1,0:T(8,128)(2,1)S(1)}, bf16[128,1152]{1,0:T(8,128)(2,1)S(1)}, u32[]{:S(2)}, u32[]{:S(2)}) collective-permute-start(bf16[128,1152]{1,0:T(8,128)(2,1)S(1)} %get-tuple-element.191.rest_3_), channel_id=1, source_target_pairs={{0,1},{1,0},{2,3},{3,2},{4,5},{5,4},{6,7},{7,6},{8,9},{9,8},{10,11... | collective-permute-start | bytes 884744 | tf_op jit(solution)/shard_map/ppermute | solution.py:28
  300.9 17.4 %collective-permute-start.59 = (bf16[128,1152]{1,0:T(8,128)(2,1)S(1)}, bf16[128,1152]{1,0:T(8,128)(2,1)S(1)}, u32[]{:S(2)}, u32[]{:S(2)}) collective-permute-start(bf16[128,1152]{1,0:T(8,128)(2,1)S(1)} %get-tuple-element.192.rest_3_), channel_id=1, source_target_pairs={{0,1},{1,0},{2,3},{3,2},{4,5},{5,4},{6,7},{7,6},{8,9},{9,8},{10,11... | collective-permute-start | bytes 884744 | tf_op jit(solution)/shard_map/ppermute | solution.py:28
  315.3 11.9 %collective-permute-start.64 = (bf16[128,1152]{1,0:T(8,128)(2,1)S(1)}, bf16[128,1152]{1,0:T(8,128)(2,1)S(1)}, u32[]{:S(2)}, u32[]{:S(2)}) collective-permute-start(bf16[128,1152]{1,0:T(8,128)(2,1)S(1)} %get-tuple-element.199.rest_3_), channel_id=1, source_target_pairs={{0,1},{1,0},{2,3},{3,2},{4,5},{5,4},{6,7},{7,6},{8,9},{9,8},{10,11... | collective-permute-start | bytes 884744 | tf_op jit(solution)/shard_map/ppermute | solution.py:28
  324.5 11.5 %collective-permute-start.63 = (bf16[128,1152]{1,0:T(8,128)(2,1)S(1)}, bf16[128,1152]{1,0:T(8,128)(2,1)S(1)}, u32[]{:S(2)}, u32[]{:S(2)}) collective-permute-start(bf16[128,1152]{1,0:T(8,128)(2,1)S(1)} %get-tuple-element.202.rest_3_), channel_id=1, source_target_pairs={{0,1},{1,0},{2,3},{3,2},{4,5},{5,4},{6,7},{7,6},{8,9},{9,8},{10,11... | collective-permute-start | bytes 884744 | tf_op jit(solution)/shard_map/ppermute | solution.py:28
  341.2 16.9 %collective-permute-start.71 = (bf16[128,4096]{1,0:T(8,128)(2,1)S(1)}, bf16[128,4096]{1,0:T(8,128)(2,1)S(1)}, u32[]{:S(2)}, u32[]{:S(2)}) collective-permute-start(bf16[128,4096]{1,0:T(8,128)(2,1)S(1)} %advance.44.rest_3_), channel_id=1, source_target_pairs={{0,2},{2,4},{4,6},{6,8},{8,10},{10,12},{12,14},{14,16},{16,18},{18... | collective-permute-start | bytes 3145736 | tf_op jit(solution)/shard_map/ppermute | solution.py:28
  341.2 28.2 %collective-permute-start.70 = (bf16[128,4096]{1,0:T(8,128)(2,1)S(1)}, bf16[128,4096]{1,0:T(8,128)(2,1)S(1)}, u32[]{:S(2)}, u32[]{:S(2)}) collective-permute-start(bf16[128,4096]{1,0:T(8,128)(2,1)S(1)} %advance.45.rest_3_), channel_id=1, source_target_pairs={{0,2},{2,4},{4,6},{6,8},{8,10},{10,12},{12,14},{14,16},{16,18},{18... | collective-permute-start | bytes 3145736 | tf_op jit(solution)/shard_map/ppermute | solution.py:28
  343.3 37.3 %collective-permute-start.69 = (bf16[128,4096]{1,0:T(8,128)(2,1)S(1)}, bf16[128,4096]{1,0:T(8,128)(2,1)S(1)}, u32[]{:S(2)}, u32[]{:S(2)}) collective-permute-start(bf16[128,4096]{1,0:T(8,128)(2,1)S(1)} %advance.46.rest_3_), channel_id=1, source_target_pairs={{0,2},{2,4},{4,6},{6,8},{8,10},{10,12},{12,14},{14,16},{16,18},{18... | collective-permute-start | bytes 3145736 | tf_op jit(solution)/shard_map/ppermute | solution.py:28
  345.0 46.8 %collective-permute-start.68 = (bf16[128,4096]{1,0:T(8,128)(2,1)S(1)}, bf16[128,4096]{1,0:T(8,128)(2,1)S(1)}, u32[]{:S(2)}, u32[]{:S(2)}) collective-permute-start(bf16[128,4096]{1,0:T(8,128)(2,1)S(1)} %advance.47), channel_id=1, source_target_pairs={{0,2},{2,4},{4,6},{6,8},{8,10},{10,12},{12,14},{14,16},{16,18},{18... | collective-permute-start | bytes 3145736 | tf_op jit(solution)/shard_map/ppermute | solution.py:28
  (25 other events, 111.3 us)

commit v4 on v3

--- a/solution.py
+++ b/solution.py
@@ -113,6 +113,75 @@
         cost_estimate=pl.CostEstimate(flops=0, transcendentals=0, bytes_accessed=0),
         name="refresh",
     )(table, *stacked, *resident, *after)
+
+
+def open_body(table_ref, stream_ref, down_src, router_src, *rest):
+    down_ref, router_ref, h_ref, own_ref, square_ref, sent_ref, semaphores = rest
+    rows, features = h_ref.shape
+    lap = table_ref[0]
+    extent = features // PIECES
+    copies = []
+    for piece in range(PIECES):
+        part = pl.ds(piece * extent, extent)
+        copies.append(
+            (
+                pltpu.make_async_copy(
+                    stream_ref.at[0, pl.ds(0, rows), part], h_ref.at[:, part], semaphores.at[0, piece]
+                ),
+                pltpu.make_async_copy(down_src.at[lap, 0, part], down_ref.at[part], semaphores.at[1, piece]),
+                pltpu.make_async_copy(router_src.at[lap, 0, part], router_ref.at[part], semaphores.at[2, piece]),
+            )
+        )
+    for group in copies:
+        for copy in group:
+            copy.start()
+    partial = jnp.zeros((rows, LANES), jnp.float32)
+    for piece, group in enumerate(copies):
+        for copy in group:
+            copy.wait()
+        span = slice(piece * extent, (piece + 1) * extent)
+        for at in range(span.start, span.stop, LANES):
+            wide = h_ref[:, at : at + LANES]
+            partial = partial + wide * wide
+        low = h_ref[:, span].astype(jnp.bfloat16)
+        start = 0
+        for weight_ref in (down_ref, router_ref):
+            columns = weight_ref.shape[1]
+            value = jnp.dot(low, weight_ref[span, :], preferred_element_type=jnp.float32)
+            if piece:
+                value = value + own_ref[:, start : start + columns]
+            own_ref[:, start : start + columns] = value
+            if piece == PIECES - 1:
+                sent_ref[:, start : start + columns] = value.astype(jnp.bfloat16)
+            start += columns
+    square = jnp.broadcast_to(jnp.sum(partial, axis=1, keepdims=True), (rows, LANES))
+    square_ref[...] = square
+    upper = square.astype(jnp.bfloat16).astype(jnp.float32)
+    lane = lax.broadcasted_iota(jnp.int32, (rows, LANES), 1)
+    sent_ref[:, start:] = jnp.where(lane < LANES // 2, upper, square - upper).astype(jnp.bfloat16)
+
+
+def open_up(table, stream, rows, stacked):
+    features = stream.shape[2]
+    total = sum(value.shape[3] for value in stacked)
+    return pl.pallas_call(
+        open_body,
+        in_specs=[IN_SMEM] + [IN_HBM] * 3,
+        out_specs=[IN_VMEM] * 6,
+        out_shape=[pltpu.VMEM(value.shape[2:], value.dtype) for value in stacked]
+        + [
+            pltpu.VMEM((rows, features), stream.dtype),
+            jax.ShapeDtypeStruct((rows, total), jnp.float32),
+            jax.ShapeDtypeStruct((rows, LANES), jnp.float32),
+            jax.ShapeDtypeStruct((rows, total + LANES), jnp.bfloat16),
+        ],
+        scratch_shapes=[pltpu.SemaphoreType.DMA((3, PIECES))],
+        compiler_params=params(),
+        cost_estimate=pl.CostEstimate(
+            flops=2 * rows * features * total, bytes_accessed=2 * features * total, transcendentals=0
+        ),
+        name="open_up",
+    )(table, stream, *stacked)
 
 
 def project_body(h_ref, down_ref, router_ref, *rest):
@@ -310,7 +379,7 @@
         rows = stream.shape[1] * share // sum(SHARES)
         blocks.append((start, rows))
         start += rows
-    *early, front = fetch(table, 0, stream, blocks[:1], stacked[:2], [])
+    *early, front, own, square, sent = open_up(table, stream, blocks[0][1], stacked[:2])
     *late, back = fetch(table, 0, stream, blocks[1:2], stacked[2:], [])
     held = [front, back]
 
@@ -327,7 +396,8 @@
         return [piece] + [from_behind(piece, "tensor", 1)] * (parts - 1)
 
     steps = TICKS * CHUNKS
-    projected = [exchange(*project(held[at], *early, [])) for at in range(LEAD)]
+    projected = [exchange(own, square, sent)]
+    projected += [exchange(*project(held[at], *early, [])) for at in range(1, LEAD)]
     piece = core(table, 0, *projected[0], expert, late[0], width, [])
     held += fetch(table, 0, stream, blocks[2:], [], [piece])
     for step in range(steps):

time: 401 us -> 401 us (level)
    pallas_call x0 -> x1, Pallas kernels: none -> 5.15 us  [open_up(): pl.pallas_call(open_body, in_specs=[IN_SMEM] + [IN_HBM] * 3, out_specs=[I...]
    pallas_call x3 -> x2, Pallas kernels: 13.2 us -> 8.55 us  [fetch(): pl.pallas_call(functools.partial(fetch_body, count, tick, blocks), in_spe...]
    pallas_call x24 -> x23, Pallas kernels: 32.4 us -> 31.1 us  [project(): pl.pallas_call(project_body, in_specs=[IN_VMEM] * 3 + [ANYWHERE] * len(af...]
where the time goes in v4:
time: 401 us; the launch traced here: 393 us
  Pallas kernels  164 us (41%)
  waiting for transfers between devices  158 us (39%)
  starting transfers between devices  70.1 us (17%)
    ppermute x72, waiting for transfers between devices, from_behind(): return lax.ppermute(value, axis, pairs)  158 us
    pallas_call x24, Pallas kernels, core(): pl.pallas_call(functools.partial(core_body, others, width, tick), in_spec...  76.8 us
    ppermute x72, starting transfers between devices, from_behind(): return lax.ppermute(value, axis, pairs)  70.1 us
    pallas_call x23, Pallas kernels, project(): pl.pallas_call(project_body, in_specs=[IN_VMEM] * 3 + [ANYWHERE] * len(af...  31.1 us
    pallas_call x24, Pallas kernels, advance(): pl.pallas_call(functools.partial(advance_body, pieces), in_specs=[IN_SMEM...  30.5 us
    pallas_call x2, Pallas kernels, fetch(): pl.pallas_call(functools.partial(fetch_body, count, tick, blocks), in_spe...  8.55 us
  transfers between devices with their start and end apart: 72, of which 38 were waited for; matrix products, arithmetic and copies ran while one was open for 0% of the time, Pallas kernels for 39%

profile of v4, /device:TPU:0, one launch (start us, length us, event | category | flops | bytes accessed | tf_op | source)
XLA Modules:
  0.0 392.8 jit_solution(12128131479401043403)
XLA Ops:
  0.0 5.2 %open_up.1 = (bf16[4096,512]{1,0:T(8,128)(2,1)S(1)}, bf16[4096,512]{1,0:T(8,128)(2,1)S(1)}, f32[128,4096]{1,0:T(8,128)S(1)}, f32[128,1024]{1,0:T(8,128)S(1)}, f3...) custom-call(s32[7]{0:T(128)S(1)} %compare_select_fusion.2.table_ref, f32[1,512,4096]{2,1,0:T(8,128)} %stream_ref.5, ...), custom_call_target="tpu_custom_call" | custom-call | flops 1073741824 | bytes 8388608 | tf_op jit(solution)/shard_map/open_up/pallas_call | solution.py:167
  5.2 3.1 collective-permute-start
  8.2 5.8 %fetch.2 = (bf16[256,32,512]{2,1,0:T(8,128)(2,1)S(1)}, bf16[512,4096]{1,0:T(8,128)(2,1)S(1)}, f32[128,4096]{1,0:T(8,128)S(1)}) custom-call(s32[7]{0:T(128)S(1)} %compare_select_fusion.2.table_ref, f32[1,512,4096]{2,1,0:T(8,128)} %stream_ref.5, bf16[2,1,256,32,512]{4,3,2,1,0:T(8,128)(2,1)} %refs_0_.21, bf16[2,1,512,4096]{3,2,1,0:T(8,128)(2,1)} %refs_1_.21), custom_call_target="tpu_custom_call" | custom-call | bytes 25165824 | tf_op jit(solution)/shard_map/fetch/pallas_call | solution.py:75
  15.4 3.2 core.24.refs_0_.rest_0_
  20.7 2.8 fetch.3
  26.6 3.2 core.25.rest_0_
  38.9 7.9 %collective-permute-done.4.rest_0_ = bf16[128,1152]{1,0:T(8,128)(2,1)S(1)} collective-permute-done((bf16[128,1152]{1,0:T(8,128)(2,1)S(1)}, bf16[128,1152]{1,0:T(8,128)(2,1)S(1)}, u32[]{:S(2)}, u32[]{:S(2)}) %collective-permute-start.4) | collective-permute-done | bytes 294944 | tf_op jit(solution)/shard_map/ppermute | solution.py:28
  46.7 3.2 core.26.rest_0_
  51.8 2.5 collective-permute-done.6.rest_1_
  55.7 3.2 core.27.rest_0_
  68.2 7.2 %collective-permute-done.12.rest_0_ = bf16[128,1152]{1,0:T(8,128)(2,1)S(1)} collective-permute-done((bf16[128,1152]{1,0:T(8,128)(2,1)S(1)}, bf16[128,1152]{1,0:T(8,128)(2,1)S(1)}, u32[]{:S(2)}, u32[]{:S(2)}) %collective-permute-start.12) | collective-permute-done | bytes 294944 | tf_op jit(solution)/shard_map/ppermute | solution.py:28
  75.4 3.2 core.28.rest_0_
  80.5 2.6 collective-permute-done.13.rest_1_
  84.5 3.2 core.29.rest_0_
  96.4 7.6 %collective-permute-done.16.rest_0_ = bf16[128,1152]{1,0:T(8,128)(2,1)S(1)} collective-permute-done((bf16[128,1152]{1,0:T(8,128)(2,1)S(1)}, bf16[128,1152]{1,0:T(8,128)(2,1)S(1)}, u32[]{:S(2)}, u32[]{:S(2)}) %collective-permute-start.16) | collective-permute-done | bytes 294944 | tf_op jit(solution)/shard_map/ppermute | solution.py:28
  104.0 3.2 core.30.rest_0_
  108.9 3.1 collective-permute-done.18.rest_1_
  113.3 3.2 core.31.rest_0_
  118.6 2.5 collective-permute-done.20.rest_1_
  125.9 7.2 %collective-permute-done.24.rest_0_ = bf16[128,1152]{1,0:T(8,128)(2,1)S(1)} collective-permute-done((bf16[128,1152]{1,0:T(8,128)(2,1)S(1)}, bf16[128,1152]{1,0:T(8,128)(2,1)S(1)}, u32[]{:S(2)}, u32[]{:S(2)}) %collective-permute-start.24) | collective-permute-done | bytes 294944 | tf_op jit(solution)/shard_map/ppermute | solution.py:28
  133.2 3.2 core.32.rest_0_
  142.0 3.2 core.33.rest_0_
  154.8 7.7 %collective-permute-done.28.rest_0_ = bf16[128,1152]{1,0:T(8,128)(2,1)S(1)} collective-permute-done((bf16[128,1152]{1,0:T(8,128)(2,1)S(1)}, bf16[128,1152]{1,0:T(8,128)(2,1)S(1)}, u32[]{:S(2)}, u32[]{:S(2)}) %collective-permute-start.28) | collective-permute-done | bytes 294944 | tf_op jit(solution)/shard_map/ppermute | solution.py:28
  162.5 3.2 core.34.rest_0_
  171.7 3.2 core.35.rest_0_
  184.2 7.2 %collective-permute-done.36.rest_0_ = bf16[128,1152]{1,0:T(8,128)(2,1)S(1)} collective-permute-done((bf16[128,1152]{1,0:T(8,128)(2,1)S(1)}, bf16[128,1152]{1,0:T(8,128)(2,1)S(1)}, u32[]{:S(2)}, u32[]{:S(2)}) %collective-permute-start.36) | collective-permute-done | bytes 294944 | tf_op jit(solution)/shard_map/ppermute | solution.py:28
  191.4 3.2 core.36.rest_0_
  200.4 3.2 core.37.rest_0_
  209.2 2.6 collective-permute-start.45
  213.8 7.6 %collective-permute-done.40.rest_0_ = bf16[128,1152]{1,0:T(8,128)(2,1)S(1)} collective-permute-done((bf16[128,1152]{1,0:T(8,128)(2,1)S(1)}, bf16[128,1152]{1,0:T(8,128)(2,1)S(1)}, u32[]{:S(2)}, u32[]{:S(2)}) %collective-permute-start.40) | collective-permute-done | bytes 294944 | tf_op jit(solution)/shard_map/ppermute | solution.py:28
  221.4 3.2 core.38.rest_0_
  230.7 3.2 core.39.rest_0_
  243.3 6.7 %collective-permute-done.48.rest_0_ = bf16[128,1152]{1,0:T(8,128)(2,1)S(1)} collective-permute-done((bf16[128,1152]{1,0:T(8,128)(2,1)S(1)}, bf16[128,1152]{1,0:T(8,128)(2,1)S(1)}, u32[]{:S(2)}, u32[]{:S(2)}) %collective-permute-start.48) | collective-permute-done | bytes 294944 | tf_op jit(solution)/shard_map/ppermute | solution.py:28
  250.1 3.2 core.40.rest_0_
  259.8 3.2 core.41.rest_0_
  271.9 7.9 %collective-permute-done.52.rest_0_ = bf16[128,1152]{1,0:T(8,128)(2,1)S(1)} collective-permute-done((bf16[128,1152]{1,0:T(8,128)(2,1)S(1)}, bf16[128,1152]{1,0:T(8,128)(2,1)S(1)}, u32[]{:S(2)}, u32[]{:S(2)}) %collective-permute-start.52) | collective-permute-done | bytes 294944 | tf_op jit(solution)/shard_map/ppermute | solution.py:28
  279.8 3.2 core.42.rest_0_
  288.8 3.2 core.43.rest_0_
  301.4 7.1 %collective-permute-done.60.rest_0_ = bf16[128,1152]{1,0:T(8,128)(2,1)S(1)} collective-permute-done((bf16[128,1152]{1,0:T(8,128)(2,1)S(1)}, bf16[128,1152]{1,0:T(8,128)(2,1)S(1)}, u32[]{:S(2)}, u32[]{:S(2)}) %collective-permute-start.60) | collective-permute-done | bytes 294944 | tf_op jit(solution)/shard_map/ppermute | solution.py:28
  308.5 3.2 core.44.rest_0_
  317.6 3.2 core.45.rest_0_
  326.4 3.2 core.46.rest_0_
  331.4 2.5 collective-permute-done.66.rest_1_
  335.2 3.4 core.47.rest_0_
  344.3 13.1 %collective-permute-done.71.refs_0_ = bf16[128,4096]{1,0:T(8,128)(2,1)S(1)} collective-permute-done((bf16[128,4096]{1,0:T(8,128)(2,1)S(1)}, bf16[128,4096]{1,0:T(8,128)(2,1)S(1)}, u32[]{:S(2)}, u32[]{:S(2)}) %collective-permute-start.71) | collective-permute-done | bytes 1048608 | tf_op jit(solution)/shard_map/ppermute | solution.py:28
  358.8 9.8 %collective-permute-done.70.refs_0_ = bf16[128,4096]{1,0:T(8,128)(2,1)S(1)} collective-permute-done((bf16[128,4096]{1,0:T(8,128)(2,1)S(1)}, bf16[128,4096]{1,0:T(8,128)(2,1)S(1)}, u32[]{:S(2)}, u32[]{:S(2)}) %collective-permute-start.70) | collective-permute-done | bytes 1048608 | tf_op jit(solution)/shard_map/ppermute | solution.py:28
  370.0 9.8 %collective-permute-done.69.refs_0_ = bf16[128,4096]{1,0:T(8,128)(2,1)S(1)} collective-permute-done((bf16[128,4096]{1,0:T(8,128)(2,1)S(1)}, bf16[128,4096]{1,0:T(8,128)(2,1)S(1)}, u32[]{:S(2)}, u32[]{:S(2)}) %collective-permute-start.69) | collective-permute-done | bytes 1048608 | tf_op jit(solution)/shard_map/ppermute | solution.py:28
  381.3 9.8 %collective-permute-done.68.refs_0_ = bf16[128,4096]{1,0:T(8,128)(2,1)S(1)} collective-permute-done((bf16[128,4096]{1,0:T(8,128)(2,1)S(1)}, bf16[128,4096]{1,0:T(8,128)(2,1)S(1)}, u32[]{:S(2)}, u32[]{:S(2)}) %collective-permute-start.68) | collective-permute-done | bytes 1048608 | tf_op jit(solution)/shard_map/ppermute | solution.py:28
  (187 shorter events, 165.6 us)
Async XLA Ops:
  5.2 10.2 %collective-permute-start = (bf16[128,1152]{1,0:T(8,128)(2,1)S(1)}, bf16[128,1152]{1,0:T(8,128)(2,1)S(1)}, u32[]{:S(2)}, u32[]{:S(2)}) collective-permute-start(bf16[128,1152]{1,0:T(8,128)(2,1)S(1)} %get-tuple-element.107), channel_id=1, source_target_pairs={{0,1},{1,0},{2,3},{3,2},{4,5},{5,4},{6,7},{7,6},{8,9},{9,8},{10,11... | collective-permute-start | bytes 884744 | tf_op jit(solution)/shard_map/ppermute | solution.py:28
  15.4 11.3 %collective-permute-start.1 = (bf16[128,1152]{1,0:T(8,128)(2,1)S(1)}, bf16[128,1152]{1,0:T(8,128)(2,1)S(1)}, u32[]{:S(2)}, u32[]{:S(2)}) collective-permute-start(bf16[128,1152]{1,0:T(8,128)(2,1)S(1)} %get-tuple-element.115), channel_id=1, source_target_pairs={{0,1},{1,0},{2,3},{3,2},{4,5},{5,4},{6,7},{7,6},{8,9},{9,8},{10,11... | collective-permute-start | bytes 884744 | tf_op jit(solution)/shard_map/ppermute | solution.py:28
  26.6 23.9 %collective-permute-start.7 = (bf16[128,4096]{1,0:T(8,128)(2,1)S(1)}, bf16[128,4096]{1,0:T(8,128)(2,1)S(1)}, u32[]{:S(2)}, u32[]{:S(2)}) collective-permute-start(bf16[128,4096]{1,0:T(8,128)(2,1)S(1)} %advance.24.rest_3_), channel_id=1, source_target_pairs={{0,2},{2,4},{4,6},{6,8},{8,10},{10,12},{12,14},{14,16},{16,18},{18... | collective-permute-start | bytes 3145736 | tf_op jit(solution)/shard_map/ppermute | solution.py:28
  35.5 23.9 %collective-permute-start.9 = (bf16[128,4096]{1,0:T(8,128)(2,1)S(1)}, bf16[128,4096]{1,0:T(8,128)(2,1)S(1)}, u32[]{:S(2)}, u32[]{:S(2)}) collective-permute-start(bf16[128,4096]{1,0:T(8,128)(2,1)S(1)} %advance.25.rest_3_), channel_id=1, source_target_pairs={{0,2},{2,4},{4,6},{6,8},{8,10},{10,12},{12,14},{14,16},{16,18},{18... | collective-permute-start | bytes 3145736 | tf_op jit(solution)/shard_map/ppermute | solution.py:28
  36.8 9.9 %collective-permute-start.4 = (bf16[128,1152]{1,0:T(8,128)(2,1)S(1)}, bf16[128,1152]{1,0:T(8,128)(2,1)S(1)}, u32[]{:S(2)}, u32[]{:S(2)}) collective-permute-start(bf16[128,1152]{1,0:T(8,128)(2,1)S(1)} %get-tuple-element.119.rest_3_), channel_id=1, source_target_pairs={{0,1},{1,0},{2,3},{3,2},{4,5},{5,4},{6,7},{7,6},{8,9},{9,8},{10,11... | collective-permute-start | bytes 884744 | tf_op jit(solution)/shard_map/ppermute | solution.py:28
  37.3 18.4 %collective-permute-start.3 = (bf16[128,1152]{1,0:T(8,128)(2,1)S(1)}, bf16[128,1152]{1,0:T(8,128)(2,1)S(1)}, u32[]{:S(2)}, u32[]{:S(2)}) collective-permute-start(bf16[128,1152]{1,0:T(8,128)(2,1)S(1)} %get-tuple-element.122.refs_4_.rest_3_), channel_id=1, source_target_pairs={{0,1},{1,0},{2,3},{3,2},{4,5},{5,4},{6,7},{7,6},{8,9},{9,8},{10,11... | collective-permute-start | bytes 884744 | tf_op jit(solution)/shard_map/ppermute | solution.py:28
  55.6 23.6 %collective-permute-start.14 = (bf16[128,4096]{1,0:T(8,128)(2,1)S(1)}, bf16[128,4096]{1,0:T(8,128)(2,1)S(1)}, u32[]{:S(2)}, u32[]{:S(2)}) collective-permute-start(bf16[128,4096]{1,0:T(8,128)(2,1)S(1)} %advance.26.rest_3_), channel_id=1, source_target_pairs={{0,2},{2,4},{4,6},{6,8},{8,10},{10,12},{12,14},{14,16},{16,18},{18... | collective-permute-start | bytes 3145736 | tf_op jit(solution)/shard_map/ppermute | solution.py:28
  64.5 23.8 %collective-permute-start.10 = (bf16[128,4096]{1,0:T(8,128)(2,1)S(1)}, bf16[128,4096]{1,0:T(8,128)(2,1)S(1)}, u32[]{:S(2)}, u32[]{:S(2)}) collective-permute-start(bf16[128,4096]{1,0:T(8,128)(2,1)S(1)} %advance.27.refs_4_.rest_3_), channel_id=1, source_target_pairs={{0,2},{2,4},{4,6},{6,8},{8,10},{10,12},{12,14},{14,16},{16,18},{18... | collective-permute-start | bytes 3145736 | tf_op jit(solution)/shard_map/ppermute | solution.py:28
  65.5 9.9 %collective-permute-start.12 = (bf16[128,1152]{1,0:T(8,128)(2,1)S(1)}, bf16[128,1152]{1,0:T(8,128)(2,1)S(1)}, u32[]{:S(2)}, u32[]{:S(2)}) collective-permute-start(bf16[128,1152]{1,0:T(8,128)(2,1)S(1)} %get-tuple-element.127.rest_3_), channel_id=1, source_target_pairs={{0,1},{1,0},{2,3},{3,2},{4,5},{5,4},{6,7},{7,6},{8,9},{9,8},{10,11... | collective-permute-start | bytes 884744 | tf_op jit(solution)/shard_map/ppermute | solution.py:28
  66.0 18.5 %collective-permute-start.11 = (bf16[128,1152]{1,0:T(8,128)(2,1)S(1)}, bf16[128,1152]{1,0:T(8,128)(2,1)S(1)}, u32[]{:S(2)}, u32[]{:S(2)}) collective-permute-start(bf16[128,1152]{1,0:T(8,128)(2,1)S(1)} %get-tuple-element.128.rest_3_), channel_id=1, source_target_pairs={{0,1},{1,0},{2,3},{3,2},{4,5},{5,4},{6,7},{7,6},{8,9},{9,8},{10,11... | collective-permute-start | bytes 884744 | tf_op jit(solution)/shard_map/ppermute | solution.py:28
  84.4 23.2 %collective-permute-start.19 = (bf16[128,4096]{1,0:T(8,128)(2,1)S(1)}, bf16[128,4096]{1,0:T(8,128)(2,1)S(1)}, u32[]{:S(2)}, u32[]{:S(2)}) collective-permute-start(bf16[128,4096]{1,0:T(8,128)(2,1)S(1)} %advance.28.rest_3_), channel_id=1, source_target_pairs={{0,2},{2,4},{4,6},{6,8},{8,10},{10,12},{12,14},{14,16},{16,18},{18... | collective-permute-start | bytes 3145736 | tf_op jit(solution)/shard_map/ppermute | solution.py:28
  93.3 24.0 %collective-permute-start.21 = (bf16[128,4096]{1,0:T(8,128)(2,1)S(1)}, bf16[128,4096]{1,0:T(8,128)(2,1)S(1)}, u32[]{:S(2)}, u32[]{:S(2)}) collective-permute-start(bf16[128,4096]{1,0:T(8,128)(2,1)S(1)} %advance.29.rest_3_), channel_id=1, source_target_pairs={{0,2},{2,4},{4,6},{6,8},{8,10},{10,12},{12,14},{14,16},{16,18},{18... | collective-permute-start | bytes 3145736 | tf_op jit(solution)/shard_map/ppermute | solution.py:28
  94.4 9.7 %collective-permute-start.16 = (bf16[128,1152]{1,0:T(8,128)(2,1)S(1)}, bf16[128,1152]{1,0:T(8,128)(2,1)S(1)}, u32[]{:S(2)}, u32[]{:S(2)}) collective-permute-start(bf16[128,1152]{1,0:T(8,128)(2,1)S(1)} %get-tuple-element.135.rest_3_), channel_id=1, source_target_pairs={{0,1},{1,0},{2,3},{3,2},{4,5},{5,4},{6,7},{7,6},{8,9},{9,8},{10,11... | collective-permute-start | bytes 884744 | tf_op jit(solution)/shard_map/ppermute | solution.py:28
  94.9 18.5 %collective-permute-start.15 = (bf16[128,1152]{1,0:T(8,128)(2,1)S(1)}, bf16[128,1152]{1,0:T(8,128)(2,1)S(1)}, u32[]{:S(2)}, u32[]{:S(2)}) collective-permute-start(bf16[128,1152]{1,0:T(8,128)(2,1)S(1)} %get-tuple-element.138.refs_4_.rest_3_), channel_id=1, source_target_pairs={{0,1},{1,0},{2,3},{3,2},{4,5},{5,4},{6,7},{7,6},{8,9},{9,8},{10,11... | collective-permute-start | bytes 884744 | tf_op jit(solution)/shard_map/ppermute | solution.py:28
  113.3 23.8 %collective-permute-start.26 = (bf16[128,4096]{1,0:T(8,128)(2,1)S(1)}, bf16[128,4096]{1,0:T(8,128)(2,1)S(1)}, u32[]{:S(2)}, u32[]{:S(2)}) collective-permute-start(bf16[128,4096]{1,0:T(8,128)(2,1)S(1)} %advance.30.rest_3_), channel_id=1, source_target_pairs={{0,2},{2,4},{4,6},{6,8},{8,10},{10,12},{12,14},{14,16},{16,18},{18... | collective-permute-start | bytes 3145736 | tf_op jit(solution)/shard_map/ppermute | solution.py:28
  122.4 23.6 %collective-permute-start.22 = (bf16[128,4096]{1,0:T(8,128)(2,1)S(1)}, bf16[128,4096]{1,0:T(8,128)(2,1)S(1)}, u32[]{:S(2)}, u32[]{:S(2)}) collective-permute-start(bf16[128,4096]{1,0:T(8,128)(2,1)S(1)} %advance.31.refs_4_.rest_3_), channel_id=1, source_target_pairs={{0,2},{2,4},{4,6},{6,8},{8,10},{10,12},{12,14},{14,16},{16,18},{18... | collective-permute-start | bytes 3145736 | tf_op jit(solution)/shard_map/ppermute | solution.py:28
  123.3 9.9 %collective-permute-start.24 = (bf16[128,1152]{1,0:T(8,128)(2,1)S(1)}, bf16[128,1152]{1,0:T(8,128)(2,1)S(1)}, u32[]{:S(2)}, u32[]{:S(2)}) collective-permute-start(bf16[128,1152]{1,0:T(8,128)(2,1)S(1)} %get-tuple-element.143.rest_3_), channel_id=1, source_target_pairs={{0,1},{1,0},{2,3},{3,2},{4,5},{5,4},{6,7},{7,6},{8,9},{9,8},{10,11... | collective-permute-start | bytes 884744 | tf_op jit(solution)/shard_map/ppermute | solution.py:28
  123.9 18.1 %collective-permute-start.23 = (bf16[128,1152]{1,0:T(8,128)(2,1)S(1)}, bf16[128,1152]{1,0:T(8,128)(2,1)S(1)}, u32[]{:S(2)}, u32[]{:S(2)}) collective-permute-start(bf16[128,1152]{1,0:T(8,128)(2,1)S(1)} %get-tuple-element.144.rest_3_), channel_id=1, source_target_pairs={{0,1},{1,0},{2,3},{3,2},{4,5},{5,4},{6,7},{7,6},{8,9},{9,8},{10,11... | collective-permute-start | bytes 884744 | tf_op jit(solution)/shard_map/ppermute | solution.py:28
  142.0 25.3 %collective-permute-start.31 = (bf16[128,4096]{1,0:T(8,128)(2,1)S(1)}, bf16[128,4096]{1,0:T(8,128)(2,1)S(1)}, u32[]{:S(2)}, u32[]{:S(2)}) collective-permute-start(bf16[128,4096]{1,0:T(8,128)(2,1)S(1)} %advance.32.rest_3_), channel_id=1, source_target_pairs={{0,2},{2,4},{4,6},{6,8},{8,10},{10,12},{12,14},{14,16},{16,18},{18... | collective-permute-start | bytes 3145736 | tf_op jit(solution)/shard_map/ppermute | solution.py:28
  150.9 25.8 %collective-permute-start.33 = (bf16[128,4096]{1,0:T(8,128)(2,1)S(1)}, bf16[128,4096]{1,0:T(8,128)(2,1)S(1)}, u32[]{:S(2)}, u32[]{:S(2)}) collective-permute-start(bf16[128,4096]{1,0:T(8,128)(2,1)S(1)} %advance.33.rest_3_), channel_id=1, source_target_pairs={{0,2},{2,4},{4,6},{6,8},{8,10},{10,12},{12,14},{14,16},{16,18},{18... | collective-permute-start | bytes 3145736 | tf_op jit(solution)/shard_map/ppermute | solution.py:28
  152.7 9.8 %collective-permute-start.28 = (bf16[128,1152]{1,0:T(8,128)(2,1)S(1)}, bf16[128,1152]{1,0:T(8,128)(2,1)S(1)}, u32[]{:S(2)}, u32[]{:S(2)}) collective-permute-start(bf16[128,1152]{1,0:T(8,128)(2,1)S(1)} %get-tuple-element.151.rest_3_), channel_id=1, source_target_pairs={{0,1},{1,0},{2,3},{3,2},{4,5},{5,4},{6,7},{7,6},{8,9},{9,8},{10,11... | collective-permute-start | bytes 884744 | tf_op jit(solution)/shard_map/ppermute | solution.py:28
  154.4 17.3 %collective-permute-start.27 = (bf16[128,1152]{1,0:T(8,128)(2,1)S(1)}, bf16[128,1152]{1,0:T(8,128)(2,1)S(1)}, u32[]{:S(2)}, u32[]{:S(2)}) collective-permute-start(bf16[128,1152]{1,0:T(8,128)(2,1)S(1)} %get-tuple-element.154.refs_4_.rest_3_), channel_id=1, source_target_pairs={{0,1},{1,0},{2,3},{3,2},{4,5},{5,4},{6,7},{7,6},{8,9},{9,8},{10,11... | collective-permute-start | bytes 884744 | tf_op jit(solution)/shard_map/ppermute | solution.py:28
  171.6 24.7 %collective-permute-start.38 = (bf16[128,4096]{1,0:T(8,128)(2,1)S(1)}, bf16[128,4096]{1,0:T(8,128)(2,1)S(1)}, u32[]{:S(2)}, u32[]{:S(2)}) collective-permute-start(bf16[128,4096]{1,0:T(8,128)(2,1)S(1)} %advance.34.rest_3_), channel_id=1, source_target_pairs={{0,2},{2,4},{4,6},{6,8},{8,10},{10,12},{12,14},{14,16},{16,18},{18... | collective-permute-start | bytes 3145736 | tf_op jit(solution)/shard_map/ppermute | solution.py:28
  180.6 24.7 %collective-permute-start.34 = (bf16[128,4096]{1,0:T(8,128)(2,1)S(1)}, bf16[128,4096]{1,0:T(8,128)(2,1)S(1)}, u32[]{:S(2)}, u32[]{:S(2)}) collective-permute-start(bf16[128,4096]{1,0:T(8,128)(2,1)S(1)} %advance.35.refs_4_.rest_3_), channel_id=1, source_target_pairs={{0,2},{2,4},{4,6},{6,8},{8,10},{10,12},{12,14},{14,16},{16,18},{18... | collective-permute-start | bytes 3145736 | tf_op jit(solution)/shard_map/ppermute | solution.py:28
  181.6 9.9 %collective-permute-start.36 = (bf16[128,1152]{1,0:T(8,128)(2,1)S(1)}, bf16[128,1152]{1,0:T(8,128)(2,1)S(1)}, u32[]{:S(2)}, u32[]{:S(2)}) collective-permute-start(bf16[128,1152]{1,0:T(8,128)(2,1)S(1)} %get-tuple-element.159.rest_3_), channel_id=1, source_target_pairs={{0,1},{1,0},{2,3},{3,2},{4,5},{5,4},{6,7},{7,6},{8,9},{9,8},{10,11... | collective-permute-start | bytes 884744 | tf_op jit(solution)/shard_map/ppermute | solution.py:28
  183.2 17.1 %collective-permute-start.35 = (bf16[128,1152]{1,0:T(8,128)(2,1)S(1)}, bf16[128,1152]{1,0:T(8,128)(2,1)S(1)}, u32[]{:S(2)}, u32[]{:S(2)}) collective-permute-start(bf16[128,1152]{1,0:T(8,128)(2,1)S(1)} %get-tuple-element.160.rest_3_), channel_id=1, source_target_pairs={{0,1},{1,0},{2,3},{3,2},{4,5},{5,4},{6,7},{7,6},{8,9},{9,8},{10,11... | collective-permute-start | bytes 884744 | tf_op jit(solution)/shard_map/ppermute | solution.py:28
  200.3 26.0 %collective-permute-start.43 = (bf16[128,4096]{1,0:T(8,128)(2,1)S(1)}, bf16[128,4096]{1,0:T(8,128)(2,1)S(1)}, u32[]{:S(2)}, u32[]{:S(2)}) collective-permute-start(bf16[128,4096]{1,0:T(8,128)(2,1)S(1)} %advance.36.rest_3_), channel_id=1, source_target_pairs={{0,2},{2,4},{4,6},{6,8},{8,10},{10,12},{12,14},{14,16},{16,18},{18... | collective-permute-start | bytes 3145736 | tf_op jit(solution)/shard_map/ppermute | solution.py:28
  209.2 26.4 %collective-permute-start.45 = (bf16[128,4096]{1,0:T(8,128)(2,1)S(1)}, bf16[128,4096]{1,0:T(8,128)(2,1)S(1)}, u32[]{:S(2)}, u32[]{:S(2)}) collective-permute-start(bf16[128,4096]{1,0:T(8,128)(2,1)S(1)} %advance.37.rest_3_), channel_id=1, source_target_pairs={{0,2},{2,4},{4,6},{6,8},{8,10},{10,12},{12,14},{14,16},{16,18},{18... | collective-permute-start | bytes 3145736 | tf_op jit(solution)/shard_map/ppermute | solution.py:28
  211.8 9.6 %collective-permute-start.40 = (bf16[128,1152]{1,0:T(8,128)(2,1)S(1)}, bf16[128,1152]{1,0:T(8,128)(2,1)S(1)}, u32[]{:S(2)}, u32[]{:S(2)}) collective-permute-start(bf16[128,1152]{1,0:T(8,128)(2,1)S(1)} %get-tuple-element.167.rest_3_), channel_id=1, source_target_pairs={{0,1},{1,0},{2,3},{3,2},{4,5},{5,4},{6,7},{7,6},{8,9},{9,8},{10,11... | collective-permute-start | bytes 884744 | tf_op jit(solution)/shard_map/ppermute | solution.py:28
  213.3 17.4 %collective-permute-start.39 = (bf16[128,1152]{1,0:T(8,128)(2,1)S(1)}, bf16[128,1152]{1,0:T(8,128)(2,1)S(1)}, u32[]{:S(2)}, u32[]{:S(2)}) collective-permute-start(bf16[128,1152]{1,0:T(8,128)(2,1)S(1)} %get-tuple-element.170.refs_4_.rest_3_), channel_id=1, source_target_pairs={{0,1},{1,0},{2,3},{3,2},{4,5},{5,4},{6,7},{7,6},{8,9},{9,8},{10,11... | collective-permute-start | bytes 884744 | tf_op jit(solution)/shard_map/ppermute | solution.py:28
  230.7 24.2 %collective-permute-start.50 = (bf16[128,4096]{1,0:T(8,128)(2,1)S(1)}, bf16[128,4096]{1,0:T(8,128)(2,1)S(1)}, u32[]{:S(2)}, u32[]{:S(2)}) collective-permute-start(bf16[128,4096]{1,0:T(8,128)(2,1)S(1)} %advance.38.rest_3_), channel_id=1, source_target_pairs={{0,2},{2,4},{4,6},{6,8},{8,10},{10,12},{12,14},{14,16},{16,18},{18... | collective-permute-start | bytes 3145736 | tf_op jit(solution)/shard_map/ppermute | solution.py:28
  239.6 25.0 %collective-permute-start.46 = (bf16[128,4096]{1,0:T(8,128)(2,1)S(1)}, bf16[128,4096]{1,0:T(8,128)(2,1)S(1)}, u32[]{:S(2)}, u32[]{:S(2)}) collective-permute-start(bf16[128,4096]{1,0:T(8,128)(2,1)S(1)} %advance.39.refs_4_.rest_3_), channel_id=1, source_target_pairs={{0,2},{2,4},{4,6},{6,8},{8,10},{10,12},{12,14},{14,16},{16,18},{18... | collective-permute-start | bytes 3145736 | tf_op jit(solution)/shard_map/ppermute | solution.py:28
  240.7 9.4 %collective-permute-start.48 = (bf16[128,1152]{1,0:T(8,128)(2,1)S(1)}, bf16[128,1152]{1,0:T(8,128)(2,1)S(1)}, u32[]{:S(2)}, u32[]{:S(2)}) collective-permute-start(bf16[128,1152]{1,0:T(8,128)(2,1)S(1)} %get-tuple-element.175.rest_3_), channel_id=1, source_target_pairs={{0,1},{1,0},{2,3},{3,2},{4,5},{5,4},{6,7},{7,6},{8,9},{9,8},{10,11... | collective-permute-start | bytes 884744 | tf_op jit(solution)/shard_map/ppermute | solution.py:28
  242.2 17.6 %collective-permute-start.47 = (bf16[128,1152]{1,0:T(8,128)(2,1)S(1)}, bf16[128,1152]{1,0:T(8,128)(2,1)S(1)}, u32[]{:S(2)}, u32[]{:S(2)}) collective-permute-start(bf16[128,1152]{1,0:T(8,128)(2,1)S(1)} %get-tuple-element.176.rest_3_), channel_id=1, source_target_pairs={{0,1},{1,0},{2,3},{3,2},{4,5},{5,4},{6,7},{7,6},{8,9},{9,8},{10,11... | collective-permute-start | bytes 884744 | tf_op jit(solution)/shard_map/ppermute | solution.py:28
  259.5 25.1 %collective-permute-start.55 = (bf16[128,4096]{1,0:T(8,128)(2,1)S(1)}, bf16[128,4096]{1,0:T(8,128)(2,1)S(1)}, u32[]{:S(2)}, u32[]{:S(2)}) collective-permute-start(bf16[128,4096]{1,0:T(8,128)(2,1)S(1)} %advance.40.rest_3_), channel_id=1, source_target_pairs={{0,2},{2,4},{4,6},{6,8},{8,10},{10,12},{12,14},{14,16},{16,18},{18... | collective-permute-start | bytes 3145736 | tf_op jit(solution)/shard_map/ppermute | solution.py:28
  269.1 24.5 %collective-permute-start.57 = (bf16[128,4096]{1,0:T(8,128)(2,1)S(1)}, bf16[128,4096]{1,0:T(8,128)(2,1)S(1)}, u32[]{:S(2)}, u32[]{:S(2)}) collective-permute-start(bf16[128,4096]{1,0:T(8,128)(2,1)S(1)} %advance.41.rest_3_), channel_id=1, source_target_pairs={{0,2},{2,4},{4,6},{6,8},{8,10},{10,12},{12,14},{14,16},{16,18},{18... | collective-permute-start | bytes 3145736 | tf_op jit(solution)/shard_map/ppermute | solution.py:28
  269.9 9.9 %collective-permute-start.52 = (bf16[128,1152]{1,0:T(8,128)(2,1)S(1)}, bf16[128,1152]{1,0:T(8,128)(2,1)S(1)}, u32[]{:S(2)}, u32[]{:S(2)}) collective-permute-start(bf16[128,1152]{1,0:T(8,128)(2,1)S(1)} %get-tuple-element.183.rest_3_), channel_id=1, source_target_pairs={{0,1},{1,0},{2,3},{3,2},{4,5},{5,4},{6,7},{7,6},{8,9},{9,8},{10,11... | collective-permute-start | bytes 884744 | tf_op jit(solution)/shard_map/ppermute | solution.py:28
  271.4 17.4 %collective-permute-start.51 = (bf16[128,1152]{1,0:T(8,128)(2,1)S(1)}, bf16[128,1152]{1,0:T(8,128)(2,1)S(1)}, u32[]{:S(2)}, u32[]{:S(2)}) collective-permute-start(bf16[128,1152]{1,0:T(8,128)(2,1)S(1)} %get-tuple-element.186.refs_4_.rest_3_), channel_id=1, source_target_pairs={{0,1},{1,0},{2,3},{3,2},{4,5},{5,4},{6,7},{7,6},{8,9},{9,8},{10,11... | collective-permute-start | bytes 884744 | tf_op jit(solution)/shard_map/ppermute | solution.py:28
  288.8 24.5 %collective-permute-start.62 = (bf16[128,4096]{1,0:T(8,128)(2,1)S(1)}, bf16[128,4096]{1,0:T(8,128)(2,1)S(1)}, u32[]{:S(2)}, u32[]{:S(2)}) collective-permute-start(bf16[128,4096]{1,0:T(8,128)(2,1)S(1)} %advance.42.rest_3_), channel_id=1, source_target_pairs={{0,2},{2,4},{4,6},{6,8},{8,10},{10,12},{12,14},{14,16},{16,18},{18... | collective-permute-start | bytes 3145736 | tf_op jit(solution)/shard_map/ppermute | solution.py:28
  298.1 24.2 %collective-permute-start.58 = (bf16[128,4096]{1,0:T(8,128)(2,1)S(1)}, bf16[128,4096]{1,0:T(8,128)(2,1)S(1)}, u32[]{:S(2)}, u32[]{:S(2)}) collective-permute-start(bf16[128,4096]{1,0:T(8,128)(2,1)S(1)} %advance.43.refs_4_.rest_3_), channel_id=1, source_target_pairs={{0,2},{2,4},{4,6},{6,8},{8,10},{10,12},{12,14},{14,16},{16,18},{18... | collective-permute-start | bytes 3145736 | tf_op jit(solution)/shard_map/ppermute | solution.py:28
  298.7 9.8 %collective-permute-start.60 = (bf16[128,1152]{1,0:T(8,128)(2,1)S(1)}, bf16[128,1152]{1,0:T(8,128)(2,1)S(1)}, u32[]{:S(2)}, u32[]{:S(2)}) collective-permute-start(bf16[128,1152]{1,0:T(8,128)(2,1)S(1)} %get-tuple-element.191.rest_3_), channel_id=1, source_target_pairs={{0,1},{1,0},{2,3},{3,2},{4,5},{5,4},{6,7},{7,6},{8,9},{9,8},{10,11... | collective-permute-start | bytes 884744 | tf_op jit(solution)/shard_map/ppermute | solution.py:28
  300.2 17.4 %collective-permute-start.59 = (bf16[128,1152]{1,0:T(8,128)(2,1)S(1)}, bf16[128,1152]{1,0:T(8,128)(2,1)S(1)}, u32[]{:S(2)}, u32[]{:S(2)}) collective-permute-start(bf16[128,1152]{1,0:T(8,128)(2,1)S(1)} %get-tuple-element.192.rest_3_), channel_id=1, source_target_pairs={{0,1},{1,0},{2,3},{3,2},{4,5},{5,4},{6,7},{7,6},{8,9},{9,8},{10,11... | collective-permute-start | bytes 884744 | tf_op jit(solution)/shard_map/ppermute | solution.py:28
  314.6 11.8 %collective-permute-start.64 = (bf16[128,1152]{1,0:T(8,128)(2,1)S(1)}, bf16[128,1152]{1,0:T(8,128)(2,1)S(1)}, u32[]{:S(2)}, u32[]{:S(2)}) collective-permute-start(bf16[128,1152]{1,0:T(8,128)(2,1)S(1)} %get-tuple-element.199.rest_3_), channel_id=1, source_target_pairs={{0,1},{1,0},{2,3},{3,2},{4,5},{5,4},{6,7},{7,6},{8,9},{9,8},{10,11... | collective-permute-start | bytes 884744 | tf_op jit(solution)/shard_map/ppermute | solution.py:28
  323.7 11.5 %collective-permute-start.63 = (bf16[128,1152]{1,0:T(8,128)(2,1)S(1)}, bf16[128,1152]{1,0:T(8,128)(2,1)S(1)}, u32[]{:S(2)}, u32[]{:S(2)}) collective-permute-start(bf16[128,1152]{1,0:T(8,128)(2,1)S(1)} %get-tuple-element.202.rest_3_), channel_id=1, source_target_pairs={{0,1},{1,0},{2,3},{3,2},{4,5},{5,4},{6,7},{7,6},{8,9},{9,8},{10,11... | collective-permute-start | bytes 884744 | tf_op jit(solution)/shard_map/ppermute | solution.py:28
  340.5 16.9 %collective-permute-start.71 = (bf16[128,4096]{1,0:T(8,128)(2,1)S(1)}, bf16[128,4096]{1,0:T(8,128)(2,1)S(1)}, u32[]{:S(2)}, u32[]{:S(2)}) collective-permute-start(bf16[128,4096]{1,0:T(8,128)(2,1)S(1)} %advance.44.rest_3_), channel_id=1, source_target_pairs={{0,2},{2,4},{4,6},{6,8},{8,10},{10,12},{12,14},{14,16},{16,18},{18... | collective-permute-start | bytes 3145736 | tf_op jit(solution)/shard_map/ppermute | solution.py:28
  340.5 28.2 %collective-permute-start.70 = (bf16[128,4096]{1,0:T(8,128)(2,1)S(1)}, bf16[128,4096]{1,0:T(8,128)(2,1)S(1)}, u32[]{:S(2)}, u32[]{:S(2)}) collective-permute-start(bf16[128,4096]{1,0:T(8,128)(2,1)S(1)} %advance.45.rest_3_), channel_id=1, source_target_pairs={{0,2},{2,4},{4,6},{6,8},{8,10},{10,12},{12,14},{14,16},{16,18},{18... | collective-permute-start | bytes 3145736 | tf_op jit(solution)/shard_map/ppermute | solution.py:28
  342.6 37.3 %collective-permute-start.69 = (bf16[128,4096]{1,0:T(8,128)(2,1)S(1)}, bf16[128,4096]{1,0:T(8,128)(2,1)S(1)}, u32[]{:S(2)}, u32[]{:S(2)}) collective-permute-start(bf16[128,4096]{1,0:T(8,128)(2,1)S(1)} %advance.46.rest_3_), channel_id=1, source_target_pairs={{0,2},{2,4},{4,6},{6,8},{8,10},{10,12},{12,14},{14,16},{16,18},{18... | collective-permute-start | bytes 3145736 | tf_op jit(solution)/shard_map/ppermute | solution.py:28
  344.3 46.9 %collective-permute-start.68 = (bf16[128,4096]{1,0:T(8,128)(2,1)S(1)}, bf16[128,4096]{1,0:T(8,128)(2,1)S(1)}, u32[]{:S(2)}, u32[]{:S(2)}) collective-permute-start(bf16[128,4096]{1,0:T(8,128)(2,1)S(1)} %advance.47), channel_id=1, source_target_pairs={{0,2},{2,4},{4,6},{6,8},{8,10},{10,12},{12,14},{14,16},{16,18},{18... | collective-permute-start | bytes 3145736 | tf_op jit(solution)/shard_map/ppermute | solution.py:28
  (25 other events, 111.5 us)

commit v5 on v4

--- a/solution.py
+++ b/solution.py
@@ -119,9 +119,10 @@
     down_ref, router_ref, h_ref, own_ref, square_ref, sent_ref, semaphores = rest
     rows, features = h_ref.shape
     lap = table_ref[0]
-    extent = features // PIECES
+    pieces = semaphores.shape[1]
+    extent = features // pieces
     copies = []
-    for piece in range(PIECES):
+    for piece in range(pieces):
         part = pl.ds(piece * extent, extent)
         copies.append(
             (
@@ -151,7 +152,7 @@
             if piece:
                 value = value + own_ref[:, start : start + columns]
             own_ref[:, start : start + columns] = value
-            if piece == PIECES - 1:
+            if piece == pieces - 1:
                 sent_ref[:, start : start + columns] = value.astype(jnp.bfloat16)
             start += columns
     square = jnp.broadcast_to(jnp.sum(partial, axis=1, keepdims=True), (rows, LANES))
@@ -175,7 +176,7 @@
             jax.ShapeDtypeStruct((rows, LANES), jnp.float32),
             jax.ShapeDtypeStruct((rows, total + LANES), jnp.bfloat16),
         ],
-        scratch_shapes=[pltpu.SemaphoreType.DMA((3, PIECES))],
+        scratch_shapes=[pltpu.SemaphoreType.DMA((3, min(2 * PIECES, features // LANES)))],
         compiler_params=params(),
         cost_estimate=pl.CostEstimate(
             flops=2 * rows * features * total, bytes_accessed=2 * features * total, transcendentals=0

time: 401 us -> 401 us (level)
  no operation moved by 1% of the time
where the time goes in v5:
time: 401 us; the launch traced here: 393 us
  Pallas kernels  164 us (41%)
  waiting for transfers between devices  157 us (39%)
  starting transfers between devices  70.6 us (18%)
    ppermute x72, waiting for transfers between devices, from_behind(): return lax.ppermute(value, axis, pairs)  157 us
    pallas_call x24, Pallas kernels, core(): pl.pallas_call(functools.partial(core_body, others, width, tick), in_spec...  76.8 us
    ppermute x72, starting transfers between devices, from_behind(): return lax.ppermute(value, axis, pairs)  70.6 us
    pallas_call x23, Pallas kernels, project(): pl.pallas_call(project_body, in_specs=[IN_VMEM] * 3 + [ANYWHERE] * len(af...  31 us
    pallas_call x24, Pallas kernels, advance(): pl.pallas_call(functools.partial(advance_body, pieces), in_specs=[IN_SMEM...  30.6 us
    pallas_call x2, Pallas kernels, fetch(): pl.pallas_call(functools.partial(fetch_body, count, tick, blocks), in_spe...  8.55 us
  transfers between devices with their start and end apart: 72, of which 38 were waited for; matrix products, arithmetic and copies ran while one was open for 0% of the time, Pallas kernels for 39%

profile of v5, /device:TPU:0, one launch (start us, length us, event | category | flops | bytes accessed | tf_op | source)
XLA Modules:
  0.0 392.7 jit_solution(17650164603829882434)
XLA Ops:
  0.0 5.1 %open_up.1 = (bf16[4096,512]{1,0:T(8,128)(2,1)S(1)}, bf16[4096,512]{1,0:T(8,128)(2,1)S(1)}, f32[128,4096]{1,0:T(8,128)S(1)}, f32[128,1024]{1,0:T(8,128)S(1)}, f3...) custom-call(s32[7]{0:T(128)S(1)} %compare_select_fusion.2.table_ref, f32[1,512,4096]{2,1,0:T(8,128)} %stream_ref.5, ...), custom_call_target="tpu_custom_call" | custom-call | flops 1073741824 | bytes 8388608 | tf_op jit(solution)/shard_map/open_up/pallas_call | solution.py:168
  5.1 3.1 collective-permute-start
  8.2 5.8 %fetch.2 = (bf16[256,32,512]{2,1,0:T(8,128)(2,1)S(1)}, bf16[512,4096]{1,0:T(8,128)(2,1)S(1)}, f32[128,4096]{1,0:T(8,128)S(1)}) custom-call(s32[7]{0:T(128)S(1)} %compare_select_fusion.2.table_ref, f32[1,512,4096]{2,1,0:T(8,128)} %stream_ref.5, bf16[2,1,256,32,512]{4,3,2,1,0:T(8,128)(2,1)} %refs_0_.21, bf16[2,1,512,4096]{3,2,1,0:T(8,128)(2,1)} %refs_1_.21), custom_call_target="tpu_custom_call" | custom-call | bytes 25165824 | tf_op jit(solution)/shard_map/fetch/pallas_call | solution.py:75
  15.4 3.2 core.24.refs_0_.rest_0_
  20.7 2.8 fetch.3
  26.6 3.2 core.25.rest_0_
  38.8 7.9 %collective-permute-done.4.rest_0_ = bf16[128,1152]{1,0:T(8,128)(2,1)S(1)} collective-permute-done((bf16[128,1152]{1,0:T(8,128)(2,1)S(1)}, bf16[128,1152]{1,0:T(8,128)(2,1)S(1)}, u32[]{:S(2)}, u32[]{:S(2)}) %collective-permute-start.4) | collective-permute-done | bytes 294944 | tf_op jit(solution)/shard_map/ppermute | solution.py:28
  46.7 3.2 core.26.rest_0_
  51.7 2.5 collective-permute-done.6.rest_1_
  55.6 3.2 core.27.rest_0_
  68.2 7.2 %collective-permute-done.12.rest_0_ = bf16[128,1152]{1,0:T(8,128)(2,1)S(1)} collective-permute-done((bf16[128,1152]{1,0:T(8,128)(2,1)S(1)}, bf16[128,1152]{1,0:T(8,128)(2,1)S(1)}, u32[]{:S(2)}, u32[]{:S(2)}) %collective-permute-start.12) | collective-permute-done | bytes 294944 | tf_op jit(solution)/shard_map/ppermute | solution.py:28
  75.4 3.2 core.28.rest_0_
  80.5 2.5 collective-permute-done.13.rest_1_
  84.4 3.2 core.29.rest_0_
  96.4 7.6 %collective-permute-done.16.rest_0_ = bf16[128,1152]{1,0:T(8,128)(2,1)S(1)} collective-permute-done((bf16[128,1152]{1,0:T(8,128)(2,1)S(1)}, bf16[128,1152]{1,0:T(8,128)(2,1)S(1)}, u32[]{:S(2)}, u32[]{:S(2)}) %collective-permute-start.16) | collective-permute-done | bytes 294944 | tf_op jit(solution)/shard_map/ppermute | solution.py:28
  104.0 3.2 core.30.rest_0_
  109.0 3.0 collective-permute-done.18.rest_1_
  113.3 3.2 core.31.rest_0_
  118.6 2.4 collective-permute-done.20.rest_1_
  125.9 7.2 %collective-permute-done.24.rest_0_ = bf16[128,1152]{1,0:T(8,128)(2,1)S(1)} collective-permute-done((bf16[128,1152]{1,0:T(8,128)(2,1)S(1)}, bf16[128,1152]{1,0:T(8,128)(2,1)S(1)}, u32[]{:S(2)}, u32[]{:S(2)}) %collective-permute-start.24) | collective-permute-done | bytes 294944 | tf_op jit(solution)/shard_map/ppermute | solution.py:28
  133.2 3.2 core.32.rest_0_
  142.0 3.2 core.33.rest_0_
  154.7 7.9 %collective-permute-done.28.rest_0_ = bf16[128,1152]{1,0:T(8,128)(2,1)S(1)} collective-permute-done((bf16[128,1152]{1,0:T(8,128)(2,1)S(1)}, bf16[128,1152]{1,0:T(8,128)(2,1)S(1)}, u32[]{:S(2)}, u32[]{:S(2)}) %collective-permute-start.28) | collective-permute-done | bytes 294944 | tf_op jit(solution)/shard_map/ppermute | solution.py:28
  162.6 3.2 core.34.rest_0_
  171.6 3.2 core.35.rest_0_
  184.1 7.2 %collective-permute-done.36.rest_0_ = bf16[128,1152]{1,0:T(8,128)(2,1)S(1)} collective-permute-done((bf16[128,1152]{1,0:T(8,128)(2,1)S(1)}, bf16[128,1152]{1,0:T(8,128)(2,1)S(1)}, u32[]{:S(2)}, u32[]{:S(2)}) %collective-permute-start.36) | collective-permute-done | bytes 294944 | tf_op jit(solution)/shard_map/ppermute | solution.py:28
  191.3 3.2 core.36.rest_0_
  200.3 3.2 core.37.rest_0_
  209.2 2.6 collective-permute-start.45
  213.8 7.6 %collective-permute-done.40.rest_0_ = bf16[128,1152]{1,0:T(8,128)(2,1)S(1)} collective-permute-done((bf16[128,1152]{1,0:T(8,128)(2,1)S(1)}, bf16[128,1152]{1,0:T(8,128)(2,1)S(1)}, u32[]{:S(2)}, u32[]{:S(2)}) %collective-permute-start.40) | collective-permute-done | bytes 294944 | tf_op jit(solution)/shard_map/ppermute | solution.py:28
  221.4 3.2 core.38.rest_0_
  230.7 3.2 core.39.rest_0_
  243.3 6.8 %collective-permute-done.48.rest_0_ = bf16[128,1152]{1,0:T(8,128)(2,1)S(1)} collective-permute-done((bf16[128,1152]{1,0:T(8,128)(2,1)S(1)}, bf16[128,1152]{1,0:T(8,128)(2,1)S(1)}, u32[]{:S(2)}, u32[]{:S(2)}) %collective-permute-start.48) | collective-permute-done | bytes 294944 | tf_op jit(solution)/shard_map/ppermute | solution.py:28
  250.1 3.2 core.40.rest_0_
  259.8 3.2 core.41.rest_0_
  271.9 7.9 %collective-permute-done.52.rest_0_ = bf16[128,1152]{1,0:T(8,128)(2,1)S(1)} collective-permute-done((bf16[128,1152]{1,0:T(8,128)(2,1)S(1)}, bf16[128,1152]{1,0:T(8,128)(2,1)S(1)}, u32[]{:S(2)}, u32[]{:S(2)}) %collective-permute-start.52) | collective-permute-done | bytes 294944 | tf_op jit(solution)/shard_map/ppermute | solution.py:28
  279.8 3.2 core.42.rest_0_
  288.7 3.2 core.43.rest_0_
  301.2 7.0 %collective-permute-done.60.rest_0_ = bf16[128,1152]{1,0:T(8,128)(2,1)S(1)} collective-permute-done((bf16[128,1152]{1,0:T(8,128)(2,1)S(1)}, bf16[128,1152]{1,0:T(8,128)(2,1)S(1)}, u32[]{:S(2)}, u32[]{:S(2)}) %collective-permute-start.60) | collective-permute-done | bytes 294944 | tf_op jit(solution)/shard_map/ppermute | solution.py:28
  308.3 3.2 core.44.rest_0_
  317.5 3.2 core.45.rest_0_
  326.3 3.2 core.46.rest_0_
  331.4 2.4 collective-permute-done.66.rest_1_
  335.1 3.4 core.47.rest_0_
  344.6 12.7 %collective-permute-done.71.refs_0_ = bf16[128,4096]{1,0:T(8,128)(2,1)S(1)} collective-permute-done((bf16[128,4096]{1,0:T(8,128)(2,1)S(1)}, bf16[128,4096]{1,0:T(8,128)(2,1)S(1)}, u32[]{:S(2)}, u32[]{:S(2)}) %collective-permute-start.71) | collective-permute-done | bytes 1048608 | tf_op jit(solution)/shard_map/ppermute | solution.py:28
  358.7 9.8 %collective-permute-done.70.refs_0_ = bf16[128,4096]{1,0:T(8,128)(2,1)S(1)} collective-permute-done((bf16[128,4096]{1,0:T(8,128)(2,1)S(1)}, bf16[128,4096]{1,0:T(8,128)(2,1)S(1)}, u32[]{:S(2)}, u32[]{:S(2)}) %collective-permute-start.70) | collective-permute-done | bytes 1048608 | tf_op jit(solution)/shard_map/ppermute | solution.py:28
  370.0 9.8 %collective-permute-done.69.refs_0_ = bf16[128,4096]{1,0:T(8,128)(2,1)S(1)} collective-permute-done((bf16[128,4096]{1,0:T(8,128)(2,1)S(1)}, bf16[128,4096]{1,0:T(8,128)(2,1)S(1)}, u32[]{:S(2)}, u32[]{:S(2)}) %collective-permute-start.69) | collective-permute-done | bytes 1048608 | tf_op jit(solution)/shard_map/ppermute | solution.py:28
  381.2 9.8 %collective-permute-done.68.refs_0_ = bf16[128,4096]{1,0:T(8,128)(2,1)S(1)} collective-permute-done((bf16[128,4096]{1,0:T(8,128)(2,1)S(1)}, bf16[128,4096]{1,0:T(8,128)(2,1)S(1)}, u32[]{:S(2)}, u32[]{:S(2)}) %collective-permute-start.68) | collective-permute-done | bytes 1048608 | tf_op jit(solution)/shard_map/ppermute | solution.py:28
  (187 shorter events, 166.1 us)
Async XLA Ops:
  5.1 10.2 %collective-permute-start = (bf16[128,1152]{1,0:T(8,128)(2,1)S(1)}, bf16[128,1152]{1,0:T(8,128)(2,1)S(1)}, u32[]{:S(2)}, u32[]{:S(2)}) collective-permute-start(bf16[128,1152]{1,0:T(8,128)(2,1)S(1)} %get-tuple-element.107), channel_id=1, source_target_pairs={{0,1},{1,0},{2,3},{3,2},{4,5},{5,4},{6,7},{7,6},{8,9},{9,8},{10,11... | collective-permute-start | bytes 884744 | tf_op jit(solution)/shard_map/ppermute | solution.py:28
  15.3 11.3 %collective-permute-start.1 = (bf16[128,1152]{1,0:T(8,128)(2,1)S(1)}, bf16[128,1152]{1,0:T(8,128)(2,1)S(1)}, u32[]{:S(2)}, u32[]{:S(2)}) collective-permute-start(bf16[128,1152]{1,0:T(8,128)(2,1)S(1)} %get-tuple-element.115), channel_id=1, source_target_pairs={{0,1},{1,0},{2,3},{3,2},{4,5},{5,4},{6,7},{7,6},{8,9},{9,8},{10,11... | collective-permute-start | bytes 884744 | tf_op jit(solution)/shard_map/ppermute | solution.py:28
  26.5 23.8 %collective-permute-start.7 = (bf16[128,4096]{1,0:T(8,128)(2,1)S(1)}, bf16[128,4096]{1,0:T(8,128)(2,1)S(1)}, u32[]{:S(2)}, u32[]{:S(2)}) collective-permute-start(bf16[128,4096]{1,0:T(8,128)(2,1)S(1)} %advance.24.rest_3_), channel_id=1, source_target_pairs={{0,2},{2,4},{4,6},{6,8},{8,10},{10,12},{12,14},{14,16},{16,18},{18... | collective-permute-start | bytes 3145736 | tf_op jit(solution)/shard_map/ppermute | solution.py:28
  35.5 23.9 %collective-permute-start.9 = (bf16[128,4096]{1,0:T(8,128)(2,1)S(1)}, bf16[128,4096]{1,0:T(8,128)(2,1)S(1)}, u32[]{:S(2)}, u32[]{:S(2)}) collective-permute-start(bf16[128,4096]{1,0:T(8,128)(2,1)S(1)} %advance.25.rest_3_), channel_id=1, source_target_pairs={{0,2},{2,4},{4,6},{6,8},{8,10},{10,12},{12,14},{14,16},{16,18},{18... | collective-permute-start | bytes 3145736 | tf_op jit(solution)/shard_map/ppermute | solution.py:28
  36.8 9.9 %collective-permute-start.4 = (bf16[128,1152]{1,0:T(8,128)(2,1)S(1)}, bf16[128,1152]{1,0:T(8,128)(2,1)S(1)}, u32[]{:S(2)}, u32[]{:S(2)}) collective-permute-start(bf16[128,1152]{1,0:T(8,128)(2,1)S(1)} %get-tuple-element.119.rest_3_), channel_id=1, source_target_pairs={{0,1},{1,0},{2,3},{3,2},{4,5},{5,4},{6,7},{7,6},{8,9},{9,8},{10,11... | collective-permute-start | bytes 884744 | tf_op jit(solution)/shard_map/ppermute | solution.py:28
  37.2 18.4 %collective-permute-start.3 = (bf16[128,1152]{1,0:T(8,128)(2,1)S(1)}, bf16[128,1152]{1,0:T(8,128)(2,1)S(1)}, u32[]{:S(2)}, u32[]{:S(2)}) collective-permute-start(bf16[128,1152]{1,0:T(8,128)(2,1)S(1)} %get-tuple-element.122.refs_4_.rest_3_), channel_id=1, source_target_pairs={{0,1},{1,0},{2,3},{3,2},{4,5},{5,4},{6,7},{7,6},{8,9},{9,8},{10,11... | collective-permute-start | bytes 884744 | tf_op jit(solution)/shard_map/ppermute | solution.py:28
  55.5 23.6 %collective-permute-start.14 = (bf16[128,4096]{1,0:T(8,128)(2,1)S(1)}, bf16[128,4096]{1,0:T(8,128)(2,1)S(1)}, u32[]{:S(2)}, u32[]{:S(2)}) collective-permute-start(bf16[128,4096]{1,0:T(8,128)(2,1)S(1)} %advance.26.rest_3_), channel_id=1, source_target_pairs={{0,2},{2,4},{4,6},{6,8},{8,10},{10,12},{12,14},{14,16},{16,18},{18... | collective-permute-start | bytes 3145736 | tf_op jit(solution)/shard_map/ppermute | solution.py:28
  64.4 23.8 %collective-permute-start.10 = (bf16[128,4096]{1,0:T(8,128)(2,1)S(1)}, bf16[128,4096]{1,0:T(8,128)(2,1)S(1)}, u32[]{:S(2)}, u32[]{:S(2)}) collective-permute-start(bf16[128,4096]{1,0:T(8,128)(2,1)S(1)} %advance.27.refs_4_.rest_3_), channel_id=1, source_target_pairs={{0,2},{2,4},{4,6},{6,8},{8,10},{10,12},{12,14},{14,16},{16,18},{18... | collective-permute-start | bytes 3145736 | tf_op jit(solution)/shard_map/ppermute | solution.py:28
  65.5 9.9 %collective-permute-start.12 = (bf16[128,1152]{1,0:T(8,128)(2,1)S(1)}, bf16[128,1152]{1,0:T(8,128)(2,1)S(1)}, u32[]{:S(2)}, u32[]{:S(2)}) collective-permute-start(bf16[128,1152]{1,0:T(8,128)(2,1)S(1)} %get-tuple-element.127.rest_3_), channel_id=1, source_target_pairs={{0,1},{1,0},{2,3},{3,2},{4,5},{5,4},{6,7},{7,6},{8,9},{9,8},{10,11... | collective-permute-start | bytes 884744 | tf_op jit(solution)/shard_map/ppermute | solution.py:28
  66.0 18.4 %collective-permute-start.11 = (bf16[128,1152]{1,0:T(8,128)(2,1)S(1)}, bf16[128,1152]{1,0:T(8,128)(2,1)S(1)}, u32[]{:S(2)}, u32[]{:S(2)}) collective-permute-start(bf16[128,1152]{1,0:T(8,128)(2,1)S(1)} %get-tuple-element.128.rest_3_), channel_id=1, source_target_pairs={{0,1},{1,0},{2,3},{3,2},{4,5},{5,4},{6,7},{7,6},{8,9},{9,8},{10,11... | collective-permute-start | bytes 884744 | tf_op jit(solution)/shard_map/ppermute | solution.py:28
  84.4 23.2 %collective-permute-start.19 = (bf16[128,4096]{1,0:T(8,128)(2,1)S(1)}, bf16[128,4096]{1,0:T(8,128)(2,1)S(1)}, u32[]{:S(2)}, u32[]{:S(2)}) collective-permute-start(bf16[128,4096]{1,0:T(8,128)(2,1)S(1)} %advance.28.rest_3_), channel_id=1, source_target_pairs={{0,2},{2,4},{4,6},{6,8},{8,10},{10,12},{12,14},{14,16},{16,18},{18... | collective-permute-start | bytes 3145736 | tf_op jit(solution)/shard_map/ppermute | solution.py:28
  93.2 24.0 %collective-permute-start.21 = (bf16[128,4096]{1,0:T(8,128)(2,1)S(1)}, bf16[128,4096]{1,0:T(8,128)(2,1)S(1)}, u32[]{:S(2)}, u32[]{:S(2)}) collective-permute-start(bf16[128,4096]{1,0:T(8,128)(2,1)S(1)} %advance.29.rest_3_), channel_id=1, source_target_pairs={{0,2},{2,4},{4,6},{6,8},{8,10},{10,12},{12,14},{14,16},{16,18},{18... | collective-permute-start | bytes 3145736 | tf_op jit(solution)/shard_map/ppermute | solution.py:28
  94.4 9.6 %collective-permute-start.16 = (bf16[128,1152]{1,0:T(8,128)(2,1)S(1)}, bf16[128,1152]{1,0:T(8,128)(2,1)S(1)}, u32[]{:S(2)}, u32[]{:S(2)}) collective-permute-start(bf16[128,1152]{1,0:T(8,128)(2,1)S(1)} %get-tuple-element.135.rest_3_), channel_id=1, source_target_pairs={{0,1},{1,0},{2,3},{3,2},{4,5},{5,4},{6,7},{7,6},{8,9},{9,8},{10,11... | collective-permute-start | bytes 884744 | tf_op jit(solution)/shard_map/ppermute | solution.py:28
  94.9 18.4 %collective-permute-start.15 = (bf16[128,1152]{1,0:T(8,128)(2,1)S(1)}, bf16[128,1152]{1,0:T(8,128)(2,1)S(1)}, u32[]{:S(2)}, u32[]{:S(2)}) collective-permute-start(bf16[128,1152]{1,0:T(8,128)(2,1)S(1)} %get-tuple-element.138.refs_4_.rest_3_), channel_id=1, source_target_pairs={{0,1},{1,0},{2,3},{3,2},{4,5},{5,4},{6,7},{7,6},{8,9},{9,8},{10,11... | collective-permute-start | bytes 884744 | tf_op jit(solution)/shard_map/ppermute | solution.py:28
  113.3 23.8 %collective-permute-start.26 = (bf16[128,4096]{1,0:T(8,128)(2,1)S(1)}, bf16[128,4096]{1,0:T(8,128)(2,1)S(1)}, u32[]{:S(2)}, u32[]{:S(2)}) collective-permute-start(bf16[128,4096]{1,0:T(8,128)(2,1)S(1)} %advance.30.rest_3_), channel_id=1, source_target_pairs={{0,2},{2,4},{4,6},{6,8},{8,10},{10,12},{12,14},{14,16},{16,18},{18... | collective-permute-start | bytes 3145736 | tf_op jit(solution)/shard_map/ppermute | solution.py:28
  122.4 23.6 %collective-permute-start.22 = (bf16[128,4096]{1,0:T(8,128)(2,1)S(1)}, bf16[128,4096]{1,0:T(8,128)(2,1)S(1)}, u32[]{:S(2)}, u32[]{:S(2)}) collective-permute-start(bf16[128,4096]{1,0:T(8,128)(2,1)S(1)} %advance.31.refs_4_.rest_3_), channel_id=1, source_target_pairs={{0,2},{2,4},{4,6},{6,8},{8,10},{10,12},{12,14},{14,16},{16,18},{18... | collective-permute-start | bytes 3145736 | tf_op jit(solution)/shard_map/ppermute | solution.py:28
  123.3 9.9 %collective-permute-start.24 = (bf16[128,1152]{1,0:T(8,128)(2,1)S(1)}, bf16[128,1152]{1,0:T(8,128)(2,1)S(1)}, u32[]{:S(2)}, u32[]{:S(2)}) collective-permute-start(bf16[128,1152]{1,0:T(8,128)(2,1)S(1)} %get-tuple-element.143.rest_3_), channel_id=1, source_target_pairs={{0,1},{1,0},{2,3},{3,2},{4,5},{5,4},{6,7},{7,6},{8,9},{9,8},{10,11... | collective-permute-start | bytes 884744 | tf_op jit(solution)/shard_map/ppermute | solution.py:28
  124.0 18.1 %collective-permute-start.23 = (bf16[128,1152]{1,0:T(8,128)(2,1)S(1)}, bf16[128,1152]{1,0:T(8,128)(2,1)S(1)}, u32[]{:S(2)}, u32[]{:S(2)}) collective-permute-start(bf16[128,1152]{1,0:T(8,128)(2,1)S(1)} %get-tuple-element.144.rest_3_), channel_id=1, source_target_pairs={{0,1},{1,0},{2,3},{3,2},{4,5},{5,4},{6,7},{7,6},{8,9},{9,8},{10,11... | collective-permute-start | bytes 884744 | tf_op jit(solution)/shard_map/ppermute | solution.py:28
  142.0 25.4 %collective-permute-start.31 = (bf16[128,4096]{1,0:T(8,128)(2,1)S(1)}, bf16[128,4096]{1,0:T(8,128)(2,1)S(1)}, u32[]{:S(2)}, u32[]{:S(2)}) collective-permute-start(bf16[128,4096]{1,0:T(8,128)(2,1)S(1)} %advance.32.rest_3_), channel_id=1, source_target_pairs={{0,2},{2,4},{4,6},{6,8},{8,10},{10,12},{12,14},{14,16},{16,18},{18... | collective-permute-start | bytes 3145736 | tf_op jit(solution)/shard_map/ppermute | solution.py:28
  150.9 25.6 %collective-permute-start.33 = (bf16[128,4096]{1,0:T(8,128)(2,1)S(1)}, bf16[128,4096]{1,0:T(8,128)(2,1)S(1)}, u32[]{:S(2)}, u32[]{:S(2)}) collective-permute-start(bf16[128,4096]{1,0:T(8,128)(2,1)S(1)} %advance.33.rest_3_), channel_id=1, source_target_pairs={{0,2},{2,4},{4,6},{6,8},{8,10},{10,12},{12,14},{14,16},{16,18},{18... | collective-permute-start | bytes 3145736 | tf_op jit(solution)/shard_map/ppermute | solution.py:28
  152.7 9.9 %collective-permute-start.28 = (bf16[128,1152]{1,0:T(8,128)(2,1)S(1)}, bf16[128,1152]{1,0:T(8,128)(2,1)S(1)}, u32[]{:S(2)}, u32[]{:S(2)}) collective-permute-start(bf16[128,1152]{1,0:T(8,128)(2,1)S(1)} %get-tuple-element.151.rest_3_), channel_id=1, source_target_pairs={{0,1},{1,0},{2,3},{3,2},{4,5},{5,4},{6,7},{7,6},{8,9},{9,8},{10,11... | collective-permute-start | bytes 884744 | tf_op jit(solution)/shard_map/ppermute | solution.py:28
  154.2 17.3 %collective-permute-start.27 = (bf16[128,1152]{1,0:T(8,128)(2,1)S(1)}, bf16[128,1152]{1,0:T(8,128)(2,1)S(1)}, u32[]{:S(2)}, u32[]{:S(2)}) collective-permute-start(bf16[128,1152]{1,0:T(8,128)(2,1)S(1)} %get-tuple-element.154.refs_4_.rest_3_), channel_id=1, source_target_pairs={{0,1},{1,0},{2,3},{3,2},{4,5},{5,4},{6,7},{7,6},{8,9},{9,8},{10,11... | collective-permute-start | bytes 884744 | tf_op jit(solution)/shard_map/ppermute | solution.py:28
  171.5 24.7 %collective-permute-start.38 = (bf16[128,4096]{1,0:T(8,128)(2,1)S(1)}, bf16[128,4096]{1,0:T(8,128)(2,1)S(1)}, u32[]{:S(2)}, u32[]{:S(2)}) collective-permute-start(bf16[128,4096]{1,0:T(8,128)(2,1)S(1)} %advance.34.rest_3_), channel_id=1, source_target_pairs={{0,2},{2,4},{4,6},{6,8},{8,10},{10,12},{12,14},{14,16},{16,18},{18... | collective-permute-start | bytes 3145736 | tf_op jit(solution)/shard_map/ppermute | solution.py:28
  180.4 24.7 %collective-permute-start.34 = (bf16[128,4096]{1,0:T(8,128)(2,1)S(1)}, bf16[128,4096]{1,0:T(8,128)(2,1)S(1)}, u32[]{:S(2)}, u32[]{:S(2)}) collective-permute-start(bf16[128,4096]{1,0:T(8,128)(2,1)S(1)} %advance.35.refs_4_.rest_3_), channel_id=1, source_target_pairs={{0,2},{2,4},{4,6},{6,8},{8,10},{10,12},{12,14},{14,16},{16,18},{18... | collective-permute-start | bytes 3145736 | tf_op jit(solution)/shard_map/ppermute | solution.py:28
  181.5 9.9 %collective-permute-start.36 = (bf16[128,1152]{1,0:T(8,128)(2,1)S(1)}, bf16[128,1152]{1,0:T(8,128)(2,1)S(1)}, u32[]{:S(2)}, u32[]{:S(2)}) collective-permute-start(bf16[128,1152]{1,0:T(8,128)(2,1)S(1)} %get-tuple-element.159.rest_3_), channel_id=1, source_target_pairs={{0,1},{1,0},{2,3},{3,2},{4,5},{5,4},{6,7},{7,6},{8,9},{9,8},{10,11... | collective-permute-start | bytes 884744 | tf_op jit(solution)/shard_map/ppermute | solution.py:28
  183.0 17.3 %collective-permute-start.35 = (bf16[128,1152]{1,0:T(8,128)(2,1)S(1)}, bf16[128,1152]{1,0:T(8,128)(2,1)S(1)}, u32[]{:S(2)}, u32[]{:S(2)}) collective-permute-start(bf16[128,1152]{1,0:T(8,128)(2,1)S(1)} %get-tuple-element.160.rest_3_), channel_id=1, source_target_pairs={{0,1},{1,0},{2,3},{3,2},{4,5},{5,4},{6,7},{7,6},{8,9},{9,8},{10,11... | collective-permute-start | bytes 884744 | tf_op jit(solution)/shard_map/ppermute | solution.py:28
  200.3 25.9 %collective-permute-start.43 = (bf16[128,4096]{1,0:T(8,128)(2,1)S(1)}, bf16[128,4096]{1,0:T(8,128)(2,1)S(1)}, u32[]{:S(2)}, u32[]{:S(2)}) collective-permute-start(bf16[128,4096]{1,0:T(8,128)(2,1)S(1)} %advance.36.rest_3_), channel_id=1, source_target_pairs={{0,2},{2,4},{4,6},{6,8},{8,10},{10,12},{12,14},{14,16},{16,18},{18... | collective-permute-start | bytes 3145736 | tf_op jit(solution)/shard_map/ppermute | solution.py:28
  209.2 26.3 %collective-permute-start.45 = (bf16[128,4096]{1,0:T(8,128)(2,1)S(1)}, bf16[128,4096]{1,0:T(8,128)(2,1)S(1)}, u32[]{:S(2)}, u32[]{:S(2)}) collective-permute-start(bf16[128,4096]{1,0:T(8,128)(2,1)S(1)} %advance.37.rest_3_), channel_id=1, source_target_pairs={{0,2},{2,4},{4,6},{6,8},{8,10},{10,12},{12,14},{14,16},{16,18},{18... | collective-permute-start | bytes 3145736 | tf_op jit(solution)/shard_map/ppermute | solution.py:28
  211.7 9.7 %collective-permute-start.40 = (bf16[128,1152]{1,0:T(8,128)(2,1)S(1)}, bf16[128,1152]{1,0:T(8,128)(2,1)S(1)}, u32[]{:S(2)}, u32[]{:S(2)}) collective-permute-start(bf16[128,1152]{1,0:T(8,128)(2,1)S(1)} %get-tuple-element.167.rest_3_), channel_id=1, source_target_pairs={{0,1},{1,0},{2,3},{3,2},{4,5},{5,4},{6,7},{7,6},{8,9},{9,8},{10,11... | collective-permute-start | bytes 884744 | tf_op jit(solution)/shard_map/ppermute | solution.py:28
  213.3 17.4 %collective-permute-start.39 = (bf16[128,1152]{1,0:T(8,128)(2,1)S(1)}, bf16[128,1152]{1,0:T(8,128)(2,1)S(1)}, u32[]{:S(2)}, u32[]{:S(2)}) collective-permute-start(bf16[128,1152]{1,0:T(8,128)(2,1)S(1)} %get-tuple-element.170.refs_4_.rest_3_), channel_id=1, source_target_pairs={{0,1},{1,0},{2,3},{3,2},{4,5},{5,4},{6,7},{7,6},{8,9},{9,8},{10,11... | collective-permute-start | bytes 884744 | tf_op jit(solution)/shard_map/ppermute | solution.py:28
  230.6 24.2 %collective-permute-start.50 = (bf16[128,4096]{1,0:T(8,128)(2,1)S(1)}, bf16[128,4096]{1,0:T(8,128)(2,1)S(1)}, u32[]{:S(2)}, u32[]{:S(2)}) collective-permute-start(bf16[128,4096]{1,0:T(8,128)(2,1)S(1)} %advance.38.rest_3_), channel_id=1, source_target_pairs={{0,2},{2,4},{4,6},{6,8},{8,10},{10,12},{12,14},{14,16},{16,18},{18... | collective-permute-start | bytes 3145736 | tf_op jit(solution)/shard_map/ppermute | solution.py:28
  239.5 25.0 %collective-permute-start.46 = (bf16[128,4096]{1,0:T(8,128)(2,1)S(1)}, bf16[128,4096]{1,0:T(8,128)(2,1)S(1)}, u32[]{:S(2)}, u32[]{:S(2)}) collective-permute-start(bf16[128,4096]{1,0:T(8,128)(2,1)S(1)} %advance.39.refs_4_.rest_3_), channel_id=1, source_target_pairs={{0,2},{2,4},{4,6},{6,8},{8,10},{10,12},{12,14},{14,16},{16,18},{18... | collective-permute-start | bytes 3145736 | tf_op jit(solution)/shard_map/ppermute | solution.py:28
  240.6 9.4 %collective-permute-start.48 = (bf16[128,1152]{1,0:T(8,128)(2,1)S(1)}, bf16[128,1152]{1,0:T(8,128)(2,1)S(1)}, u32[]{:S(2)}, u32[]{:S(2)}) collective-permute-start(bf16[128,1152]{1,0:T(8,128)(2,1)S(1)} %get-tuple-element.175.rest_3_), channel_id=1, source_target_pairs={{0,1},{1,0},{2,3},{3,2},{4,5},{5,4},{6,7},{7,6},{8,9},{9,8},{10,11... | collective-permute-start | bytes 884744 | tf_op jit(solution)/shard_map/ppermute | solution.py:28
  242.2 17.6 %collective-permute-start.47 = (bf16[128,1152]{1,0:T(8,128)(2,1)S(1)}, bf16[128,1152]{1,0:T(8,128)(2,1)S(1)}, u32[]{:S(2)}, u32[]{:S(2)}) collective-permute-start(bf16[128,1152]{1,0:T(8,128)(2,1)S(1)} %get-tuple-element.176.rest_3_), channel_id=1, source_target_pairs={{0,1},{1,0},{2,3},{3,2},{4,5},{5,4},{6,7},{7,6},{8,9},{9,8},{10,11... | collective-permute-start | bytes 884744 | tf_op jit(solution)/shard_map/ppermute | solution.py:28
  259.5 25.0 %collective-permute-start.55 = (bf16[128,4096]{1,0:T(8,128)(2,1)S(1)}, bf16[128,4096]{1,0:T(8,128)(2,1)S(1)}, u32[]{:S(2)}, u32[]{:S(2)}) collective-permute-start(bf16[128,4096]{1,0:T(8,128)(2,1)S(1)} %advance.40.rest_3_), channel_id=1, source_target_pairs={{0,2},{2,4},{4,6},{6,8},{8,10},{10,12},{12,14},{14,16},{16,18},{18... | collective-permute-start | bytes 3145736 | tf_op jit(solution)/shard_map/ppermute | solution.py:28
  269.1 24.4 %collective-permute-start.57 = (bf16[128,4096]{1,0:T(8,128)(2,1)S(1)}, bf16[128,4096]{1,0:T(8,128)(2,1)S(1)}, u32[]{:S(2)}, u32[]{:S(2)}) collective-permute-start(bf16[128,4096]{1,0:T(8,128)(2,1)S(1)} %advance.41.rest_3_), channel_id=1, source_target_pairs={{0,2},{2,4},{4,6},{6,8},{8,10},{10,12},{12,14},{14,16},{16,18},{18... | collective-permute-start | bytes 3145736 | tf_op jit(solution)/shard_map/ppermute | solution.py:28
  269.9 9.9 %collective-permute-start.52 = (bf16[128,1152]{1,0:T(8,128)(2,1)S(1)}, bf16[128,1152]{1,0:T(8,128)(2,1)S(1)}, u32[]{:S(2)}, u32[]{:S(2)}) collective-permute-start(bf16[128,1152]{1,0:T(8,128)(2,1)S(1)} %get-tuple-element.183.rest_3_), channel_id=1, source_target_pairs={{0,1},{1,0},{2,3},{3,2},{4,5},{5,4},{6,7},{7,6},{8,9},{9,8},{10,11... | collective-permute-start | bytes 884744 | tf_op jit(solution)/shard_map/ppermute | solution.py:28
  271.4 17.3 %collective-permute-start.51 = (bf16[128,1152]{1,0:T(8,128)(2,1)S(1)}, bf16[128,1152]{1,0:T(8,128)(2,1)S(1)}, u32[]{:S(2)}, u32[]{:S(2)}) collective-permute-start(bf16[128,1152]{1,0:T(8,128)(2,1)S(1)} %get-tuple-element.186.refs_4_.rest_3_), channel_id=1, source_target_pairs={{0,1},{1,0},{2,3},{3,2},{4,5},{5,4},{6,7},{7,6},{8,9},{9,8},{10,11... | collective-permute-start | bytes 884744 | tf_op jit(solution)/shard_map/ppermute | solution.py:28
  288.6 24.4 %collective-permute-start.62 = (bf16[128,4096]{1,0:T(8,128)(2,1)S(1)}, bf16[128,4096]{1,0:T(8,128)(2,1)S(1)}, u32[]{:S(2)}, u32[]{:S(2)}) collective-permute-start(bf16[128,4096]{1,0:T(8,128)(2,1)S(1)} %advance.42.rest_3_), channel_id=1, source_target_pairs={{0,2},{2,4},{4,6},{6,8},{8,10},{10,12},{12,14},{14,16},{16,18},{18... | collective-permute-start | bytes 3145736 | tf_op jit(solution)/shard_map/ppermute | solution.py:28
  297.9 24.4 %collective-permute-start.58 = (bf16[128,4096]{1,0:T(8,128)(2,1)S(1)}, bf16[128,4096]{1,0:T(8,128)(2,1)S(1)}, u32[]{:S(2)}, u32[]{:S(2)}) collective-permute-start(bf16[128,4096]{1,0:T(8,128)(2,1)S(1)} %advance.43.refs_4_.rest_3_), channel_id=1, source_target_pairs={{0,2},{2,4},{4,6},{6,8},{8,10},{10,12},{12,14},{14,16},{16,18},{18... | collective-permute-start | bytes 3145736 | tf_op jit(solution)/shard_map/ppermute | solution.py:28
  298.6 9.7 %collective-permute-start.60 = (bf16[128,1152]{1,0:T(8,128)(2,1)S(1)}, bf16[128,1152]{1,0:T(8,128)(2,1)S(1)}, u32[]{:S(2)}, u32[]{:S(2)}) collective-permute-start(bf16[128,1152]{1,0:T(8,128)(2,1)S(1)} %get-tuple-element.191.rest_3_), channel_id=1, source_target_pairs={{0,1},{1,0},{2,3},{3,2},{4,5},{5,4},{6,7},{7,6},{8,9},{9,8},{10,11... | collective-permute-start | bytes 884744 | tf_op jit(solution)/shard_map/ppermute | solution.py:28
  300.1 17.3 %collective-permute-start.59 = (bf16[128,1152]{1,0:T(8,128)(2,1)S(1)}, bf16[128,1152]{1,0:T(8,128)(2,1)S(1)}, u32[]{:S(2)}, u32[]{:S(2)}) collective-permute-start(bf16[128,1152]{1,0:T(8,128)(2,1)S(1)} %get-tuple-element.192.rest_3_), channel_id=1, source_target_pairs={{0,1},{1,0},{2,3},{3,2},{4,5},{5,4},{6,7},{7,6},{8,9},{9,8},{10,11... | collective-permute-start | bytes 884744 | tf_op jit(solution)/shard_map/ppermute | solution.py:28
  314.4 11.9 %collective-permute-start.64 = (bf16[128,1152]{1,0:T(8,128)(2,1)S(1)}, bf16[128,1152]{1,0:T(8,128)(2,1)S(1)}, u32[]{:S(2)}, u32[]{:S(2)}) collective-permute-start(bf16[128,1152]{1,0:T(8,128)(2,1)S(1)} %get-tuple-element.199.rest_3_), channel_id=1, source_target_pairs={{0,1},{1,0},{2,3},{3,2},{4,5},{5,4},{6,7},{7,6},{8,9},{9,8},{10,11... | collective-permute-start | bytes 884744 | tf_op jit(solution)/shard_map/ppermute | solution.py:28
  323.6 11.5 %collective-permute-start.63 = (bf16[128,1152]{1,0:T(8,128)(2,1)S(1)}, bf16[128,1152]{1,0:T(8,128)(2,1)S(1)}, u32[]{:S(2)}, u32[]{:S(2)}) collective-permute-start(bf16[128,1152]{1,0:T(8,128)(2,1)S(1)} %get-tuple-element.202.rest_3_), channel_id=1, source_target_pairs={{0,1},{1,0},{2,3},{3,2},{4,5},{5,4},{6,7},{7,6},{8,9},{9,8},{10,11... | collective-permute-start | bytes 884744 | tf_op jit(solution)/shard_map/ppermute | solution.py:28
  340.4 16.9 %collective-permute-start.71 = (bf16[128,4096]{1,0:T(8,128)(2,1)S(1)}, bf16[128,4096]{1,0:T(8,128)(2,1)S(1)}, u32[]{:S(2)}, u32[]{:S(2)}) collective-permute-start(bf16[128,4096]{1,0:T(8,128)(2,1)S(1)} %advance.44.rest_3_), channel_id=1, source_target_pairs={{0,2},{2,4},{4,6},{6,8},{8,10},{10,12},{12,14},{14,16},{16,18},{18... | collective-permute-start | bytes 3145736 | tf_op jit(solution)/shard_map/ppermute | solution.py:28
  340.4 28.2 %collective-permute-start.70 = (bf16[128,4096]{1,0:T(8,128)(2,1)S(1)}, bf16[128,4096]{1,0:T(8,128)(2,1)S(1)}, u32[]{:S(2)}, u32[]{:S(2)}) collective-permute-start(bf16[128,4096]{1,0:T(8,128)(2,1)S(1)} %advance.45.rest_3_), channel_id=1, source_target_pairs={{0,2},{2,4},{4,6},{6,8},{8,10},{10,12},{12,14},{14,16},{16,18},{18... | collective-permute-start | bytes 3145736 | tf_op jit(solution)/shard_map/ppermute | solution.py:28
  342.6 37.2 %collective-permute-start.69 = (bf16[128,4096]{1,0:T(8,128)(2,1)S(1)}, bf16[128,4096]{1,0:T(8,128)(2,1)S(1)}, u32[]{:S(2)}, u32[]{:S(2)}) collective-permute-start(bf16[128,4096]{1,0:T(8,128)(2,1)S(1)} %advance.46.rest_3_), channel_id=1, source_target_pairs={{0,2},{2,4},{4,6},{6,8},{8,10},{10,12},{12,14},{14,16},{16,18},{18... | collective-permute-start | bytes 3145736 | tf_op jit(solution)/shard_map/ppermute | solution.py:28
  344.1 46.9 %collective-permute-start.68 = (bf16[128,4096]{1,0:T(8,128)(2,1)S(1)}, bf16[128,4096]{1,0:T(8,128)(2,1)S(1)}, u32[]{:S(2)}, u32[]{:S(2)}) collective-permute-start(bf16[128,4096]{1,0:T(8,128)(2,1)S(1)} %advance.47), channel_id=1, source_target_pairs={{0,2},{2,4},{4,6},{6,8},{8,10},{10,12},{12,14},{14,16},{16,18},{18... | collective-permute-start | bytes 3145736 | tf_op jit(solution)/shard_map/ppermute | solution.py:28
  (25 other events, 111.2 us)
